TPU v7x, 128 devices: a whole 4x4x4 slice. The times are simulated.
128 devices in a mesh: row: 8 (over y_lo, x), col: 16 (over y_hi, z, core).
Axes of the slice: x: 4, y: 4 (y_hi: 2, y_lo: 2; y = y_hi * 2 + y_lo), z: 4, core: 2. Of those that a mesh axis runs over, the one named last changes fastest.
Arguments:
- sign_iterate: bfloat16 [8192, 8192], P('row', 'col'), may hold values from -6 to 6
- sign_square: bfloat16 [8192, 8192], P('row', 'col'), may hold values from -0.125 to 0.125
- pattern_x: int32 [64, 64], P('row', 'col'), may hold values 0 or 1
- pattern_y: int32 [64, 64], P('row', 'col'), may hold values 0 or 1
- pattern_product: int32 [64, 64], P('row', 'col'), may hold values 0 or 1
- orbital_energy: bfloat16 [8192], P('row'), may hold values from -3 to 1
- pair_dest: int32 [128, 128, 1], P(('row', 'col')), may hold values from 0 to 127; in each aligned block of 128 rows (0 to 127, 128 to 255, ..., all dimensions but the last counted through in order) at most 2 rows name the same one
- pair_block: int32 [128, 128], P(('row', 'col')), may hold values from 0 to 31
- force_h: bfloat16 [32768, 128, 128], P(('row', 'col')), may hold values from -0.5 to 0.5
- force_s: bfloat16 [32768, 128, 128], P(('row', 'col')), may hold values from -0.5 to 0.5
Outputs:
- sign_next: bfloat16 [8192, 8192], P('row', 'col')
- forces: float32 [32768], P(('row', 'col'))
Inputs may be any that keep to these rules, and one draw needn't show every extreme that they name: `pair_dest`: among the 128 entries of one device no owner is named more than 2 times, a bound that some block reaches. `pair_block`: A row-major index into the device's own 8 x 4 grid of blocks.
All inputs are finite; a program needn't handle non-finite values. No bound on the sum of `pattern_x` or of `pattern_y` or of `pattern_product` on one device may be relied on, other than what follows from the above.
Results may differ from a plain program's by a relative error of at most 0.003.
Values may be sent and summed in bfloat16 or wider, within the bound.
No kernel may reach another device: no remote copies, remote signals or barrier semaphores. Data moves between devices by JAX's collectives and lax.ppermute only.
A program may use at most 128 MiB of HBM per device.

v0:
```python
import jax
import jax.numpy as jnp
from jax import lax
from jax.sharding import PartitionSpec as P

BS = 128
QB = 4
CAP = 2


def masked_tile(tile, pattern):
    rows, cols = tile.shape
    shaped = tile.reshape(rows // BS, BS, cols // BS, BS) * pattern[:, None, :, None].astype(
        tile.dtype
    )
    return shaped.reshape(rows, cols)


def tile_blocks(tile):
    rows, cols = tile.shape
    shaped = tile.reshape(rows // BS, BS, cols // BS, BS).transpose(0, 2, 1, 3)
    return shaped.reshape(rows // BS * (cols // BS), BS * BS)


def rank_within(dest):
    entries = dest.shape[-1]
    order = jnp.arange(entries, dtype=jnp.int32)
    same = (dest[..., :, None] == dest[..., None, :]) & (order[None, :] < order[:, None])
    return jnp.sum(same.astype(jnp.int32), axis=-1)


def shards(
    sign_iterate,
    sign_square,
    pattern_x,
    pattern_y,
    pattern_product,
    orbital_energy,
    pair_dest,
    pair_block,
    force_h,
    force_s,
):
    rows_x, cols_x = sign_iterate.shape
    xmask = masked_tile(sign_iterate, pattern_x)
    ymask = masked_tile(sign_square, pattern_y)
    y_whole = lax.all_gather(ymask, "row", axis=0, tiled=True)
    product = jnp.dot(
        lax.all_gather(xmask, "col", axis=1, tiled=True),
        y_whole,
        preferred_element_type=jnp.float32,
    )
    product = masked_tile(product, pattern_product)
    xnew = 1.5 * xmask.astype(jnp.float32) - 0.5 * product
    sign_next = xnew.astype(jnp.bfloat16)
    global_rows = lax.axis_index("row") * rows_x + jnp.arange(rows_x, dtype=jnp.int32)
    global_cols = lax.axis_index("col") * cols_x + jnp.arange(cols_x, dtype=jnp.int32)
    identity = (global_rows[:, None] == global_cols[None, :]).astype(jnp.float32)
    density = (0.5 * identity - 0.5 * xnew).astype(jnp.bfloat16)
    dens_blocks = tile_blocks(density)
    n_rows = lax.axis_size("row")
    n_cols = lax.axis_size("col")
    devices = n_rows * n_cols
    slots = devices * CAP
    local_rows = rows_x // BS
    dest = pair_dest[0, :, 0]
    wanted = pair_block[0]
    rank = rank_within(dest)
    slot = dest * CAP + rank
    pick_slot = (jnp.arange(slots, dtype=jnp.int32)[:, None] == slot[None, :]).astype(jnp.bfloat16)
    pick_block = (
        wanted[:, None] == jnp.arange(dens_blocks.shape[0], dtype=jnp.int32)[None, :]
    ).astype(jnp.bfloat16)
    routing_table = jnp.dot(pick_slot, pick_block, preferred_element_type=jnp.float32).astype(
        jnp.bfloat16
    )
    send_dens = jnp.dot(routing_table, dens_blocks, preferred_element_type=jnp.float32).astype(
        jnp.bfloat16
    )
    pick_row = ((wanted // QB)[:, None] == jnp.arange(local_rows, dtype=jnp.int32)[None, :]).astype(
        jnp.bfloat16
    )
    slot_rows = jnp.dot(pick_slot, pick_row, preferred_element_type=jnp.float32).astype(
        jnp.bfloat16
    )
    send_energy = jnp.dot(
        slot_rows, orbital_energy.reshape(local_rows, BS), preferred_element_type=jnp.float32
    ).astype(jnp.bfloat16)
    payload = jnp.concatenate([send_dens.reshape(slots, BS, BS), send_energy[:, None, :]], axis=1)
    height = BS + 1
    received = lax.all_to_all(
        payload.reshape(devices, CAP, height * BS),
        ("row", "col"),
        split_axis=0,
        concat_axis=0,
        tiled=True,
    )
    received = received.reshape(slots, height, BS)
    recv_dens = received[:, :BS, :]
    energies = received[:, BS, :].astype(jnp.float32)
    h_term = jnp.einsum("sab,sab->s", recv_dens, force_h, preferred_element_type=jnp.float32)
    s_rows = jnp.einsum("sab,sab->sa", recv_dens, force_s, preferred_element_type=jnp.float32)
    forces = h_term - jnp.sum(energies * s_rows, axis=1)
    return (sign_next, forces)


def solution(mesh):
    in_specs = (
        P("row", "col"),
        P("row", "col"),
        P("row", "col"),
        P("row", "col"),
        P("row", "col"),
        P("row"),
        P(("row", "col"), None, None),
        P(("row", "col"), None),
        P(("row", "col"), None, None),
        P(("row", "col"), None, None),
    )
    out_specs = (P("row", "col"), P(("row", "col")))
    return jax.shard_map(shards, mesh=mesh, in_specs=in_specs, out_specs=out_specs, check_vma=False)
```

profile of v0, /device:TPU:7, one launch (start us, length us, event | category | flops | bytes accessed | tf_op | source)
XLA Modules:
  0.0 425.2 jit_solution(5564351684399702492)
XLA Ops:
  7.3 0.7 convert_element_type.48
  8.0 0.3 mul.72
  8.4 2.4 bitcast_multiply_fusion.1
  10.9 0.7 convert_element_type.46
  11.7 0.3 mul.67
  12.0 2.3 bitcast_multiply_fusion.2
  14.5 0.2 convert_reduce_fusion
  14.7 0.5 fusion.5
  15.3 87.7 %all-gather.5.cloned.1.call-done = bf16[8192,512]{1,0:T(8,128)(2,1)} async-done(((bf16[1024,512]{1,0:T(8,128)(2,1)}), bf16[8192,512]{1,0:T(8,128)(2,1)}) %all-gather.5.cloned.1.call-update) | async-done | bytes 8388624 | tf_op jit(solution)/shard_map/all_gather | solution.py:47
  103.0 123.4 %all-gather.3.cloned.1.call-done = bf16[1024,8192]{1,0:T(8,128)(2,1)} async-done(((bf16[1024,512]{1,0:T(8,128)(2,1)}), bf16[1024,8192]{1,0:T(8,128)(2,1)}) %all-gather.3.cloned.1.call-update) | async-done | bytes 16777232 | tf_op jit(solution)/shard_map/all_gather | solution.py:49
  226.4 0.3 mul.75
  226.7 16.1 %subtract_convert_fusion = (bf16[1024,512]{1,0:T(8,128)(2,1)S(1)}, bf16[1024,512]{1,0:T(8,128)(2,1)}) fusion(s32[512]{0:T(512)S(1)} %iota_add_fusion.1, s32[1024]{0:T(1024)S(1)} %iota_add_fusion, f32[128,8,4,128]{3,2,1,0:T(4,128)S(1)} %bitcast.41, bf16[1024,8192]{1,0:T(8,128)(2,1)} %all-gather.3.cloned.1.call-done, ...), kind=kOutput, calls=%fused_computation.10 | convolution fusion | flops 8595701760 | bytes 30414848 | tf_op jit(solution)/shard_map/dot_general | solution.py:48
  242.8 0.3 reshape.86
  243.1 0.2 copy.24
  243.4 5.2 %fusion.2 = bf16[32,8,128,128]{3,1,2,0:T(8,128)(2,1)} fusion(bf16[4,8,128,128]{3,2,1,0:T(8,128)(2,1)S(1)} %bitcast.38, s32[128]{0:T(128)S(1)} %get-tuple-element.8, s32[128]{0:T(128)S(1)} %bitcast.43), kind=kOutput, calls=%fused_computation.6 | convolution fusion | flops 274771968 | bytes 9438208 | tf_op jit(solution)/shard_map/dot_general | solution.py:77
  248.6 9.2 %copy.40 = bf16[32,8,128,128]{3,2,1,0:T(8,128)(2,1)} copy(bf16[32,8,128,128]{3,1,2,0:T(8,128)(2,1)} %fusion.2) | data formatting | bytes 16777216
  257.8 9.0 %pad_maximum_fusion = bf16[256,129,128]{2,1,0:T(8,128)(2,1)} fusion(bf16[256,1,128]{2,1,0:T(2,128)(2,1)S(1)} %copy.25, bf16[256,128,128]{2,1,0:T(8,128)(2,1)} %bitcast.37), kind=kLoop, calls=%fused_computation.5 | loop fusion | flops 16908288 | bytes 16908288 | tf_op jit(solution)/shard_map/concatenate | solution.py:89
  266.8 13.2 %reshape.90 = bf16[128,2,16512]{2,1,0:T(2,128)(2,1)} reshape(bf16[256,129,128]{2,1,0:T(8,128)(2,1)} %pad_maximum_fusion) | data formatting | bytes 16908288 | tf_op jit(solution)/shard_map/reshape | solution.py:92
  280.0 110.5 %all_to_all.5 = bf16[128,2,16512]{2,1,0:T(2,128)(2,1)} all-to-all(bf16[128,2,16512]{2,1,0:T(2,128)(2,1)} %reshape.90), channel_id=1, replica_groups=mesh['row'=8,'col'=16] {'row','col'}, dimensions={0} | all-to-all | bytes 16908288 | tf_op jit(solution)/shard_map/all_to_all | solution.py:91
  390.5 14.2 %reshape.91 = bf16[256,129,128]{2,1,0:T(8,128)(2,1)} reshape(bf16[128,2,16512]{2,1,0:T(2,128)(2,1)} %all_to_all.5) | data formatting | bytes 16908288 | tf_op jit(solution)/shard_map/reshape | solution.py:98
  404.7 1.1 slice_convert_fusion
  405.8 11.8 %fusion.1 = (f32[256,128]{1,0:T(8,128)S(1)}, f32[256]{0:T(256)S(1)}) fusion(bf16[256,128,128]{2,1,0:T(8,128)(2,1)} %param.19, bf16[256,129,128]{2,1,0:T(8,128)(2,1)} %reshape.91, bf16[256,128,128]{2,1,0:T(8,128)(2,1)} %param.18), kind=kLoop, calls=%fused_computation.4 | loop fusion | flops 29327104 | bytes 25297920 | tf_op jit(solution)/shard_map/sab,sab->sa/dot_general | solution.py:102
  417.7 0.1 multiply_reduce_fusion
  417.8 0.6 sub.18
  (22 shorter events, 0.5 us)
Async XLA Ops:
  7.2 7.5 %copy-start = (bf16[1024]{0:T(1024)(128)(2,1)S(1)}, bf16[1024]{0:T(1024)(128)(2,1)}, u32[]{:S(2)}) copy-start(bf16[1024]{0:T(1024)(128)(2,1)} %param.15) | copy-start | bytes 6148
  7.2 7.2 %copy-start.3 = (s32[8,4]{0,1:T(4,128)S(1)}, s32[8,4]{0,1:T(4,128)}, u32[]{:S(2)}) copy-start(s32[8,4]{0,1:T(4,128)} %param.14) | copy-start | bytes 388
  7.2 7.3 %copy-start.4 = (s32[1,128,1]{1,2,0:T(1,128)S(1)}, s32[1,128,1]{1,2,0:T(1,128)}, u32[]{:S(2)}) copy-start(s32[1,128,1]{1,2,0:T(1,128)} %param.16) | copy-start | bytes 1540
  7.2 7.5 %copy-start.2 = (s32[1,128]{1,0:T(1,128)S(1)}, s32[1,128]{1,0:T(1,128)}, u32[]{:S(2)}) copy-start(s32[1,128]{1,0:T(1,128)} %param.17) | copy-start | bytes 1540
  7.2 95.8 %all-gather.5.cloned.1.call-start = ((), (), s32[]{:S(2)}) async-start(), calls=%async_computation.2 | async-start | bytes 9437184 | tf_op jit(solution)/shard_map/all_gather | solution.py:47
  10.8 215.6 %all-gather.3.cloned.1.call-start = ((), (), s32[]{:S(2)}) async-start(), calls=%async_computation.1 | async-start | bytes 17825792 | tf_op jit(solution)/shard_map/all_gather | solution.py:49
  404.7 13.7 %copy-start.1 = (bf16[1024]{0:T(1024)(128)(2,1)S(1)}, bf16[1024]{0:T(1024)(128)(2,1)}, u32[]{:S(2)}) copy-start(bf16[1024]{0:T(1024)(128)(2,1)} %param.15) | copy-start | bytes 6148
Sparse Core Ops, SparseCore 0:
  11.0 92.0 all-gather.4
  105.8 120.5 all-gather.2
where the time goes:
time: 426 us; the launch traced here: 425 us
  waiting for transfers between devices  211 us (50%)
  blocking collectives  110 us (26%)
  local copies, waits for them, and re-layouts  38.6 us (9%)
  other arithmetic  28.9 us (7%)
  matrix products  21.8 us (5%)
  between operations  14.2 us (3%)
    all_gather x1, waiting for transfers between devices, shards(): lax.all_gather(xmask, 'col', axis=1, tiled=True)  123 us
    all_to_all x1, blocking collectives, shards(): lax.all_to_all(payload.reshape(devices, CAP, height * BS), ('row', 'col')...  110 us
    all_gather x1, waiting for transfers between devices, shards(): y_whole = lax.all_gather(ymask, 'row', axis=0, tiled=True)  87.7 us
    dot_general x1, matrix products, shards(): jnp.dot(lax.all_gather(xmask, 'col', axis=1, tiled=True), y_whole, prefer...  16.1 us
    reshape x1, local copies, waits for them, and re-layouts, shards(): received = received.reshape(slots, height, BS)  14.2 us
    reshape x1, local copies, waits for them, and re-layouts, shards(): payload.reshape(devices, CAP, height * BS)  13.2 us
    dot_general x1, other arithmetic, shards(): jnp.einsum('sab,sab->sa', recv_dens, force_s, preferred_element_type=jnp....  11.8 us
    unnamed x11, local copies, waits for them, and re-layouts  9.24 us
  transfers between devices with their start and end apart: 2, of which 2 were waited for; matrix products, arithmetic and copies ran while one was open for 1% of the time, Pallas kernels for 0%

commit v1 on v0

v1 whole, which is shorter than its diff:
```python
import jax
import jax.numpy as jnp
from jax import lax
from jax.experimental import pallas as pl
from jax.experimental.pallas import tpu as pltpu
from jax.sharding import Mesh, PartitionSpec as P

BS = 128
QB = 4
CAP = 2
RB = 8
BLOCKS = RB * QB
ROWS = RB * BS
COLS = QB * BS
RING = 4
AXES = ("yl", "x", "yh", "z", "c")
SWAP = [(0, 1), (1, 0)]
UP = [(i, (i + 1) % RING) for i in range(RING)]
DOWN = [(i, (i - 1) % RING) for i in range(RING)]


def mask_kernel(px_ref, py_ref, x_ref, y_ref, xo_ref, yo_ref):
    i = pl.program_id(0)
    for r in range(2):
        for j in range(QB):
            rows, cols = slice(r * BS, (r + 1) * BS), slice(j * BS, (j + 1) * BS)
            for p_ref, in_ref, out_ref in ((px_ref, x_ref, xo_ref), (py_ref, y_ref, yo_ref)):
                keep = (p_ref[i * 2 + r, j] > 0).astype(jnp.float32).astype(jnp.bfloat16)
                out_ref[rows, cols] = in_ref[rows, cols] * keep


def masked_tiles(x, y, pattern_x, pattern_y):
    tile = pl.BlockSpec((2 * BS, COLS), lambda i: (i, 0))
    smem = pl.BlockSpec(memory_space=pltpu.SMEM)
    return pl.pallas_call(
        mask_kernel,
        grid=(RB // 2,),
        in_specs=[smem, smem, tile, tile],
        out_specs=[tile, tile],
        out_shape=[jax.ShapeDtypeStruct((ROWS, COLS), jnp.bfloat16)] * 2,
        cost_estimate=pl.CostEstimate(flops=2 * ROWS * COLS, bytes_accessed=8 * ROWS * COLS, transcendentals=0),
        name="mask_tiles",
    )(pattern_x, pattern_y, x, y)


def ring_gather(tile, axis):
    half = ROWS // 2
    below = lax.ppermute(tile, axis, UP)
    above = lax.ppermute(tile, axis, DOWN)
    far_top = lax.ppermute(below[:half], axis, UP)
    far_bottom = lax.ppermute(above[half:], axis, DOWN)
    return [tile, below, above, far_top, far_bottom]


def product_kernel(*refs):
    x_own, x_peer, y_in = refs[:10], refs[10:20], refs[20:30]
    where_ref, pattern_ref, index_ref, xm_ref = refs[30:34]
    sign_ref, payload_ref = refs[34:36]
    x_buf, y_buf, acc, dens, x_sem, y_sem, out_sem = refs[36:]
    yl, xi, yh, z, core = (where_ref[k] for k in range(5))
    half = ROWS // 2
    own_cols = pl.ds(pl.multiple_of(core * COLS, COLS), COLS)
    peer_cols = pl.ds(pl.multiple_of((1 - core) * COLS, COLS), COLS)

    def place(group, member):
        position = group * 4 + min(member, 3)
        rows = {3: pl.ds(0, half), 4: pl.ds(half, half)}.get(member, pl.ds(0, ROWS))
        return position, rows

    for group in range(2):
        for member in range(5):
            position, rows = place(group, member)
            pltpu.make_async_copy(
                y_in[group * 5 + member], y_buf.at[position, rows], y_sem.at[position]
            ).start()
    for group in range(2):
        for member in range(5):
            position, rows = place(group, member)
            for source, cols in ((x_own, own_cols), (x_peer, peer_cols)):
                pltpu.make_async_copy(
                    source[group * 5 + member], x_buf.at[position, rows, cols], x_sem.at[position]
                ).start()

    acc[...] = jnp.zeros_like(acc)
    for position in range(8):
        pltpu.make_async_copy(y_buf.at[position], y_buf.at[position], y_sem.at[position]).wait()

    def step(position, carry):
        pltpu.make_async_copy(x_buf.at[position], x_buf.at[position], x_sem.at[position]).wait()
        group, member = position // 4, position % 4
        offset = jnp.where(member == 0, 0, jnp.where(member == 1, 3, jnp.where(member == 2, 1, 2)))
        t = yh ^ group
        s = (z + offset) % RING
        gap = (s - xi + RING) % RING
        y_member = jnp.where(gap == 0, 0, jnp.where(gap == 3, 1, jnp.where(gap == 1, 2, 3)))
        y_position = (t ^ yl) * 4 + y_member
        for part in range(2):
            rows = slice(part * half, (part + 1) * half)
            acc[rows, :] += jnp.dot(
                x_buf[position, rows, :], y_buf[y_position], preferred_element_type=jnp.float32
            )
        return carry

    lax.fori_loop(0, 8, step, 0)

    block_row = (yl * 4 + xi) * RB
    block_col = ((yh * 4 + z) * 2 + core) * QB
    same = lax.broadcasted_iota(jnp.int32, (BS, BS), 0) == lax.broadcasted_iota(jnp.int32, (BS, BS), 1)
    half_eye = jnp.where(same, 0.5, 0.0).astype(jnp.float32)

    def finish(i, carry):
        rows = pl.ds(pl.multiple_of(i * BS, BS), BS)
        for j in range(QB):
            cols = slice(j * BS, (j + 1) * BS)
            kept = jnp.where(pattern_ref[i, j] > 0, 0.5, 0.0)
            xnew = 1.5 * xm_ref[rows, cols].astype(jnp.float32) - kept * acc[rows, cols]
            sign_ref[rows, cols] = xnew.astype(jnp.bfloat16)
            on_diagonal = jnp.where(block_row + i == block_col + j, 1.0, 0.0)
            dens[i * QB + j] = (on_diagonal * half_eye - 0.5 * xnew).astype(jnp.bfloat16)
        return carry

    lax.fori_loop(0, RB, finish, 0)
    dens[BLOCKS] = jnp.zeros((BS, BS), jnp.bfloat16)

    slots = payload_ref.shape[0]

    def send(slot, carry):
        pltpu.make_async_copy(dens.at[index_ref[slot]], payload_ref.at[slot], out_sem).start()
        return carry

    lax.fori_loop(0, slots, send, 0)
    pltpu.make_async_copy(payload_ref, payload_ref, out_sem).wait()


def product_and_payload(x_own, x_peer, y_parts, where, pattern, index, xm):
    slots = index.shape[0]
    hbm = pl.BlockSpec(memory_space=pl.ANY)
    smem = pl.BlockSpec(memory_space=pltpu.SMEM)
    vmem = pl.BlockSpec(memory_space=pltpu.VMEM)
    return pl.pallas_call(
        product_kernel,
        in_specs=[hbm] * 30 + [smem] * 3 + [vmem],
        out_specs=[vmem, hbm],
        out_shape=[
            jax.ShapeDtypeStruct((ROWS, COLS), jnp.bfloat16),
            jax.ShapeDtypeStruct((slots, BS, BS), jnp.bfloat16),
        ],
        scratch_shapes=[
            pltpu.VMEM((8, ROWS, 2 * COLS), jnp.bfloat16),
            pltpu.VMEM((8, ROWS, COLS), jnp.bfloat16),
            pltpu.VMEM((ROWS, COLS), jnp.float32),
            pltpu.VMEM((BLOCKS + 1, BS, BS), jnp.bfloat16),
            pltpu.SemaphoreType.DMA((8,)),
            pltpu.SemaphoreType.DMA((8,)),
            pltpu.SemaphoreType.DMA,
        ],
        compiler_params=pltpu.CompilerParams(vmem_limit_bytes=48 * 2**20),
        cost_estimate=pl.CostEstimate(
            flops=2 * ROWS * COLS * 8 * ROWS, bytes_accessed=34 * 2**20, transcendentals=0
        ),
        name="product_payload",
    )(*x_own, *x_peer, *y_parts, where, pattern, index, xm)


FCH = 16


def force_kernel(d_ref, h_ref, s_ref, e_ref, out_ref):
    same = lax.broadcasted_iota(jnp.int32, (BS, BS), 0) == lax.broadcasted_iota(jnp.int32, (BS, BS), 1)
    ones = jnp.ones((BS, BS), jnp.bfloat16)
    for k in range(FCH):
        spread = jnp.where(same, e_ref[k : k + 1, :].astype(jnp.float32), 0.0).astype(jnp.bfloat16)
        energy = jnp.dot(spread, ones, preferred_element_type=jnp.float32)
        term = d_ref[k].astype(jnp.float32) * (
            h_ref[k].astype(jnp.float32) - energy * s_ref[k].astype(jnp.float32)
        )
        out_ref[k : k + 1, :] = jnp.sum(term, axis=0, keepdims=True)


def force_sums(dens, force_h, force_s, energy):
    slots = dens.shape[0]
    block = pl.BlockSpec((FCH, BS, BS), lambda i: (i, 0, 0))
    line = pl.BlockSpec((FCH, BS), lambda i: (i, 0))
    partial = pl.pallas_call(
        force_kernel,
        grid=(slots // FCH,),
        in_specs=[block, block, block, line],
        out_specs=line,
        out_shape=jax.ShapeDtypeStruct((slots, BS), jnp.float32),
        cost_estimate=pl.CostEstimate(
            flops=6 * slots * BS * BS, bytes_accessed=6 * slots * BS * BS, transcendentals=0
        ),
        name="force_sums",
    )(dens, force_h, force_s, energy)
    return jnp.sum(partial, axis=1)


def exchange(payload):
    return lax.all_to_all(payload, AXES, split_axis=0, concat_axis=0, tiled=True)


def shards(x, y, pattern_x, pattern_y, pattern_product, orbital_energy, pair_dest, pair_block, force_h, force_s):
    dest, wanted = pair_dest[0, :, 0], pair_block[0]
    slots = force_h.shape[0]
    entries = dest.shape[0]
    order = jnp.arange(entries, dtype=jnp.int32)
    earlier = (dest[:, None] == dest[None, :]) & (order[None, :] < order[:, None])
    rank = jnp.sum(earlier.astype(jnp.int32), axis=1)
    slot = dest * CAP + rank
    named = slot[None, :] == jnp.arange(slots, dtype=jnp.int32)[:, None]
    index = jnp.sum(jnp.where(named, wanted[None, :] - BLOCKS, 0), axis=1) + BLOCKS
    pick_row = (index[:, None] // QB == jnp.arange(RB, dtype=jnp.int32)[None, :]).astype(jnp.bfloat16)
    send_energy = jnp.dot(
        pick_row, orbital_energy.reshape(RB, BS), preferred_element_type=jnp.float32
    ).astype(jnp.bfloat16)

    xm, ym = masked_tiles(x, y, pattern_x, pattern_y)
    y_far = lax.ppermute(ym, "yl", SWAP)
    x_far = lax.ppermute(xm, "yh", SWAP)
    y_parts = ring_gather(ym, "x") + ring_gather(y_far, "x")
    x_own = ring_gather(xm, "z") + ring_gather(x_far, "z")
    x_peer = [lax.ppermute(part, "c", SWAP) for part in x_own]
    energy = exchange(send_energy)

    where = jnp.stack([lax.axis_index(axis) for axis in AXES]).astype(jnp.int32)
    sign_next, payload = product_and_payload(x_own, x_peer, y_parts, where, pattern_product, index, xm)
    received = exchange(payload)
    return sign_next, force_sums(received, force_h, force_s, energy)


def solution(mesh):
    fine = Mesh(mesh.devices.reshape(2, 4, 2, 4, 2), AXES)
    row, col = ("yl", "x"), ("yh", "z", "c")
    in_specs = (
        P(row, col),
        P(row, col),
        P(row, col),
        P(row, col),
        P(row, col),
        P(row),
        P(AXES, None, None),
        P(AXES, None),
        P(AXES, None, None),
        P(AXES, None, None),
    )
    out_specs = (P(row, col), P(AXES))
    return jax.shard_map(shards, mesh=fine, in_specs=in_specs, out_specs=out_specs, check_vma=False)
```

time: 426 us -> 283 us (0.66)
  waiting for transfers between devices: 211 us -> 65.9 us
  starting transfers between devices: 0.08 us -> 49.7 us
  Pallas kernels: 0 us -> 41.2 us
  local copies, waits for them, and re-layouts: 38.6 us -> 8.66 us
  other arithmetic: 28.9 us -> 1.88 us
  matrix products: 21.8 us -> 0.84 us
  between operations: 14.2 us -> 0.95 us
    all_gather x2 -> x0, waiting for transfers between devices: 211 us -> none  [the longest x1 123 us: shards(): lax.all_gather(xmask, 'col', axis=1, tiled=True)]
    ppermute x0 -> x28, waiting for transfers between devices: none -> 65.9 us  [the longest x4 29.9 us: ring_gather(): below = lax.ppermute(tile, axis, UP)]
    ppermute x0 -> x28, starting transfers between devices: none -> 44.4 us  [the longest x10 23.5 us: shards(): x_peer = [lax.ppermute(part, 'c', SWAP) for part in x_own]]
    pallas_call x0 -> x3, Pallas kernels: none -> 41.2 us  [the longest x1 21 us: product_and_payload(): pl.pallas_call(product_kernel, in_specs=[hbm] * 30 + [smem] * 3 + [vmem],...]
    reshape x4 -> x0, local copies, waits for them, and re-layouts: 27.9 us -> none  [the longest x1 14.2 us: shards(): received = received.reshape(slots, height, BS)]
    dot_general x3 -> x1, matrix products: 21.8 us -> 0.84 us  [shards(): jnp.dot(pick_row, orbital_energy.reshape(RB, BS), preferred_element_type=...]
    dot_general x1 -> x0, other arithmetic: 11.8 us -> none  [shards(): jnp.einsum('sab,sab->sa', recv_dens, force_s, preferred_element_type=jnp....]
    concatenate x1 -> x0, other arithmetic: 8.97 us -> none  [shards(): jnp.concatenate([send_dens.reshape(slots, BS, BS), send_energy[:, None, :...]
  transfers between devices with their start and end apart: 2 -> 29, of which waited for: 2 -> 8; matrix products, arithmetic and copies ran while one was open for 1% -> 2% of each run, Pallas kernels for 0% -> 7%
where the time goes in v1:
time: 283 us; the launch traced here: 281 us
  blocking collectives  111 us (39%)
  waiting for transfers between devices  65.9 us (23%)
  starting transfers between devices  49.7 us (18%)
  Pallas kernels  41.2 us (15%)
  local copies, waits for them, and re-layouts  8.66 us (3%)
    all_to_all x1, blocking collectives, exchange(): lax.all_to_all(payload, AXES, split_axis=0, concat_axis=0, tiled=True)  111 us
    ppermute x4, waiting for transfers between devices, ring_gather(): below = lax.ppermute(tile, axis, UP)  29.9 us
    ppermute x10, starting transfers between devices, shards(): x_peer = [lax.ppermute(part, 'c', SWAP) for part in x_own]  23.5 us
    pallas_call x1, Pallas kernels, product_and_payload(): pl.pallas_call(product_kernel, in_specs=[hbm] * 30 + [smem] * 3 + [vmem],...  21 us
    ppermute x1, waiting for transfers between devices, shards(): y_far = lax.ppermute(ym, 'yl', SWAP)  20 us
    pallas_call x1, Pallas kernels, force_sums(): pl.pallas_call(force_kernel, grid=(slots // FCH,), in_specs=[block, block...  16.3 us
    ppermute x4, waiting for transfers between devices, ring_gather(): far_top = lax.ppermute(below[:half], axis, UP)  12.2 us
    ppermute x4, starting transfers between devices, ring_gather(): above = lax.ppermute(tile, axis, DOWN)  6.67 us
  transfers between devices with their start and end apart: 29, of which 8 were waited for; matrix products, arithmetic and copies ran while one was open for 2% of the time, Pallas kernels for 7%

profile of v1, /device:TPU:7, one launch (start us, length us, event | category | flops | bytes accessed | tf_op | source)
XLA Modules:
  0.0 280.6 jit_solution(12982981147651589649)
XLA Ops:
  3.4 3.9 %mask_tiles.1 = (bf16[1024,512]{1,0:T(8,128)(2,1)}, bf16[1024,512]{1,0:T(8,128)(2,1)}) custom-call(s32[8,4]{1,0:T(8,128)} %copy.15.px_ref, s32[8,4]{1,0:T(8,128)} %copy.16.py_ref, bf16[1024,512]{1,0:T(8,128)(2,1)} %x_ref.1, bf16[1024,512]{1,0:T(8,128)(2,1)} %y_ref.1), custom_call_target="tpu_custom_call" | custom-call | flops 1048576 | bytes 4194304 | tf_op jit(solution)/shard_map/mask_tiles/pallas_call | solution.py:35
  7.3 1.6 collective-permute-start
  9.0 2.2 collective-permute-start.1
  11.4 2.9 %collective-permute-start.4 = (bf16[1024,512]{1,0:T(8,128)(2,1)}, bf16[1024,512]{1,0:T(8,128)(2,1)S(1)}, u32[]{:S(2)}, u32[]{:S(2)}) collective-permute-start(bf16[1024,512]{1,0:T(8,128)(2,1)} %get-tuple-element.6.refs_0_.refs_33_), channel_id=1, source_target_pairs={{0,8},{8,0},{1,9},{9,1},{2,10},{10,2},{3,11},{11,3},{4,12},{12,4},... | collective-permute-start | bytes 3145736 | tf_op jit(solution)/shard_map/ppermute | solution.py:219
  14.7 19.5 %collective-permute-done.refs_1_ = bf16[1024,512]{1,0:T(8,128)(2,1)S(1)} collective-permute-done((bf16[1024,512]{1,0:T(8,128)(2,1)}, bf16[1024,512]{1,0:T(8,128)(2,1)S(1)}, u32[]{:S(2)}, u32[]{:S(2)}) %collective-permute-start) | collective-permute-done | bytes 1048608 | tf_op jit(solution)/shard_map/ppermute | solution.py:48
  37.3 1.9 collective-permute-start.3
  39.2 20.0 %collective-permute-done.23.refs_25_ = bf16[1024,512]{1,0:T(8,128)(2,1)S(1)} collective-permute-done((bf16[1024,512]{1,0:T(8,128)(2,1)}, bf16[1024,512]{1,0:T(8,128)(2,1)S(1)}, u32[]{:S(2)}, u32[]{:S(2)}) %collective-permute-start.23) | collective-permute-done | bytes 1048608 | tf_op jit(solution)/shard_map/ppermute | solution.py:218
  59.3 2.7 collective-permute-start.6
  64.8 8.0 %collective-permute-done.21.refs_23_ = bf16[512,512]{1,0:T(8,128)(2,1)S(1)} collective-permute-done((bf16[512,512]{1,0:T(8,128)(2,1)S(1)}, bf16[512,512]{1,0:T(8,128)(2,1)S(1)}, u32[]{:S(2)}, u32[]{:S(2)}) %collective-permute-start.21) | collective-permute-done | bytes 524320 | tf_op jit(solution)/shard_map/ppermute | solution.py:50
  72.8 6.8 %collective-permute-start.12 = (bf16[512,512]{1,0:T(8,128)(2,1)S(1)}, bf16[512,512]{1,0:T(8,128)(2,1)S(1)}, u32[]{:S(2)}, u32[]{:S(2)}) collective-permute-start(bf16[512,512]{1,0:T(8,128)(2,1)S(1)} %collective-permute-done.2.refs_3_), channel_id=1, source_target_pairs={{0,1},{1,0},{2,3},{3,2},{4,5},{5,4},{6,7},{7,6},{8,9},{9,8},{10,11... | collective-permute-start | bytes 1572872 | tf_op jit(solution)/shard_map/ppermute | solution.py:222
  80.1 3.0 %collective-permute-done.5.refs_6_ = bf16[1024,512]{1,0:T(8,128)(2,1)} collective-permute-done((bf16[1024,512]{1,0:T(8,128)(2,1)S(1)}, bf16[1024,512]{1,0:T(8,128)(2,1)}, u32[]{:S(2)}, u32[]{:S(2)}) %collective-permute-start.5) | collective-permute-done | bytes 1048608 | tf_op jit(solution)/shard_map/ppermute | solution.py:48
  84.4 3.4 %collective-permute-start.10 = (bf16[1024,512]{1,0:T(8,128)(2,1)S(1)}, bf16[1024,512]{1,0:T(8,128)(2,1)S(1)}, u32[]{:S(2)}, u32[]{:S(2)}) collective-permute-start(bf16[1024,512]{1,0:T(8,128)(2,1)S(1)} %collective-permute-done.refs_1_), channel_id=1, source_target_pairs={{0,1},{1,0},{2,3},{3,2},{4,5},{5,4},{6,7},{7,6},{8,9},{9,8},{10,11... | collective-permute-start | bytes 3145736 | tf_op jit(solution)/shard_map/ppermute | solution.py:222
  87.8 7.3 %collective-permute-done.24.refs_26_ = bf16[1024,512]{1,0:T(8,128)(2,1)S(1)} collective-permute-done((bf16[1024,512]{1,0:T(8,128)(2,1)S(1)}, bf16[1024,512]{1,0:T(8,128)(2,1)S(1)}, u32[]{:S(2)}, u32[]{:S(2)}) %collective-permute-start.24) | collective-permute-done | bytes 1048608 | tf_op jit(solution)/shard_map/ppermute | solution.py:48
  95.2 3.6 %collective-permute-start.13 = (bf16[512,512]{1,0:T(8,128)(2,1)S(1)}, bf16[512,512]{1,0:T(8,128)(2,1)S(1)}, u32[]{:S(2)}, u32[]{:S(2)}) collective-permute-start(bf16[512,512]{1,0:T(8,128)(2,1)S(1)} %collective-permute-done.3.refs_4_), channel_id=1, source_target_pairs={{0,1},{1,0},{2,3},{3,2},{4,5},{5,4},{6,7},{7,6},{8,9},{9,8},{10,11... | collective-permute-start | bytes 1572872 | tf_op jit(solution)/shard_map/ppermute | solution.py:222
  101.1 2.6 collective-permute-start.8
  103.8 2.2 collective-permute-done.25.refs_27_
  106.2 4.0 %collective-permute-start.15 = (bf16[1024,512]{1,0:T(8,128)(2,1)}, bf16[1024,512]{1,0:T(8,128)(2,1)}, u32[]{:S(2)}, u32[]{:S(2)}) collective-permute-start(bf16[1024,512]{1,0:T(8,128)(2,1)} %collective-permute-done.5.refs_6_), channel_id=1, source_target_pairs={{0,1},{1,0},{2,3},{3,2},{4,5},{5,4},{6,7},{7,6},{8,9},{9,8},{10,11... | collective-permute-start | bytes 3145736 | tf_op jit(solution)/shard_map/ppermute | solution.py:222
  111.3 4.2 %collective-permute-done.7.refs_8_ = bf16[512,512]{1,0:T(8,128)(2,1)} collective-permute-done((bf16[512,512]{1,0:T(8,128)(2,1)S(1)}, bf16[512,512]{1,0:T(8,128)(2,1)}, u32[]{:S(2)}, u32[]{:S(2)}) %collective-permute-start.7) | collective-permute-done | bytes 524320 | tf_op jit(solution)/shard_map/ppermute | solution.py:50
  119.1 2.0 collective-permute-start.18
  122.2 5.3 %all-to-all-start.1 = ((bf16[128,2,128]{2,1,0:T(2,128)(2,1)}), bf16[128,2,128]{2,1,0:T(2,128)(2,1)S(1)}, u32[]{:S(2)}, u32[]{:S(2)}) async-start(bf16[128,2,128]{2,1,0:T(2,128)(2,1)} %bitcast.8), calls=%async_computation.1 | async-start | bytes 131072 | tf_op jit(solution)/shard_map/all_to_all | solution.py:199
  130.3 21.0 %product_payload.1 = (bf16[1024,512]{1,0:T(8,128)(2,1)}, bf16[256,128,128]{2,1,0:T(8,128)(2,1)}) custom-call(bf16[1024,512]{1,0:T(8,128)(2,1)} %get-tuple-element.6.refs_0_.refs_33_, bf16[1024,512]{1,0:T(8,128)(2,1)} %copy-done.4, bf16[1024,512]{1,0:T(8,128)(2,1)} %copy-done.5, bf16[512,512]{1,0:T(8,128)(2,1)S(1)} %collective-permute-done.2.refs_3_, ...), custom_call_target="tpu_custom_call" | custom-call | flops 8589934592 | bytes 35651584 | tf_op jit(solution)/shard_map/product_payload/pallas_call | solution.py:140
  151.3 111.4 %all_to_all.16.d_ref = bf16[256,128,128]{2,1,0:T(8,128)(2,1)} all-to-all(bf16[256,128,128]{2,1,0:T(8,128)(2,1)} %get-tuple-element.9), channel_id=1, replica_groups=mesh['yl'=2,'x'=4,'yh'=2,'z'=4,'c'=2] {'yl','x','yh','z','c'}, dimensions={0} | all-to-all | bytes 16777216 | tf_op jit(solution)/shard_map/all_to_all | solution.py:199
  262.7 16.3 %force_sums.1 = f32[256,128]{1,0:T(8,128)} custom-call(bf16[256,128,128]{2,1,0:T(8,128)(2,1)} %all_to_all.16.d_ref, bf16[256,128,128]{2,1,0:T(8,128)(2,1)} %h_ref.1, bf16[256,128,128]{2,1,0:T(8,128)(2,1)} %s_ref.1, bf16[256,128]{1,0:T(8,128)(2,1)} %bitcast.14), custom_call_target="tpu_custom_call" | custom-call | flops 25165824 | bytes 25165824 | tf_op jit(solution)/shard_map/force_sums/pallas_call | solution.py:184
  279.0 1.6 reduce_sum.29
  (95 shorter events, 22.0 us)
Async XLA Ops:
  7.3 26.9 %collective-permute-start = (bf16[1024,512]{1,0:T(8,128)(2,1)}, bf16[1024,512]{1,0:T(8,128)(2,1)S(1)}, u32[]{:S(2)}, u32[]{:S(2)}) collective-permute-start(bf16[1024,512]{1,0:T(8,128)(2,1)} %get-tuple-element.6.refs_0_.refs_33_), channel_id=1, source_target_pairs={{0,2},{2,4},{4,6},{6,0},{1,3},{3,5},{5,7},{7,1},{8,10},{10,12},{12... | collective-permute-start | bytes 3145736 | tf_op jit(solution)/shard_map/ppermute | solution.py:48
  9.0 25.8 %collective-permute-start.1 = (bf16[1024,512]{1,0:T(8,128)(2,1)}, bf16[1024,512]{1,0:T(8,128)(2,1)S(1)}, u32[]{:S(2)}, u32[]{:S(2)}) collective-permute-start(bf16[1024,512]{1,0:T(8,128)(2,1)} %get-tuple-element.6.refs_0_.refs_33_), channel_id=1, source_target_pairs={{0,6},{2,0},{4,2},{6,4},{1,7},{3,1},{5,3},{7,5},{8,14},{10,8},{12,... | collective-permute-start | bytes 3145736 | tf_op jit(solution)/shard_map/ppermute | solution.py:49
  11.2 25.2 %collective-permute-start.19 = (bf16[1024,512]{1,0:T(8,128)(2,1)}, bf16[1024,512]{1,0:T(8,128)(2,1)S(1)}, u32[]{:S(2)}, u32[]{:S(2)}) collective-permute-start(bf16[1024,512]{1,0:T(8,128)(2,1)} %get-tuple-element.7.refs_20_), channel_id=1, source_target_pairs={{0,16},{16,32},{32,48},{48,0},{1,17},{17,33},{33,49},{49,1},{2,18}... | collective-permute-start | bytes 3145736 | tf_op jit(solution)/shard_map/ppermute | solution.py:48
  11.4 26.0 %collective-permute-start.4 = (bf16[1024,512]{1,0:T(8,128)(2,1)}, bf16[1024,512]{1,0:T(8,128)(2,1)S(1)}, u32[]{:S(2)}, u32[]{:S(2)}) collective-permute-start(bf16[1024,512]{1,0:T(8,128)(2,1)} %get-tuple-element.6.refs_0_.refs_33_), channel_id=1, source_target_pairs={{0,8},{8,0},{1,9},{9,1},{2,10},{10,2},{3,11},{11,3},{4,12},{12,4},... | collective-permute-start | bytes 3145736 | tf_op jit(solution)/shard_map/ppermute | solution.py:219
  14.3 45.0 %collective-permute-start.23 = (bf16[1024,512]{1,0:T(8,128)(2,1)}, bf16[1024,512]{1,0:T(8,128)(2,1)S(1)}, u32[]{:S(2)}, u32[]{:S(2)}) collective-permute-start(bf16[1024,512]{1,0:T(8,128)(2,1)} %get-tuple-element.7.refs_20_), channel_id=1, source_target_pairs={{0,64},{64,0},{1,65},{65,1},{2,66},{66,2},{3,67},{67,3},{4,68},{68... | collective-permute-start | bytes 3145736 | tf_op jit(solution)/shard_map/ppermute | solution.py:218
  34.2 25.1 %collective-permute-start.20 = (bf16[1024,512]{1,0:T(8,128)(2,1)}, bf16[1024,512]{1,0:T(8,128)(2,1)S(1)}, u32[]{:S(2)}, u32[]{:S(2)}) collective-permute-start(bf16[1024,512]{1,0:T(8,128)(2,1)} %get-tuple-element.7.refs_20_), channel_id=1, source_target_pairs={{0,48},{16,0},{32,16},{48,32},{1,49},{17,1},{33,17},{49,33},{2,50}... | collective-permute-start | bytes 3145736 | tf_op jit(solution)/shard_map/ppermute | solution.py:49
  34.7 27.2 %collective-permute-start.9 = (bf16[1024,512]{1,0:T(8,128)(2,1)}, bf16[1024,512]{1,0:T(8,128)(2,1)S(1)}, u32[]{:S(2)}, u32[]{:S(2)}) collective-permute-start(bf16[1024,512]{1,0:T(8,128)(2,1)} %get-tuple-element.6.refs_0_.refs_33_), channel_id=1, source_target_pairs={{0,1},{1,0},{2,3},{3,2},{4,5},{5,4},{6,7},{7,6},{8,9},{9,8},{10,11... | collective-permute-start | bytes 3145736 | tf_op jit(solution)/shard_map/ppermute | solution.py:222
  36.3 26.9 %collective-permute-start.2 = (bf16[512,512]{1,0:T(8,128)(2,1)S(1)}, bf16[512,512]{1,0:T(8,128)(2,1)S(1)}, u32[]{:S(2)}, u32[]{:S(2)}) collective-permute-start(bf16[512,512]{1,0:T(8,128)(2,1)S(1)} %slice.32), channel_id=1, source_target_pairs={{0,2},{2,4},{4,6},{6,0},{1,3},{3,5},{5,7},{7,1},{8,10},{10,12},{12... | collective-permute-start | bytes 1572872 | tf_op jit(solution)/shard_map/ppermute | solution.py:50
  37.3 27.2 %collective-permute-start.3 = (bf16[512,512]{1,0:T(8,128)(2,1)S(1)}, bf16[512,512]{1,0:T(8,128)(2,1)S(1)}, u32[]{:S(2)}, u32[]{:S(2)}) collective-permute-start(bf16[512,512]{1,0:T(8,128)(2,1)S(1)} %slice.33), channel_id=1, source_target_pairs={{0,6},{2,0},{4,2},{6,4},{1,7},{3,1},{5,3},{7,5},{8,14},{10,8},{12,... | collective-permute-start | bytes 1572872 | tf_op jit(solution)/shard_map/ppermute | solution.py:51
  59.3 23.8 %collective-permute-start.5 = (bf16[1024,512]{1,0:T(8,128)(2,1)S(1)}, bf16[1024,512]{1,0:T(8,128)(2,1)}, u32[]{:S(2)}, u32[]{:S(2)}) collective-permute-start(bf16[1024,512]{1,0:T(8,128)(2,1)S(1)} %collective-permute-done.4.refs_5_), channel_id=1, source_target_pairs={{0,2},{2,4},{4,6},{6,0},{1,3},{3,5},{5,7},{7,1},{8,10},{10,12},{12... | collective-permute-start | bytes 3145736 | tf_op jit(solution)/shard_map/ppermute | solution.py:48
  59.3 25.1 %collective-permute-start.6 = (bf16[1024,512]{1,0:T(8,128)(2,1)S(1)}, bf16[1024,512]{1,0:T(8,128)(2,1)}, u32[]{:S(2)}, u32[]{:S(2)}) collective-permute-start(bf16[1024,512]{1,0:T(8,128)(2,1)S(1)} %collective-permute-done.4.refs_5_), channel_id=1, source_target_pairs={{0,6},{2,0},{4,2},{6,4},{1,7},{3,1},{5,3},{7,5},{8,14},{10,8},{12,... | collective-permute-start | bytes 3145736 | tf_op jit(solution)/shard_map/ppermute | solution.py:49
  63.3 31.9 %collective-permute-start.24 = (bf16[1024,512]{1,0:T(8,128)(2,1)S(1)}, bf16[1024,512]{1,0:T(8,128)(2,1)S(1)}, u32[]{:S(2)}, u32[]{:S(2)}) collective-permute-start(bf16[1024,512]{1,0:T(8,128)(2,1)S(1)} %collective-permute-done.23.refs_25_), channel_id=1, source_target_pairs={{0,16},{16,32},{32,48},{48,0},{1,17},{17,33},{33,49},{49,1},{2,18}... | collective-permute-start | bytes 3145736 | tf_op jit(solution)/shard_map/ppermute | solution.py:48
  64.5 15.0 %collective-permute-start.22 = (bf16[512,512]{1,0:T(8,128)(2,1)S(1)}, bf16[512,512]{1,0:T(8,128)(2,1)S(1)}, u32[]{:S(2)}, u32[]{:S(2)}) collective-permute-start(bf16[512,512]{1,0:T(8,128)(2,1)S(1)} %slice.37), channel_id=1, source_target_pairs={{0,48},{16,0},{32,16},{48,32},{1,49},{17,1},{33,17},{49,33},{2,50}... | collective-permute-start | bytes 1572872 | tf_op jit(solution)/shard_map/ppermute | solution.py:51
  72.8 15.0 %collective-permute-start.12 = (bf16[512,512]{1,0:T(8,128)(2,1)S(1)}, bf16[512,512]{1,0:T(8,128)(2,1)S(1)}, u32[]{:S(2)}, u32[]{:S(2)}) collective-permute-start(bf16[512,512]{1,0:T(8,128)(2,1)S(1)} %collective-permute-done.2.refs_3_), channel_id=1, source_target_pairs={{0,1},{1,0},{2,3},{3,2},{4,5},{5,4},{6,7},{7,6},{8,9},{9,8},{10,11... | collective-permute-start | bytes 1572872 | tf_op jit(solution)/shard_map/ppermute | solution.py:222
  79.6 21.5 %collective-permute-start.14 = (bf16[1024,512]{1,0:T(8,128)(2,1)S(1)}, bf16[1024,512]{1,0:T(8,128)(2,1)S(1)}, u32[]{:S(2)}, u32[]{:S(2)}) collective-permute-start(bf16[1024,512]{1,0:T(8,128)(2,1)S(1)} %collective-permute-done.4.refs_5_), channel_id=1, source_target_pairs={{0,1},{1,0},{2,3},{3,2},{4,5},{5,4},{6,7},{7,6},{8,9},{9,8},{10,11... | collective-permute-start | bytes 3145736 | tf_op jit(solution)/shard_map/ppermute | solution.py:222
  83.1 22.9 %collective-permute-start.25 = (bf16[1024,512]{1,0:T(8,128)(2,1)S(1)}, bf16[1024,512]{1,0:T(8,128)(2,1)S(1)}, u32[]{:S(2)}, u32[]{:S(2)}) collective-permute-start(bf16[1024,512]{1,0:T(8,128)(2,1)S(1)} %collective-permute-done.23.refs_25_), channel_id=1, source_target_pairs={{0,48},{16,0},{32,16},{48,32},{1,49},{17,1},{33,17},{49,33},{2,50}... | collective-permute-start | bytes 3145736 | tf_op jit(solution)/shard_map/ppermute | solution.py:49
  84.4 21.8 %collective-permute-start.10 = (bf16[1024,512]{1,0:T(8,128)(2,1)S(1)}, bf16[1024,512]{1,0:T(8,128)(2,1)S(1)}, u32[]{:S(2)}, u32[]{:S(2)}) collective-permute-start(bf16[1024,512]{1,0:T(8,128)(2,1)S(1)} %collective-permute-done.refs_1_), channel_id=1, source_target_pairs={{0,1},{1,0},{2,3},{3,2},{4,5},{5,4},{6,7},{7,6},{8,9},{9,8},{10,11... | collective-permute-start | bytes 3145736 | tf_op jit(solution)/shard_map/ppermute | solution.py:222
  87.7 22.4 %collective-permute-start.11 = (bf16[1024,512]{1,0:T(8,128)(2,1)S(1)}, bf16[1024,512]{1,0:T(8,128)(2,1)S(1)}, u32[]{:S(2)}, u32[]{:S(2)}) collective-permute-start(bf16[1024,512]{1,0:T(8,128)(2,1)S(1)} %collective-permute-done.1.refs_2_), channel_id=1, source_target_pairs={{0,1},{1,0},{2,3},{3,2},{4,5},{5,4},{6,7},{7,6},{8,9},{9,8},{10,11... | collective-permute-start | bytes 3145736 | tf_op jit(solution)/shard_map/ppermute | solution.py:222
  101.0 14.5 %collective-permute-start.7 = (bf16[512,512]{1,0:T(8,128)(2,1)S(1)}, bf16[512,512]{1,0:T(8,128)(2,1)}, u32[]{:S(2)}, u32[]{:S(2)}) collective-permute-start(bf16[512,512]{1,0:T(8,128)(2,1)S(1)} %slice.34), channel_id=1, source_target_pairs={{0,2},{2,4},{4,6},{6,0},{1,3},{3,5},{5,7},{7,1},{8,10},{10,12},{12... | collective-permute-start | bytes 1572872 | tf_op jit(solution)/shard_map/ppermute | solution.py:50
  101.1 15.7 %collective-permute-start.8 = (bf16[512,512]{1,0:T(8,128)(2,1)S(1)}, bf16[512,512]{1,0:T(8,128)(2,1)}, u32[]{:S(2)}, u32[]{:S(2)}) collective-permute-start(bf16[512,512]{1,0:T(8,128)(2,1)S(1)} %slice.35), channel_id=1, source_target_pairs={{0,6},{2,0},{4,2},{6,4},{1,7},{3,1},{5,3},{7,5},{8,14},{10,8},{12,... | collective-permute-start | bytes 1572872 | tf_op jit(solution)/shard_map/ppermute | solution.py:51
  106.2 23.1 %collective-permute-start.15 = (bf16[1024,512]{1,0:T(8,128)(2,1)}, bf16[1024,512]{1,0:T(8,128)(2,1)}, u32[]{:S(2)}, u32[]{:S(2)}) collective-permute-start(bf16[1024,512]{1,0:T(8,128)(2,1)} %collective-permute-done.5.refs_6_), channel_id=1, source_target_pairs={{0,1},{1,0},{2,3},{3,2},{4,5},{5,4},{6,7},{7,6},{8,9},{9,8},{10,11... | collective-permute-start | bytes 3145736 | tf_op jit(solution)/shard_map/ppermute | solution.py:222
  110.2 19.1 %collective-permute-start.16 = (bf16[1024,512]{1,0:T(8,128)(2,1)}, bf16[1024,512]{1,0:T(8,128)(2,1)}, u32[]{:S(2)}, u32[]{:S(2)}) collective-permute-start(bf16[1024,512]{1,0:T(8,128)(2,1)} %collective-permute-done.6.refs_7_), channel_id=1, source_target_pairs={{0,1},{1,0},{2,3},{3,2},{4,5},{5,4},{6,7},{7,6},{8,9},{9,8},{10,11... | collective-permute-start | bytes 3145736 | tf_op jit(solution)/shard_map/ppermute | solution.py:222
  115.5 13.7 %collective-permute-start.27 = (bf16[512,512]{1,0:T(8,128)(2,1)}, bf16[512,512]{1,0:T(8,128)(2,1)}, u32[]{:S(2)}, u32[]{:S(2)}) collective-permute-start(bf16[512,512]{1,0:T(8,128)(2,1)} %slice.39), channel_id=1, source_target_pairs={{0,48},{16,0},{32,16},{48,32},{1,49},{17,1},{33,17},{49,33},{2,50}... | collective-permute-start | bytes 1572872 | tf_op jit(solution)/shard_map/ppermute | solution.py:51
  122.2 29.2 %all-to-all-start.1 = ((bf16[128,2,128]{2,1,0:T(2,128)(2,1)}), bf16[128,2,128]{2,1,0:T(2,128)(2,1)S(1)}, u32[]{:S(2)}, u32[]{:S(2)}) async-start(bf16[128,2,128]{2,1,0:T(2,128)(2,1)} %bitcast.8), calls=%async_computation.1 | async-start | bytes 131072 | tf_op jit(solution)/shard_map/all_to_all | solution.py:199
  (24 other events, 1081.3 us)

commit v2 on v1

v2 whole, which is shorter than its diff:
```python
import jax
import jax.numpy as jnp
from jax import lax
from jax.experimental import pallas as pl
from jax.experimental.pallas import tpu as pltpu
from jax.sharding import Mesh, PartitionSpec as P

BS = 128
QB = 4
CAP = 2
RB = 8
BLOCKS = RB * QB
ROWS = RB * BS
COLS = QB * BS
RING = 4
AXES = ("yl", "x", "yh", "z", "c")
SWAP = [(0, 1), (1, 0)]
UP = [(i, (i + 1) % RING) for i in range(RING)]
DOWN = [(i, (i - 1) % RING) for i in range(RING)]


def mask_x_kernel(p_ref, x_ref, o_ref):
    i = pl.program_id(0)
    for r in range(2):
        for j in range(QB):
            rows, cols = slice(r * BS, (r + 1) * BS), slice(j * BS, (j + 1) * BS)
            keep = (p_ref[j, i * 2 + r] > 0).astype(jnp.float32).astype(jnp.bfloat16)
            o_ref[rows, cols] = x_ref[rows, cols] * keep


def mask_y_kernel(where_ref, p_ref, q_ref, y_ref, z_ref, o_ref):
    first = where_ref[4] * (RB // 2) + pl.program_id(0) * 2
    for r in range(2):
        for j in range(QB):
            rows, cols = slice(r * BS, (r + 1) * BS), slice(j * BS, (j + 1) * BS)
            far_cols = slice(COLS + j * BS, COLS + (j + 1) * BS)
            keep = (p_ref[j, first + r] > 0).astype(jnp.float32).astype(jnp.bfloat16)
            o_ref[rows, cols] = y_ref[rows, cols] * keep
            keep = (q_ref[j, first + r] > 0).astype(jnp.float32).astype(jnp.bfloat16)
            o_ref[rows, far_cols] = z_ref[rows, cols] * keep


SMEM = pl.BlockSpec(memory_space=pltpu.SMEM)
VMEM = pl.BlockSpec(memory_space=pltpu.VMEM)
HBM = pl.BlockSpec(memory_space=pltpu.HBM)


def mask_x(x, pattern):
    tile = pl.BlockSpec((2 * BS, COLS), lambda i: (i, 0))
    return pl.pallas_call(
        mask_x_kernel,
        grid=(RB // 2,),
        in_specs=[SMEM, tile],
        out_specs=tile,
        out_shape=jax.ShapeDtypeStruct((ROWS, COLS), jnp.bfloat16),
        cost_estimate=pl.CostEstimate(flops=ROWS * COLS, bytes_accessed=4 * ROWS * COLS, transcendentals=0),
        name="mask_x",
    )(pattern, x)


def mask_y(y, y_peer, pattern, pattern_peer, where):
    tile = pl.BlockSpec((2 * BS, COLS), lambda i, w: (w[4] * (RB // 4) + i, 0))
    return pl.pallas_call(
        mask_y_kernel,
        grid_spec=pltpu.PrefetchScalarGridSpec(
            num_scalar_prefetch=1,
            grid=(RB // 4,),
            in_specs=[SMEM, SMEM, tile, tile],
            out_specs=pl.BlockSpec((2 * BS, 2 * COLS), lambda i, w: (i, 0)),
        ),
        out_shape=jax.ShapeDtypeStruct((ROWS // 2, 2 * COLS), jnp.bfloat16),
        cost_estimate=pl.CostEstimate(flops=ROWS * COLS, bytes_accessed=4 * ROWS * COLS, transcendentals=0),
        name="mask_y",
    )(where, pattern, pattern_peer, y, y_peer)


def after(value, *others):
    return lax.optimization_barrier((value,) + others)[0]


def y_place(where_ref, position):
    yl, xi, yh, z = (where_ref[k] for k in range(4))
    member = position % 4
    offset = jnp.where(member == 0, 0, jnp.where(member == 1, 3, jnp.where(member == 2, 1, 2)))
    gap = (z + offset - xi + 2 * RING) % RING
    y_member = jnp.where(gap == 0, 0, jnp.where(gap == 3, 1, jnp.where(gap == 1, 2, 3)))
    return (yh ^ (position // 4) ^ yl) * 4 + y_member


X_PIECES = ((0, 0, 2), (1, 0, 2), (2, 0, 2), (3, 0, 1), (3, 1, 1), (4, 0, 1), (4, 1, 1), (5, 0, 1), (5, 1, 1), (6, 0, 1), (6, 1, 1))
Y_PIECES = ((0, 0, 2), (1, 0, 2), (2, 0, 2), (3, 0, 1), (3, 1, 1), (4, 0, 2), (5, 0, 2), (6, 0, 2))
EARLY = 7


def early_kernel(*refs):
    nx, ny = len(X_PIECES), len(Y_PIECES)
    x_in, y_in, where_ref = refs[:nx], refs[nx : nx + ny], refs[nx + ny]
    own_ref, far_ref, x_late, y_late = refs[nx + ny + 1 : nx + ny + 5]
    x_buf, y_buf, x_sem, y_sem = refs[nx + ny + 5 :]

    for k in range(max(nx, ny)):
        for pieces, source, buf, sem, half in (
            (X_PIECES, x_in, x_buf, x_sem, ROWS // 2),
            (Y_PIECES, y_in, y_buf, y_sem, ROWS // 4),
        ):
            if k < len(pieces):
                position, start, size = pieces[k]
                target = buf.at[position, pl.ds(start * half, size * half)]
                pltpu.make_async_copy(source[k], target, sem.at[position]).start()

    own_ref[...] = jnp.zeros_like(own_ref)
    far_ref[...] = jnp.zeros_like(far_ref)

    def step(position, carry):
        pltpu.make_async_copy(x_buf.at[position], x_buf.at[position], x_sem.at[position]).wait()
        y_position = y_place(where_ref, position)

        @pl.when(y_position != EARLY)
        def _():
            pltpu.make_async_copy(y_buf.at[y_position], y_buf.at[y_position], y_sem.at[y_position]).wait()
            for out_ref, cols in ((own_ref, slice(0, COLS)), (far_ref, slice(COLS, 2 * COLS))):
                out_ref[...] += jnp.dot(
                    x_buf[position], y_buf[y_position, :, cols], preferred_element_type=jnp.float32
                )

        @pl.when(y_position == EARLY)
        def _():
            x_late[...] = x_buf[position]

        return carry

    lax.fori_loop(0, EARLY, step, 0)
    last = y_place(where_ref, EARLY)

    @pl.when(last != EARLY)
    def _():
        pltpu.make_async_copy(y_buf.at[last], y_buf.at[last], y_sem.at[last]).wait()
        y_late[...] = y_buf[last]


def early_product(x_parts, y_parts, where):
    return pl.pallas_call(
        early_kernel,
        in_specs=[HBM] * (len(X_PIECES) + len(Y_PIECES)) + [SMEM],
        out_specs=[VMEM] * 4,
        out_shape=[
            jax.ShapeDtypeStruct((ROWS, COLS), jnp.float32),
            jax.ShapeDtypeStruct((ROWS, COLS), jnp.float32),
            jax.ShapeDtypeStruct((ROWS, COLS), jnp.bfloat16),
            jax.ShapeDtypeStruct((ROWS // 2, 2 * COLS), jnp.bfloat16),
        ],
        scratch_shapes=[
            pltpu.VMEM((EARLY, ROWS, COLS), jnp.bfloat16),
            pltpu.VMEM((EARLY, ROWS // 2, 2 * COLS), jnp.bfloat16),
            pltpu.SemaphoreType.DMA((EARLY,)),
            pltpu.SemaphoreType.DMA((EARLY,)),
        ],
        compiler_params=pltpu.CompilerParams(vmem_limit_bytes=36 * 2**20),
        cost_estimate=pl.CostEstimate(
            flops=14 * ROWS * COLS * ROWS, bytes_accessed=20 * 2**20, transcendentals=0
        ),
        name="early_product",
    )(*x_parts, *y_parts, where)


def late_kernel(where_ref, x_top, x_bottom, y_top, y_bottom, x_late, y_late, own_ref, far_ref, own_out, far_out):
    last = y_place(where_ref, EARLY)
    half, quarter = ROWS // 2, ROWS // 4

    def add(same_chunk):
        for sum_ref, out_ref, cols in (
            (own_ref, own_out, slice(0, COLS)),
            (far_ref, far_out, slice(COLS, 2 * COLS)),
        ):
            for rows, x_ref in ((slice(0, half), x_top), (slice(half, ROWS), x_bottom)):
                total = sum_ref[rows, :]
                x_last = x_ref if same_chunk else x_late.at[rows]
                total += jnp.dot(x_last[:, :quarter], y_top[:, cols], preferred_element_type=jnp.float32)
                total += jnp.dot(x_last[:, quarter:], y_bottom[:, cols], preferred_element_type=jnp.float32)
                if not same_chunk:
                    total += jnp.dot(x_ref[...], y_late[:, cols], preferred_element_type=jnp.float32)
                out_ref[rows, :] = total

    pl.when(last == EARLY)(lambda: add(True))
    pl.when(last != EARLY)(lambda: add(False))


def late_product(where, x_far, y_far, x_late, y_late, own, far):
    return pl.pallas_call(
        late_kernel,
        in_specs=[SMEM] + [VMEM] * 8,
        out_specs=[VMEM] * 2,
        out_shape=[jax.ShapeDtypeStruct((ROWS, COLS), jnp.float32)] * 2,
        compiler_params=pltpu.CompilerParams(vmem_limit_bytes=24 * 2**20),
        cost_estimate=pl.CostEstimate(
            flops=4 * ROWS * COLS * ROWS, bytes_accessed=12 * 2**20, transcendentals=0
        ),
        name="late_product",
    )(where, *x_far, *y_far, x_late, y_late, own, far)


def finish_kernel(where_ref, pattern_ref, index_ref, xm_ref, own_ref, peer_ref, sign_ref, payload_ref, dens, out_sem):
    yl, xi, yh, z, core = (where_ref[k] for k in range(5))
    block_row = (yl * 4 + xi) * RB
    block_col = ((yh * 4 + z) * 2 + core) * QB
    same = lax.broadcasted_iota(jnp.int32, (BS, BS), 0) == lax.broadcasted_iota(jnp.int32, (BS, BS), 1)
    half_eye = jnp.where(same, 0.5, 0.0).astype(jnp.float32)

    def finish(i, carry):
        rows = pl.ds(pl.multiple_of(i * BS, BS), BS)
        for j in range(QB):
            cols = slice(j * BS, (j + 1) * BS)
            kept = jnp.where(pattern_ref[j, i] > 0, 0.5, 0.0)
            product = own_ref[rows, cols] + peer_ref[rows, cols]
            xnew = 1.5 * xm_ref[rows, cols].astype(jnp.float32) - kept * product
            sign_ref[rows, cols] = xnew.astype(jnp.bfloat16)
            on_diagonal = jnp.where(block_row + i == block_col + j, 1.0, 0.0)
            dens[i * QB + j] = (on_diagonal * half_eye - 0.5 * xnew).astype(jnp.bfloat16)
        return carry

    lax.fori_loop(0, RB, finish, 0)
    dens[BLOCKS] = jnp.zeros((BS, BS), jnp.bfloat16)

    def send(slot, carry):
        pltpu.make_async_copy(dens.at[index_ref[slot]], payload_ref.at[slot], out_sem).start()
        return carry

    lax.fori_loop(0, payload_ref.shape[0], send, 0)
    pltpu.make_async_copy(payload_ref, payload_ref, out_sem).wait()


def finish_and_payload(where, pattern, index, xm, own, peer):
    slots = index.shape[0]
    return pl.pallas_call(
        finish_kernel,
        in_specs=[SMEM] * 3 + [VMEM] * 3,
        out_specs=[VMEM, HBM],
        out_shape=[
            jax.ShapeDtypeStruct((ROWS, COLS), jnp.bfloat16),
            jax.ShapeDtypeStruct((slots, BS, BS), jnp.bfloat16),
        ],
        scratch_shapes=[pltpu.VMEM((BLOCKS + 1, BS, BS), jnp.bfloat16), pltpu.SemaphoreType.DMA],
        compiler_params=pltpu.CompilerParams(vmem_limit_bytes=24 * 2**20),
        cost_estimate=pl.CostEstimate(flops=4 * ROWS * COLS, bytes_accessed=15 * 2**20, transcendentals=0),
        name="finish_payload",
    )(where, pattern, index, xm, own, peer)


FCH = 16


def force_kernel(d_ref, h_ref, s_ref, e_ref, out_ref):
    same = lax.broadcasted_iota(jnp.int32, (BS, BS), 0) == lax.broadcasted_iota(jnp.int32, (BS, BS), 1)
    ones = jnp.ones((BS, BS), jnp.bfloat16)
    for k in range(FCH):
        spread = jnp.where(same, e_ref[k : k + 1, :].astype(jnp.float32), 0.0).astype(jnp.bfloat16)
        energy = jnp.dot(spread, ones, preferred_element_type=jnp.float32)
        term = d_ref[k].astype(jnp.float32) * (
            h_ref[k].astype(jnp.float32) - energy * s_ref[k].astype(jnp.float32)
        )
        out_ref[k : k + 1, :] = jnp.sum(term, axis=0, keepdims=True)


def force_sums(dens, force_h, force_s, energy):
    slots = dens.shape[0]
    block = pl.BlockSpec((FCH, BS, BS), lambda i: (i, 0, 0))
    line = pl.BlockSpec((FCH, BS), lambda i: (i, 0))
    partial = pl.pallas_call(
        force_kernel,
        grid=(slots // FCH,),
        in_specs=[block, block, block, line],
        out_specs=line,
        out_shape=jax.ShapeDtypeStruct((slots, BS), jnp.float32),
        cost_estimate=pl.CostEstimate(
            flops=6 * slots * BS * BS, bytes_accessed=6 * slots * BS * BS, transcendentals=0
        ),
        name="force_sums",
    )(dens, force_h, force_s, energy)
    return jnp.sum(partial, axis=1)


def exchange(payload):
    return lax.all_to_all(payload, AXES, split_axis=0, concat_axis=0, tiled=True)


def shards(x, y, pattern_x, pattern_y, pattern_product, orbital_energy, pair_dest, pair_block, force_h, force_s):
    dest, wanted = pair_dest[0, :, 0], pair_block[0]
    slots = force_h.shape[0]
    entries = dest.shape[0]
    order = jnp.arange(entries, dtype=jnp.int32)
    earlier = (dest[:, None] == dest[None, :]) & (order[None, :] < order[:, None])
    rank = jnp.sum(earlier.astype(jnp.int32), axis=1)
    slot = dest * CAP + rank
    named = slot[None, :] == jnp.arange(slots, dtype=jnp.int32)[:, None]
    index = jnp.sum(jnp.where(named, wanted[None, :] - BLOCKS, 0), axis=1) + BLOCKS
    pick_row = (index[:, None] // QB == jnp.arange(RB, dtype=jnp.int32)[None, :]).astype(jnp.bfloat16)
    send_energy = jnp.dot(
        pick_row, orbital_energy.reshape(RB, BS), preferred_element_type=jnp.float32
    ).astype(jnp.bfloat16)

    where = jnp.stack([lax.axis_index(axis) for axis in AXES]).astype(jnp.int32)
    half, quarter = ROWS // 2, ROWS // 4
    y_peer = lax.ppermute(y, "c", SWAP)
    pattern_peer = lax.ppermute(pattern_y.T, "c", SWAP)
    xm = mask_x(x, pattern_x.T)
    ym = mask_y(y, y_peer, pattern_y.T, pattern_peer, where)

    xa_below = lax.ppermute(xm, "z", UP)
    xa_above = lax.ppermute(xm, "z", DOWN)
    xb_top = lax.ppermute(xm[:half], "yh", SWAP)
    ya_below = lax.ppermute(ym, "x", UP)
    ya_above = lax.ppermute(ym, "x", DOWN)
    yb = lax.ppermute(after(ym, xb_top), "yl", SWAP)
    energy = exchange(send_energy)

    xa_far = [lax.ppermute(xa_below[:half], "z", UP), lax.ppermute(xa_above[half:], "z", DOWN)]
    ya_far = [lax.ppermute(ya_below[:quarter], "x", UP), lax.ppermute(ya_above[quarter:], "x", DOWN)]
    xb_bottom = lax.ppermute(after(xm[half:], yb, energy), "yh", SWAP)

    xb_top_z = after(xb_top, *xa_far)
    xbt_below, xbt_above = lax.ppermute(xb_top_z, "z", UP), lax.ppermute(xb_top_z, "z", DOWN)
    yb_x = after(yb, *ya_far)
    yb_below, yb_above = lax.ppermute(yb_x, "x", UP), lax.ppermute(yb_x, "x", DOWN)
    xb_bottom_z = after(xb_bottom, xbt_below, xbt_above)
    xbb_below, xbb_above = lax.ppermute(xb_bottom_z, "z", UP), lax.ppermute(xb_bottom_z, "z", DOWN)

    xb_far = [
        lax.ppermute(after(xbt_below, xbb_below), "z", UP),
        lax.ppermute(xbb_above, "z", DOWN),
    ]
    yb_far = [lax.ppermute(yb_below[:quarter], "x", UP), lax.ppermute(yb_above[quarter:], "x", DOWN)]

    x_parts = [xm, xa_below, xa_above, *xa_far, xb_top, xb_bottom, xbt_below, xbb_below, xbt_above, xbb_above]
    y_parts = [ym, ya_below, ya_above, *ya_far, yb, yb_below, yb_above]
    own, far, x_late, y_late = early_product(x_parts, y_parts, where)
    own, far = late_product(where, xb_far, yb_far, x_late, y_late, own, far)
    peer = lax.ppermute(far, "c", SWAP)
    sign_next, payload = finish_and_payload(where, pattern_product.T, index, xm, own, peer)
    received = exchange(payload)
    return sign_next, force_sums(received, force_h, force_s, energy)


def solution(mesh):
    fine = Mesh(mesh.devices.reshape(2, 4, 2, 4, 2), AXES)
    row, col = ("yl", "x"), ("yh", "z", "c")
    in_specs = (
        P(row, col),
        P(row, col),
        P(row, col),
        P(row, col),
        P(row, col),
        P(row),
        P(AXES, None, None),
        P(AXES, None),
        P(AXES, None, None),
        P(AXES, None, None),
    )
    out_specs = (P(row, col), P(AXES))
    return jax.shard_map(shards, mesh=fine, in_specs=in_specs, out_specs=out_specs, check_vma=False)
```

time: 283 us -> 267 us (0.943)
  waiting for transfers between devices: 65.9 us -> 44.7 us
  Pallas kernels: 41.2 us -> 52.6 us
  starting transfers between devices: 49.7 us -> 40.7 us
  local copies, waits for them, and re-layouts: 8.66 us -> 13.8 us
    ppermute x28 -> x24, waiting for transfers between devices: 65.9 us -> 39.1 us  [the longest x1 11 us: shards(): xb_top = lax.ppermute(xm[:half], 'yh', SWAP)]
    ppermute x28 -> x24, starting transfers between devices: 44.4 us -> 31 us  [the longest x1 3.66 us: shards(): peer = lax.ppermute(far, 'c', SWAP)]
    pallas_call x2 -> x5, Pallas kernels: 24.9 us -> 36.3 us  [the longest x1 15.3 us: finish_and_payload(): pl.pallas_call(finish_kernel, in_specs=[SMEM] * 3 + [VMEM] * 3, out_specs...]
    all_to_all x1, waiting for transfers between devices: 0.01 us -> 5.6 us  [exchange(): lax.all_to_all(payload, AXES, split_axis=0, concat_axis=0, tiled=True)]
    all_to_all x1, starting transfers between devices: 5.34 us -> 9.65 us  [exchange(): lax.all_to_all(payload, AXES, split_axis=0, concat_axis=0, tiled=True)]
    unnamed x41 -> x40, local copies, waits for them, and re-layouts: 5.42 us -> 7.8 us
  transfers between devices with their start and end apart: 29 -> 25, of which waited for: 8 -> 9; matrix products, arithmetic and copies ran while one was open for 2% -> 3% of each run, Pallas kernels for 7% -> 7%
where the time goes in v2:
time: 267 us; the launch traced here: 264 us
  blocking collectives  109 us (41%)
  Pallas kernels  52.6 us (20%)
  waiting for transfers between devices  44.7 us (17%)
  starting transfers between devices  40.7 us (15%)
  local copies, waits for them, and re-layouts  13.8 us (5%)
    all_to_all x1, blocking collectives, exchange(): lax.all_to_all(payload, AXES, split_axis=0, concat_axis=0, tiled=True)  109 us
    pallas_call x1, Pallas kernels, force_sums(): pl.pallas_call(force_kernel, grid=(slots // FCH,), in_specs=[block, block...  16.3 us
    pallas_call x1, Pallas kernels, finish_and_payload(): pl.pallas_call(finish_kernel, in_specs=[SMEM] * 3 + [VMEM] * 3, out_specs...  15.3 us
    pallas_call x1, Pallas kernels, early_product(): pl.pallas_call(early_kernel, in_specs=[HBM] * (len(X_PIECES) + len(Y_PIEC...  11.5 us
    ppermute x1, waiting for transfers between devices, shards(): xb_top = lax.ppermute(xm[:half], 'yh', SWAP)  11 us
    ppermute x1, waiting for transfers between devices, shards(): lax.ppermute(xb_bottom_z, 'z', UP)  10.4 us
    all_to_all x1, starting transfers between devices, exchange(): lax.all_to_all(payload, AXES, split_axis=0, concat_axis=0, tiled=True)  9.65 us
    unnamed x40, local copies, waits for them, and re-layouts  7.8 us
  transfers between devices with their start and end apart: 25, of which 9 were waited for; matrix products, arithmetic and copies ran while one was open for 3% of the time, Pallas kernels for 7%

profile of v2, /device:TPU:7, one launch (start us, length us, event | category | flops | bytes accessed | tf_op | source)
XLA Modules:
  0.0 264.5 jit_solution(16530201600664059794)
XLA Ops:
  1.4 3.5 %mask_x.1.refs_0_.xm_ref = bf16[1024,512]{1,0:T(8,128)(2,1)} custom-call(s32[4,8]{1,0:T(4,128)} %bitcast.19, bf16[1024,512]{1,0:T(8,128)(2,1)} %x_ref.1), custom_call_target="tpu_custom_call" | custom-call | flops 524288 | bytes 2097152 | tf_op jit(solution)/shard_map/mask_x/pallas_call | solution.py:50
  4.9 1.6 collective-permute-start.1
  6.5 2.1 collective-permute-start.3
  11.4 2.9 %mask_y.1.refs_11_ = bf16[512,1024]{1,0:T(8,128)(2,1)} custom-call(s32[5]{0:T(128)} %stack.23.where_ref.refs_19_, s32[4,8]{1,0:T(4,128)} %bitcast.20, s32[4,8]{1,0:T(4,128)} %copy-done.17, bf16[1024,512]{1,0:T(8,128)(2,1)} %y_ref.1, bf16[1024,512]{1,0:T(8,128)(2,1)} %copy-done.14), custom_call_target="tpu_custom_call" | custom-call | flops 524288 | bytes 2097152 | tf_op jit(solution)/shard_map/mask_y/pallas_call | solution.py:63
  16.6 2.9 %collective-permute-start = (bf16[512,512]{1,0:T(8,128)(2,1)S(1)}, bf16[512,512]{1,0:T(8,128)(2,1)S(1)}, u32[]{:S(2)}, u32[]{:S(2)}) collective-permute-start(bf16[512,512]{1,0:T(8,128)(2,1)S(1)} %get-tuple-element.31), channel_id=1, source_target_pairs={{0,8},{8,0},{1,9},{9,1},{2,10},{10,2},{3,11},{11,3},{4,12},{12,4},... | collective-permute-start | bytes 1572872 | tf_op jit(solution)/shard_map/ppermute | solution.py:310
  19.7 11.0 %collective-permute-done.refs_5_ = bf16[512,512]{1,0:T(8,128)(2,1)S(1)} collective-permute-done((bf16[512,512]{1,0:T(8,128)(2,1)S(1)}, bf16[512,512]{1,0:T(8,128)(2,1)S(1)}, u32[]{:S(2)}, u32[]{:S(2)}) %collective-permute-start) | collective-permute-done | bytes 524320 | tf_op jit(solution)/shard_map/ppermute | solution.py:310
  33.3 1.9 slice.34
  35.2 2.7 %collective-permute-start.4 = (bf16[512,512]{1,0:T(8,128)(2,1)}, bf16[512,512]{1,0:T(8,128)(2,1)}, u32[]{:S(2)}, u32[]{:S(2)}) collective-permute-start(bf16[512,512]{1,0:T(8,128)(2,1)} %slice.34), channel_id=1, source_target_pairs={{0,6},{2,0},{4,2},{6,4},{1,7},{3,1},{5,3},{7,5},{8,14},{10,8},{12,... | collective-permute-start | bytes 1572872 | tf_op jit(solution)/shard_map/ppermute | solution.py:316
  45.1 9.7 %all-to-all-start = ((bf16[128,2,128]{2,1,0:T(2,128)(2,1)}), bf16[128,2,128]{2,1,0:T(2,128)(2,1)S(1)}, u32[]{:S(2)}, u32[]{:S(2)}) async-start(bf16[128,2,128]{2,1,0:T(2,128)(2,1)} %bitcast.11), calls=%async_computation | async-start | bytes 131072 | tf_op jit(solution)/shard_map/all_to_all | solution.py:283
  56.2 1.8 collective-permute-start.10
  58.1 5.6 %all-to-all-done = bf16[128,2,128]{2,1,0:T(2,128)(2,1)S(1)} async-done(((bf16[128,2,128]{2,1,0:T(2,128)(2,1)}), bf16[128,2,128]{2,1,0:T(2,128)(2,1)S(1)}, u32[]{:S(2)}, u32[]{:S(2)}) %all-to-all-start) | async-done | bytes 65568 | tf_op jit(solution)/shard_map/all_to_all | solution.py:283
  66.2 4.8 %collective-permute-done.5.refs_7_ = bf16[512,512]{1,0:T(8,128)(2,1)} collective-permute-done((bf16[512,512]{1,0:T(8,128)(2,1)}, bf16[512,512]{1,0:T(8,128)(2,1)}, u32[]{:S(2)}, u32[]{:S(2)}) %collective-permute-start.5) | collective-permute-done | bytes 524320 | tf_op jit(solution)/shard_map/ppermute | solution.py:321
  71.0 7.3 %collective-permute-done.9.refs_6_ = bf16[512,512]{1,0:T(8,128)(2,1)S(1)} collective-permute-done((bf16[512,512]{1,0:T(8,128)(2,1)}, bf16[512,512]{1,0:T(8,128)(2,1)S(1)}, u32[]{:S(2)}, u32[]{:S(2)}) %collective-permute-start.9) | collective-permute-done | bytes 524320 | tf_op jit(solution)/shard_map/ppermute | solution.py:318
  78.9 2.1 collective-permute-start.13
  80.9 10.4 %collective-permute-done.11.refs_8_ = bf16[512,512]{1,0:T(8,128)(2,1)S(1)} collective-permute-done((bf16[512,512]{1,0:T(8,128)(2,1)S(1)}, bf16[512,512]{1,0:T(8,128)(2,1)S(1)}, u32[]{:S(2)}, u32[]{:S(2)}) %collective-permute-start.11) | collective-permute-done | bytes 524320 | tf_op jit(solution)/shard_map/ppermute | solution.py:325
  91.4 2.7 %collective-permute-start.14 = (bf16[512,512]{1,0:T(8,128)(2,1)S(1)}, bf16[512,512]{1,0:T(8,128)(2,1)S(1)}, u32[]{:S(2)}, u32[]{:S(2)}) collective-permute-start(bf16[512,512]{1,0:T(8,128)(2,1)S(1)} %collective-permute-done.13.refs_10_), channel_id=1, source_target_pairs={{0,6},{2,0},{4,2},{6,4},{1,7},{3,1},{5,3},{7,5},{8,14},{10,8},{12,... | collective-permute-start | bytes 1572872 | tf_op jit(solution)/shard_map/ppermute | solution.py:329
  96.8 11.5 %early_product.1 = (f32[1024,512]{1,0:T(8,128)}, f32[1024,512]{1,0:T(8,128)}, bf16[1024,512]{1,0:T(8,128)(2,1)S(1)}, bf16[512,1024]{1,0:T(8,128)(2,1)S(1)}) custom-call(bf16[1024,512]{1,0:T(8,128)(2,1)S(1)} %copy-done.2, bf16[1024,512]{1,0:T(8,128)(2,1)S(1)} %collective-permute-done.1.refs_1_, bf16[1024,512]{1,0:T(8,128)(2,1)} %collective-permute-done.3.refs_2_, ...), custom_call_target="tpu_custom_call" | custom-call | flops 7516192768 | bytes 20971520 | tf_op jit(solution)/shard_map/early_product/pallas_call | solution.py:142
  110.0 1.6 copy-done.4
  111.6 3.1 %late_product.1 = (f32[1024,512]{1,0:T(8,128)S(1)}, f32[1024,512]{1,0:T(8,128)S(1)}) custom-call(s32[5]{0:T(128)S(1)} %copy-done.10, bf16[512,512]{1,0:T(8,128)(2,1)S(1)} %collective-permute-done.12.x_top, bf16[512,512]{1,0:T(8,128)(2,1)S(1)} %collective-permute-done.14.x_bottom, bf16[256,1024]{1,0:T(8,128)(2,1)S(1)} %collective-permute-done.20.y_top, ...), custom_call_target="tpu_custom_call" | custom-call | flops 2147483648 | bytes 12582912 | tf_op jit(solution)/shard_map/late_product/pallas_call | solution.py:189
  114.6 3.7 %collective-permute-start.23 = (f32[1024,512]{1,0:T(8,128)S(1)}, f32[1024,512]{1,0:T(8,128)S(1)}, u32[]{:S(2)}, u32[]{:S(2)}) collective-permute-start(f32[1024,512]{1,0:T(8,128)S(1)} %get-tuple-element.27), channel_id=1, source_target_pairs={{0,1},{1,0},{2,3},{3,2},{4,5},{5,4},{6,7},{7,6},{8,9},{9,8},{10,11... | collective-permute-start | bytes 6291464 | tf_op jit(solution)/shard_map/ppermute | solution.py:337
  118.3 3.8 %collective-permute-done.23.peer_ref = f32[1024,512]{1,0:T(8,128)S(1)} collective-permute-done((f32[1024,512]{1,0:T(8,128)S(1)}, f32[1024,512]{1,0:T(8,128)S(1)}, u32[]{:S(2)}, u32[]{:S(2)}) %collective-permute-start.23) | collective-permute-done | bytes 2097184 | tf_op jit(solution)/shard_map/ppermute | solution.py:337
  122.1 15.3 %finish_payload.1 = (bf16[1024,512]{1,0:T(8,128)(2,1)}, bf16[256,128,128]{2,1,0:T(8,128)(2,1)S(1)}) custom-call(s32[5]{0:T(128)S(1)} %copy-done.10, s32[4,8]{1,0:T(4,128)S(1)} %bitcast.17, s32[256]{0:T(256)S(1)} %get-tuple-element.33.index_ref, bf16[1024,512]{1,0:T(8,128)(2,1)S(1)} %copy-done.2, f32[1024,512]{1,0:T(8,128)S(1)} %get-tuple-element.26.own_ref, ...), custom_call_target="tpu_custom_call" | custom-call | flops 2097152 | bytes 15728640 | tf_op jit(solution)/shard_map/finish_payload/pallas_call | solution.py:234
  137.4 109.2 %all_to_all.16.d_ref = bf16[256,128,128]{2,1,0:T(8,128)(2,1)} all-to-all(bf16[256,128,128]{2,1,0:T(8,128)(2,1)S(1)} %get-tuple-element.29), channel_id=1, replica_groups=mesh['yl'=2,'x'=4,'yh'=2,'z'=4,'c'=2] {'yl','x','yh','z','c'}, dimensions={0} | all-to-all | bytes 16777216 | tf_op jit(solution)/shard_map/all_to_all | solution.py:283
  246.6 16.3 %force_sums.1 = f32[256,128]{1,0:T(8,128)} custom-call(bf16[256,128,128]{2,1,0:T(8,128)(2,1)} %all_to_all.16.d_ref, bf16[256,128,128]{2,1,0:T(8,128)(2,1)} %h_ref.1, bf16[256,128,128]{2,1,0:T(8,128)(2,1)} %s_ref.1, bf16[256,128]{1,0:T(8,128)(2,1)} %bitcast.18), custom_call_target="tpu_custom_call" | custom-call | flops 25165824 | bytes 25165824 | tf_op jit(solution)/shard_map/force_sums/pallas_call | solution.py:268
  (88 shorter events, 26.3 us)
Async XLA Ops:
  0.7 9.1 %collective-permute-start.7 = (bf16[1024,512]{1,0:T(8,128)(2,1)}, bf16[1024,512]{1,0:T(8,128)(2,1)S(1)}, u32[]{:S(2)}, u32[]{:S(2)}) collective-permute-start(bf16[1024,512]{1,0:T(8,128)(2,1)} %y_ref.1), channel_id=1, source_target_pairs={{0,1},{1,0},{2,3},{3,2},{4,5},{5,4},{6,7},{7,6},{8,9},{9,8},{10,11... | collective-permute-start | bytes 3145736 | tf_op jit(solution)/shard_map/ppermute | solution.py:303
  4.9 27.5 %collective-permute-start.1 = (bf16[1024,512]{1,0:T(8,128)(2,1)}, bf16[1024,512]{1,0:T(8,128)(2,1)S(1)}, u32[]{:S(2)}, u32[]{:S(2)}) collective-permute-start(bf16[1024,512]{1,0:T(8,128)(2,1)} %mask_x.1.refs_0_.xm_ref), channel_id=1, source_target_pairs={{0,2},{2,4},{4,6},{6,0},{1,3},{3,5},{5,7},{7,1},{8,10},{10,12},{12... | collective-permute-start | bytes 3145736 | tf_op jit(solution)/shard_map/ppermute | solution.py:308
  6.5 26.8 %collective-permute-start.3 = (bf16[1024,512]{1,0:T(8,128)(2,1)}, bf16[1024,512]{1,0:T(8,128)(2,1)}, u32[]{:S(2)}, u32[]{:S(2)}) collective-permute-start(bf16[1024,512]{1,0:T(8,128)(2,1)} %mask_x.1.refs_0_.xm_ref), channel_id=1, source_target_pairs={{0,6},{2,0},{4,2},{6,4},{1,7},{3,1},{5,3},{7,5},{8,14},{10,8},{12,... | collective-permute-start | bytes 3145736 | tf_op jit(solution)/shard_map/ppermute | solution.py:309
  14.3 24.8 %collective-permute-start.15 = (bf16[512,1024]{1,0:T(8,128)(2,1)}, bf16[512,1024]{1,0:T(8,128)(2,1)S(1)}, u32[]{:S(2)}, u32[]{:S(2)}) collective-permute-start(bf16[512,1024]{1,0:T(8,128)(2,1)} %mask_y.1.refs_11_), channel_id=1, source_target_pairs={{0,16},{16,32},{32,48},{48,0},{1,17},{17,33},{33,49},{49,1},{2,18}... | collective-permute-start | bytes 3145736 | tf_op jit(solution)/shard_map/ppermute | solution.py:311
  14.5 27.7 %collective-permute-start.17 = (bf16[512,1024]{1,0:T(8,128)(2,1)}, bf16[512,1024]{1,0:T(8,128)(2,1)S(1)}, u32[]{:S(2)}, u32[]{:S(2)}) collective-permute-start(bf16[512,1024]{1,0:T(8,128)(2,1)} %mask_y.1.refs_11_), channel_id=1, source_target_pairs={{0,48},{16,0},{32,16},{48,32},{1,49},{17,1},{33,17},{49,33},{2,50}... | collective-permute-start | bytes 3145736 | tf_op jit(solution)/shard_map/ppermute | solution.py:312
  16.6 14.1 %collective-permute-start = (bf16[512,512]{1,0:T(8,128)(2,1)S(1)}, bf16[512,512]{1,0:T(8,128)(2,1)S(1)}, u32[]{:S(2)}, u32[]{:S(2)}) collective-permute-start(bf16[512,512]{1,0:T(8,128)(2,1)S(1)} %get-tuple-element.31), channel_id=1, source_target_pairs={{0,8},{8,0},{1,9},{9,1},{2,10},{10,2},{3,11},{11,3},{4,12},{12,4},... | collective-permute-start | bytes 1572872 | tf_op jit(solution)/shard_map/ppermute | solution.py:310
  30.7 33.0 %collective-permute-start.8 = (bf16[512,1024]{1,0:T(8,128)(2,1)S(1)}, bf16[512,1024]{1,0:T(8,128)(2,1)}, u32[]{:S(2)}, u32[]{:S(2)}) collective-permute-start(bf16[512,1024]{1,0:T(8,128)(2,1)S(1)} %copy-done.5), channel_id=1, source_target_pairs={{0,64},{64,0},{1,65},{65,1},{2,66},{66,2},{3,67},{67,3},{4,68},{68... | collective-permute-start | bytes 3145736 | tf_op jit(solution)/shard_map/ppermute | solution.py:313
  33.3 21.5 %collective-permute-start.2 = (bf16[512,512]{1,0:T(8,128)(2,1)}, bf16[512,512]{1,0:T(8,128)(2,1)}, u32[]{:S(2)}, u32[]{:S(2)}) collective-permute-start(bf16[512,512]{1,0:T(8,128)(2,1)} %slice.33), channel_id=1, source_target_pairs={{0,2},{2,4},{4,6},{6,0},{1,3},{3,5},{5,7},{7,1},{8,10},{10,12},{12... | collective-permute-start | bytes 1572872 | tf_op jit(solution)/shard_map/ppermute | solution.py:316
  35.2 19.6 %collective-permute-start.4 = (bf16[512,512]{1,0:T(8,128)(2,1)}, bf16[512,512]{1,0:T(8,128)(2,1)}, u32[]{:S(2)}, u32[]{:S(2)}) collective-permute-start(bf16[512,512]{1,0:T(8,128)(2,1)} %slice.34), channel_id=1, source_target_pairs={{0,6},{2,0},{4,2},{6,4},{1,7},{3,1},{5,3},{7,5},{8,14},{10,8},{12,... | collective-permute-start | bytes 1572872 | tf_op jit(solution)/shard_map/ppermute | solution.py:316
  40.9 23.8 %collective-permute-start.16 = (bf16[256,1024]{1,0:T(8,128)(2,1)}, bf16[256,1024]{1,0:T(8,128)(2,1)}, u32[]{:S(2)}, u32[]{:S(2)}) collective-permute-start(bf16[256,1024]{1,0:T(8,128)(2,1)} %slice.36), channel_id=1, source_target_pairs={{0,16},{16,32},{32,48},{48,0},{1,17},{17,33},{33,49},{49,1},{2,18}... | collective-permute-start | bytes 1572872 | tf_op jit(solution)/shard_map/ppermute | solution.py:317
  44.0 20.7 %collective-permute-start.18 = (bf16[256,1024]{1,0:T(8,128)(2,1)}, bf16[256,1024]{1,0:T(8,128)(2,1)}, u32[]{:S(2)}, u32[]{:S(2)}) collective-permute-start(bf16[256,1024]{1,0:T(8,128)(2,1)} %slice.37), channel_id=1, source_target_pairs={{0,48},{16,0},{32,16},{48,32},{1,49},{17,1},{33,17},{49,33},{2,50}... | collective-permute-start | bytes 1572872 | tf_op jit(solution)/shard_map/ppermute | solution.py:317
  45.1 18.5 %all-to-all-start = ((bf16[128,2,128]{2,1,0:T(2,128)(2,1)}), bf16[128,2,128]{2,1,0:T(2,128)(2,1)S(1)}, u32[]{:S(2)}, u32[]{:S(2)}) async-start(bf16[128,2,128]{2,1,0:T(2,128)(2,1)} %bitcast.11), calls=%async_computation | async-start | bytes 131072 | tf_op jit(solution)/shard_map/all_to_all | solution.py:283
  54.8 16.2 %collective-permute-start.5 = (bf16[512,512]{1,0:T(8,128)(2,1)}, bf16[512,512]{1,0:T(8,128)(2,1)}, u32[]{:S(2)}, u32[]{:S(2)}) collective-permute-start(bf16[512,512]{1,0:T(8,128)(2,1)} %copy-done.12), channel_id=1, source_target_pairs={{0,2},{2,4},{4,6},{6,0},{1,3},{3,5},{5,7},{7,1},{8,10},{10,12},{12... | collective-permute-start | bytes 1572872 | tf_op jit(solution)/shard_map/ppermute | solution.py:321
  56.2 14.8 %collective-permute-start.10 = (bf16[512,512]{1,0:T(8,128)(2,1)}, bf16[512,512]{1,0:T(8,128)(2,1)}, u32[]{:S(2)}, u32[]{:S(2)}) collective-permute-start(bf16[512,512]{1,0:T(8,128)(2,1)} %copy-done.12), channel_id=1, source_target_pairs={{0,6},{2,0},{4,2},{6,4},{1,7},{3,1},{5,3},{7,5},{8,14},{10,8},{12,... | collective-permute-start | bytes 1572872 | tf_op jit(solution)/shard_map/ppermute | solution.py:321
  63.7 14.6 %collective-permute-start.9 = (bf16[512,512]{1,0:T(8,128)(2,1)}, bf16[512,512]{1,0:T(8,128)(2,1)S(1)}, u32[]{:S(2)}, u32[]{:S(2)}) collective-permute-start(bf16[512,512]{1,0:T(8,128)(2,1)} %get-tuple-element.18), channel_id=1, source_target_pairs={{0,8},{8,0},{1,9},{9,1},{2,10},{10,2},{3,11},{11,3},{4,12},{12,4},... | collective-permute-start | bytes 1572872 | tf_op jit(solution)/shard_map/ppermute | solution.py:318
  64.7 29.3 %collective-permute-start.19 = (bf16[512,1024]{1,0:T(8,128)(2,1)}, bf16[512,1024]{1,0:T(8,128)(2,1)S(1)}, u32[]{:S(2)}, u32[]{:S(2)}) collective-permute-start(bf16[512,1024]{1,0:T(8,128)(2,1)} %collective-permute-done.8.refs_16_), channel_id=1, source_target_pairs={{0,16},{16,32},{32,48},{48,0},{1,17},{17,33},{33,49},{49,1},{2,18}... | collective-permute-start | bytes 3145736 | tf_op jit(solution)/shard_map/ppermute | solution.py:323
  65.8 29.3 %collective-permute-start.21 = (bf16[512,1024]{1,0:T(8,128)(2,1)}, bf16[512,1024]{1,0:T(8,128)(2,1)S(1)}, u32[]{:S(2)}, u32[]{:S(2)}) collective-permute-start(bf16[512,1024]{1,0:T(8,128)(2,1)} %collective-permute-done.8.refs_16_), channel_id=1, source_target_pairs={{0,48},{16,0},{32,16},{48,32},{1,49},{17,1},{33,17},{49,33},{2,50}... | collective-permute-start | bytes 3145736 | tf_op jit(solution)/shard_map/ppermute | solution.py:323
  78.3 13.1 %collective-permute-start.11 = (bf16[512,512]{1,0:T(8,128)(2,1)S(1)}, bf16[512,512]{1,0:T(8,128)(2,1)S(1)}, u32[]{:S(2)}, u32[]{:S(2)}) collective-permute-start(bf16[512,512]{1,0:T(8,128)(2,1)S(1)} %collective-permute-done.9.refs_6_), channel_id=1, source_target_pairs={{0,2},{2,4},{4,6},{6,0},{1,3},{3,5},{5,7},{7,1},{8,10},{10,12},{12... | collective-permute-start | bytes 1572872 | tf_op jit(solution)/shard_map/ppermute | solution.py:325
  78.9 12.5 %collective-permute-start.13 = (bf16[512,512]{1,0:T(8,128)(2,1)S(1)}, bf16[512,512]{1,0:T(8,128)(2,1)S(1)}, u32[]{:S(2)}, u32[]{:S(2)}) collective-permute-start(bf16[512,512]{1,0:T(8,128)(2,1)S(1)} %collective-permute-done.9.refs_6_), channel_id=1, source_target_pairs={{0,6},{2,0},{4,2},{6,4},{1,7},{3,1},{5,3},{7,5},{8,14},{10,8},{12,... | collective-permute-start | bytes 1572872 | tf_op jit(solution)/shard_map/ppermute | solution.py:325
  91.3 17.0 %collective-permute-start.12 = (bf16[512,512]{1,0:T(8,128)(2,1)}, bf16[512,512]{1,0:T(8,128)(2,1)S(1)}, u32[]{:S(2)}, u32[]{:S(2)}) collective-permute-start(bf16[512,512]{1,0:T(8,128)(2,1)} %collective-permute-done.5.refs_7_), channel_id=1, source_target_pairs={{0,2},{2,4},{4,6},{6,0},{1,3},{3,5},{5,7},{7,1},{8,10},{10,12},{12... | collective-permute-start | bytes 1572872 | tf_op jit(solution)/shard_map/ppermute | solution.py:328
  91.4 17.0 %collective-permute-start.14 = (bf16[512,512]{1,0:T(8,128)(2,1)S(1)}, bf16[512,512]{1,0:T(8,128)(2,1)S(1)}, u32[]{:S(2)}, u32[]{:S(2)}) collective-permute-start(bf16[512,512]{1,0:T(8,128)(2,1)S(1)} %collective-permute-done.13.refs_10_), channel_id=1, source_target_pairs={{0,6},{2,0},{4,2},{6,4},{1,7},{3,1},{5,3},{7,5},{8,14},{10,8},{12,... | collective-permute-start | bytes 1572872 | tf_op jit(solution)/shard_map/ppermute | solution.py:329
  94.1 14.3 %collective-permute-start.20 = (bf16[256,1024]{1,0:T(8,128)(2,1)S(1)}, bf16[256,1024]{1,0:T(8,128)(2,1)S(1)}, u32[]{:S(2)}, u32[]{:S(2)}) collective-permute-start(bf16[256,1024]{1,0:T(8,128)(2,1)S(1)} %slice.38), channel_id=1, source_target_pairs={{0,16},{16,32},{32,48},{48,0},{1,17},{17,33},{33,49},{49,1},{2,18}... | collective-permute-start | bytes 1572872 | tf_op jit(solution)/shard_map/ppermute | solution.py:331
  95.1 13.2 %collective-permute-start.22 = (bf16[256,1024]{1,0:T(8,128)(2,1)S(1)}, bf16[256,1024]{1,0:T(8,128)(2,1)S(1)}, u32[]{:S(2)}, u32[]{:S(2)}) collective-permute-start(bf16[256,1024]{1,0:T(8,128)(2,1)S(1)} %slice.39), channel_id=1, source_target_pairs={{0,48},{16,0},{32,16},{48,32},{1,49},{17,1},{33,17},{49,33},{2,50}... | collective-permute-start | bytes 1572872 | tf_op jit(solution)/shard_map/ppermute | solution.py:331
  114.6 7.4 %collective-permute-start.23 = (f32[1024,512]{1,0:T(8,128)S(1)}, f32[1024,512]{1,0:T(8,128)S(1)}, u32[]{:S(2)}, u32[]{:S(2)}) collective-permute-start(f32[1024,512]{1,0:T(8,128)S(1)} %get-tuple-element.27), channel_id=1, source_target_pairs={{0,1},{1,0},{2,3},{3,2},{4,5},{5,4},{6,7},{7,6},{8,9},{9,8},{10,11... | collective-permute-start | bytes 6291464 | tf_op jit(solution)/shard_map/ppermute | solution.py:337
  (21 other events, 319.2 us)

commit v3 on v2

--- a/solution.py
+++ b/solution.py
@@ -10,6 +10,7 @@
 CAP = 2
 RB = 8
 BLOCKS = RB * QB
+SEND = 32
 ROWS = RB * BS
 COLS = QB * BS
 RING = 4
@@ -19,25 +20,30 @@
 DOWN = [(i, (i - 1) % RING) for i in range(RING)]
 
 
-def mask_x_kernel(p_ref, x_ref, o_ref):
-    i = pl.program_id(0)
-    for r in range(2):
+def keep_block(pattern_ref, j, i):
+    return (pattern_ref[j, i] > 0).astype(jnp.float32).astype(jnp.bfloat16)
+
+
+def mask_x_kernel(p_ref, x_ref, o_ref, top_ref, bottom_ref):
+    for i in range(RB):
+        half_ref, shift = (top_ref, 0) if i < RB // 2 else (bottom_ref, RB // 2)
         for j in range(QB):
-            rows, cols = slice(r * BS, (r + 1) * BS), slice(j * BS, (j + 1) * BS)
-            keep = (p_ref[j, i * 2 + r] > 0).astype(jnp.float32).astype(jnp.bfloat16)
-            o_ref[rows, cols] = x_ref[rows, cols] * keep
+            rows, cols = slice(i * BS, (i + 1) * BS), slice(j * BS, (j + 1) * BS)
+            kept = x_ref[rows, cols] * keep_block(p_ref, j, i)
+            o_ref[rows, cols] = kept
+            half_ref[slice((i - shift) * BS, (i - shift + 1) * BS), cols] = kept
 
 
 def mask_y_kernel(where_ref, p_ref, q_ref, y_ref, z_ref, o_ref):
-    first = where_ref[4] * (RB // 2) + pl.program_id(0) * 2
-    for r in range(2):
+    first = where_ref[4] * (RB // 2)
+    for i in range(RB // 2):
+        rows = slice(i * BS, (i + 1) * BS)
+        own_rows = pl.ds(pl.multiple_of((first + i) * BS, BS), BS)
         for j in range(QB):
-            rows, cols = slice(r * BS, (r + 1) * BS), slice(j * BS, (j + 1) * BS)
+            cols = slice(j * BS, (j + 1) * BS)
             far_cols = slice(COLS + j * BS, COLS + (j + 1) * BS)
-            keep = (p_ref[j, first + r] > 0).astype(jnp.float32).astype(jnp.bfloat16)
-            o_ref[rows, cols] = y_ref[rows, cols] * keep
-            keep = (q_ref[j, first + r] > 0).astype(jnp.float32).astype(jnp.bfloat16)
-            o_ref[rows, far_cols] = z_ref[rows, cols] * keep
+            o_ref[rows, cols] = y_ref[own_rows, cols] * keep_block(p_ref, j, first + i)
+            o_ref[rows, far_cols] = z_ref[own_rows, cols] * keep_block(q_ref, j, first + i)
 
 
 SMEM = pl.BlockSpec(memory_space=pltpu.SMEM)
@@ -46,28 +52,25 @@
 
 
 def mask_x(x, pattern):
-    tile = pl.BlockSpec((2 * BS, COLS), lambda i: (i, 0))
     return pl.pallas_call(
         mask_x_kernel,
-        grid=(RB // 2,),
-        in_specs=[SMEM, tile],
-        out_specs=tile,
-        out_shape=jax.ShapeDtypeStruct((ROWS, COLS), jnp.bfloat16),
-        cost_estimate=pl.CostEstimate(flops=ROWS * COLS, bytes_accessed=4 * ROWS * COLS, transcendentals=0),
+        in_specs=[SMEM, VMEM],
+        out_specs=[VMEM] * 3,
+        out_shape=[
+            jax.ShapeDtypeStruct((ROWS, COLS), jnp.bfloat16),
+            jax.ShapeDtypeStruct((ROWS // 2, COLS), jnp.bfloat16),
+            jax.ShapeDtypeStruct((ROWS // 2, COLS), jnp.bfloat16),
+        ],
+        cost_estimate=pl.CostEstimate(flops=ROWS * COLS, bytes_accessed=6 * ROWS * COLS, transcendentals=0),
         name="mask_x",
     )(pattern, x)
 
 
 def mask_y(y, y_peer, pattern, pattern_peer, where):
-    tile = pl.BlockSpec((2 * BS, COLS), lambda i, w: (w[4] * (RB // 4) + i, 0))
     return pl.pallas_call(
         mask_y_kernel,
-        grid_spec=pltpu.PrefetchScalarGridSpec(
-            num_scalar_prefetch=1,
-            grid=(RB // 4,),
-            in_specs=[SMEM, SMEM, tile, tile],
-            out_specs=pl.BlockSpec((2 * BS, 2 * COLS), lambda i, w: (i, 0)),
-        ),
+        in_specs=[SMEM] * 3 + [VMEM] * 2,
+        out_specs=VMEM,
         out_shape=jax.ShapeDtypeStruct((ROWS // 2, 2 * COLS), jnp.bfloat16),
         cost_estimate=pl.CostEstimate(flops=ROWS * COLS, bytes_accessed=4 * ROWS * COLS, transcendentals=0),
         name="mask_y",
@@ -155,7 +158,7 @@
             pltpu.SemaphoreType.DMA((EARLY,)),
             pltpu.SemaphoreType.DMA((EARLY,)),
         ],
-        compiler_params=pltpu.CompilerParams(vmem_limit_bytes=36 * 2**20),
+        compiler_params=pltpu.CompilerParams(vmem_limit_bytes=24 * 2**20),
         cost_estimate=pl.CostEstimate(
             flops=14 * ROWS * COLS * ROWS, bytes_accessed=20 * 2**20, transcendentals=0
         ),
@@ -165,31 +168,41 @@
 
 def late_kernel(where_ref, x_top, x_bottom, y_top, y_bottom, x_late, y_late, own_ref, far_ref, own_out, far_out):
     last = y_place(where_ref, EARLY)
-    half, quarter = ROWS // 2, ROWS // 4
-
-    def add(same_chunk):
+    quarter = ROWS // 4
+
+    def add(x_far, same_chunk):
+        x_last = x_far if same_chunk else x_late
         for sum_ref, out_ref, cols in (
             (own_ref, own_out, slice(0, COLS)),
             (far_ref, far_out, slice(COLS, 2 * COLS)),
         ):
-            for rows, x_ref in ((slice(0, half), x_top), (slice(half, ROWS), x_bottom)):
-                total = sum_ref[rows, :]
-                x_last = x_ref if same_chunk else x_late.at[rows]
-                total += jnp.dot(x_last[:, :quarter], y_top[:, cols], preferred_element_type=jnp.float32)
-                total += jnp.dot(x_last[:, quarter:], y_bottom[:, cols], preferred_element_type=jnp.float32)
-                if not same_chunk:
-                    total += jnp.dot(x_ref[...], y_late[:, cols], preferred_element_type=jnp.float32)
-                out_ref[rows, :] = total
-
-    pl.when(last == EARLY)(lambda: add(True))
-    pl.when(last != EARLY)(lambda: add(False))
+            total = sum_ref[...]
+            total += jnp.dot(x_last[:, :quarter], y_top[:, cols], preferred_element_type=jnp.float32)
+            total += jnp.dot(x_last[:, quarter:], y_bottom[:, cols], preferred_element_type=jnp.float32)
+            if not same_chunk:
+                total += jnp.dot(x_far[...], y_late[:, cols], preferred_element_type=jnp.float32)
+            out_ref[...] = total
+
+    for upper, x_far in ((True, x_top), (False, x_bottom)):
+        for same_chunk in (True, False):
+            here = (pl.program_id(0) < 2) == upper
+            pl.when(here & ((last == EARLY) == same_chunk))(lambda x=x_far, t=same_chunk: add(x, t))
 
 
 def late_product(where, x_far, y_far, x_late, y_late, own, far):
+    quarter = ROWS // 4
+    top = pl.BlockSpec((quarter, COLS), lambda m: (jnp.minimum(m, 1), 0))
+    bottom = pl.BlockSpec((quarter, COLS), lambda m: (jnp.maximum(m - 2, 0), 0))
+    rows = pl.BlockSpec((quarter, COLS), lambda m: (m, 0))
+
+    def whole(height):
+        return pl.BlockSpec((height, 2 * COLS), lambda m: (0, 0))
+
     return pl.pallas_call(
         late_kernel,
-        in_specs=[SMEM] + [VMEM] * 8,
-        out_specs=[VMEM] * 2,
+        grid=(4,),
+        in_specs=[SMEM, top, bottom, whole(quarter), whole(quarter), rows, whole(2 * quarter), rows, rows],
+        out_specs=[rows] * 2,
         out_shape=[jax.ShapeDtypeStruct((ROWS, COLS), jnp.float32)] * 2,
         compiler_params=pltpu.CompilerParams(vmem_limit_bytes=24 * 2**20),
         cost_estimate=pl.CostEstimate(
@@ -199,7 +212,7 @@
     )(where, *x_far, *y_far, x_late, y_late, own, far)
 
 
-def finish_kernel(where_ref, pattern_ref, index_ref, xm_ref, own_ref, peer_ref, sign_ref, payload_ref, dens, out_sem):
+def finish_kernel(where_ref, pattern_ref, index_ref, xm_ref, own_ref, peer_ref, sign_ref, payload_ref, dens, stage, out_sem):
     yl, xi, yh, z, core = (where_ref[k] for k in range(5))
     block_row = (yl * 4 + xi) * RB
     block_col = ((yh * 4 + z) * 2 + core) * QB
@@ -221,12 +234,19 @@
     lax.fori_loop(0, RB, finish, 0)
     dens[BLOCKS] = jnp.zeros((BS, BS), jnp.bfloat16)
 
-    def send(slot, carry):
-        pltpu.make_async_copy(dens.at[index_ref[slot]], payload_ref.at[slot], out_sem).start()
+    chunks = stage.shape[0] // SEND
+
+    def copy(slot, carry):
+        stage[slot] = dens[index_ref[slot]]
         return carry
 
-    lax.fori_loop(0, payload_ref.shape[0], send, 0)
-    pltpu.make_async_copy(payload_ref, payload_ref, out_sem).wait()
+    for chunk in range(chunks):
+        lax.fori_loop(chunk * SEND, (chunk + 1) * SEND, copy, 0, unroll=8)
+        part = pl.ds(chunk * SEND, SEND)
+        pltpu.make_async_copy(stage.at[part], payload_ref.at[part], out_sem.at[chunk]).start()
+    for chunk in range(chunks):
+        part = pl.ds(chunk * SEND, SEND)
+        pltpu.make_async_copy(stage.at[part], payload_ref.at[part], out_sem.at[chunk]).wait()
 
 
 def finish_and_payload(where, pattern, index, xm, own, peer):
@@ -239,14 +259,18 @@
             jax.ShapeDtypeStruct((ROWS, COLS), jnp.bfloat16),
             jax.ShapeDtypeStruct((slots, BS, BS), jnp.bfloat16),
         ],
-        scratch_shapes=[pltpu.VMEM((BLOCKS + 1, BS, BS), jnp.bfloat16), pltpu.SemaphoreType.DMA],
+        scratch_shapes=[
+            pltpu.VMEM((BLOCKS + 1, BS, BS), jnp.bfloat16),
+            pltpu.VMEM((slots, BS, BS), jnp.bfloat16),
+            pltpu.SemaphoreType.DMA((slots // SEND,)),
+        ],
         compiler_params=pltpu.CompilerParams(vmem_limit_bytes=24 * 2**20),
         cost_estimate=pl.CostEstimate(flops=4 * ROWS * COLS, bytes_accessed=15 * 2**20, transcendentals=0),
         name="finish_payload",
     )(where, pattern, index, xm, own, peer)
 
 
-FCH = 16
+FCH = 32
 
 
 def force_kernel(d_ref, h_ref, s_ref, e_ref, out_ref):
@@ -271,6 +295,7 @@
         in_specs=[block, block, block, line],
         out_specs=line,
         out_shape=jax.ShapeDtypeStruct((slots, BS), jnp.float32),
+        compiler_params=pltpu.CompilerParams(vmem_limit_bytes=24 * 2**20),
         cost_estimate=pl.CostEstimate(
             flops=6 * slots * BS * BS, bytes_accessed=6 * slots * BS * BS, transcendentals=0
         ),
@@ -302,20 +327,24 @@
     half, quarter = ROWS // 2, ROWS // 4
     y_peer = lax.ppermute(y, "c", SWAP)
     pattern_peer = lax.ppermute(pattern_y.T, "c", SWAP)
-    xm = mask_x(x, pattern_x.T)
+    xm, xm_top, xm_bottom = mask_x(x, pattern_x.T)
     ym = mask_y(y, y_peer, pattern_y.T, pattern_peer, where)
 
-    xa_below = lax.ppermute(xm, "z", UP)
-    xa_above = lax.ppermute(xm, "z", DOWN)
-    xb_top = lax.ppermute(xm[:half], "yh", SWAP)
     ya_below = lax.ppermute(ym, "x", UP)
     ya_above = lax.ppermute(ym, "x", DOWN)
-    yb = lax.ppermute(after(ym, xb_top), "yl", SWAP)
-    energy = exchange(send_energy)
-
+    yb = lax.ppermute(ym, "yl", SWAP)
+    xm_z = after(xm, ym)
+    xa_below = lax.ppermute(xm_z, "z", UP)
+    xa_above = lax.ppermute(xm_z, "z", DOWN)
+    energy = exchange(after(send_energy, xm, ym))
+
+    xa_below, xa_above, ya_below, ya_above, yb, energy = lax.optimization_barrier(
+        (xa_below, xa_above, ya_below, ya_above, yb, energy)
+    )
     xa_far = [lax.ppermute(xa_below[:half], "z", UP), lax.ppermute(xa_above[half:], "z", DOWN)]
     ya_far = [lax.ppermute(ya_below[:quarter], "x", UP), lax.ppermute(ya_above[quarter:], "x", DOWN)]
-    xb_bottom = lax.ppermute(after(xm[half:], yb, energy), "yh", SWAP)
+    xb_top = lax.ppermute(after(xm_top, yb), "yh", SWAP)
+    xb_bottom = lax.ppermute(after(xm_bottom, xb_top), "yh", SWAP)
 
     xb_top_z = after(xb_top, *xa_far)
     xbt_below, xbt_above = lax.ppermute(xb_top_z, "z", UP), lax.ppermute(xb_top_z, "z", DOWN)

time: 267 us -> 236 us (0.88)
  blocking collectives: 109 us -> 137 us
  Pallas kernels: 52.6 us -> 29.4 us
  waiting for transfers between devices: 44.7 us -> 31.7 us
  local copies, waits for them, and re-layouts: 13.8 us -> 2.51 us
  starting transfers between devices: 40.7 us -> 30.9 us
    all_to_all x1 -> x2, blocking collectives: 109 us -> 137 us  [exchange(): lax.all_to_all(payload, AXES, split_axis=0, concat_axis=0, tiled=True)]
    ppermute x5, waiting for transfers between devices: 18.7 us -> 5.96 us  [the longest x1 3.48 us: shards(): xb_bottom = lax.ppermute(after(xm_bottom, xb_top), 'yh', SWAP)]
    pallas_call x1, Pallas kernels: 15.3 us -> 3.77 us  [finish_and_payload(): pl.pallas_call(finish_kernel, in_specs=[SMEM] * 3 + [VMEM] * 3, out_specs...]
    ppermute x1, waiting for transfers between devices: 10.4 us -> 0.01 us  [shards(): lax.ppermute(xb_bottom_z, 'z', UP)]
    pallas_call x1, Pallas kernels: 16.3 us -> 6.32 us  [force_sums(): pl.pallas_call(force_kernel, grid=(slots // FCH,), in_specs=[block, block...]
    all_to_all x1 -> x0, starting transfers between devices: 9.65 us -> none  [exchange(): lax.all_to_all(payload, AXES, split_axis=0, concat_axis=0, tiled=True)]
    ppermute x1, waiting for transfers between devices: 0.01 us -> 8.59 us  [shards(): lax.ppermute(xa_below[:half], 'z', UP)]
    unnamed x40 -> x32, local copies, waits for them, and re-layouts: 7.8 us -> 1.62 us
  transfers between devices with their start and end apart: 25 -> 24, of which waited for: 9 -> 6; matrix products, arithmetic and copies ran while one was open for 3% -> 1% of each run, Pallas kernels for 7% -> 5%
where the time goes in v3:
time: 236 us; the launch traced here: 235 us
  blocking collectives  137 us (58%)
  waiting for transfers between devices  31.7 us (13%)
  starting transfers between devices  30.9 us (13%)
  Pallas kernels  29.4 us (12%)
  local copies, waits for them, and re-layouts  2.51 us (1%)
    all_to_all x2, blocking collectives, exchange(): lax.all_to_all(payload, AXES, split_axis=0, concat_axis=0, tiled=True)  137 us
    pallas_call x1, Pallas kernels, early_product(): pl.pallas_call(early_kernel, in_specs=[HBM] * (len(X_PIECES) + len(Y_PIEC...  9.99 us
    ppermute x1, waiting for transfers between devices, shards(): lax.ppermute(xa_below[:half], 'z', UP)  8.59 us
    ppermute x1, waiting for transfers between devices, shards(): lax.ppermute(xb_top_z, 'z', UP)  7.32 us
    pallas_call x1, Pallas kernels, force_sums(): pl.pallas_call(force_kernel, grid=(slots // FCH,), in_specs=[block, block...  6.32 us
    ppermute x1, waiting for transfers between devices, shards(): lax.ppermute(yb_x, 'x', UP)  5.99 us
    ppermute x1, starting transfers between devices, shards(): peer = lax.ppermute(far, 'c', SWAP)  4.83 us
  transfers between devices with their start and end apart: 24, of which 6 were waited for; matrix products, arithmetic and copies ran while one was open for 1% of the time, Pallas kernels for 5%

profile of v3, /device:TPU:7, one launch (start us, length us, event | category | flops | bytes accessed | tf_op | source)
XLA Modules:
  0.0 234.6 jit_solution(11685787664012949753)
XLA Ops:
  3.1 2.9 %mask_x.1 = (bf16[1024,512]{1,0:T(8,128)(2,1)}, bf16[512,512]{1,0:T(8,128)(2,1)}, bf16[512,512]{1,0:T(8,128)(2,1)}) custom-call(s32[4,8]{1,0:T(4,128)} %bitcast.24, bf16[1024,512]{1,0:T(8,128)(2,1)} %x_ref.1), custom_call_target="tpu_custom_call" | custom-call | flops 524288 | bytes 3145728 | tf_op jit(solution)/shard_map/mask_x/pallas_call | solution.py:55
  7.5 2.8 %mask_y.1.refs_11_ = bf16[512,1024]{1,0:T(8,128)(2,1)} custom-call(s32[5]{0:T(128)} %stack.23.where_ref.refs_19_, s32[4,8]{1,0:T(4,128)} %bitcast.26, s32[4,8]{1,0:T(4,128)} %copy-done.7, bf16[1024,512]{1,0:T(8,128)(2,1)} %y_ref.1, bf16[1024,512]{1,0:T(8,128)(2,1)} %copy-done.6), custom_call_target="tpu_custom_call" | custom-call | flops 524288 | bytes 2097152 | tf_op jit(solution)/shard_map/mask_y/pallas_call | solution.py:70
  10.4 1.6 collective-permute-start.2
  12.0 2.2 collective-permute-start.3
  15.7 1.3 collective-permute-start.6
  17.3 27.7 %all_to_all.17 = bf16[128,2,128]{2,1,0:T(2,128)(2,1)S(1)} all-to-all(bf16[128,2,128]{2,1,0:T(2,128)(2,1)S(1)} %bitcast.23), channel_id=1, replica_groups=mesh['yl'=2,'x'=4,'yh'=2,'z'=4,'c'=2] {'yl','x','yh','z','c'}, dimensions={0} | all-to-all | bytes 131072 | tf_op jit(solution)/shard_map/all_to_all | solution.py:308
  45.8 2.1 collective-permute-start.9
  50.6 8.6 %collective-permute-done.8.refs_3_ = bf16[512,512]{1,0:T(8,128)(2,1)S(1)} collective-permute-done((bf16[512,512]{1,0:T(8,128)(2,1)S(1)}, bf16[512,512]{1,0:T(8,128)(2,1)S(1)}, u32[]{:S(2)}, u32[]{:S(2)}) %collective-permute-start.8) | collective-permute-done | bytes 524320 | tf_op jit(solution)/shard_map/ppermute | solution.py:344
  59.2 2.5 %collective-permute-done.7.refs_5_ = bf16[512,512]{1,0:T(8,128)(2,1)S(1)} collective-permute-done((bf16[512,512]{1,0:T(8,128)(2,1)S(1)}, bf16[512,512]{1,0:T(8,128)(2,1)S(1)}, u32[]{:S(2)}, u32[]{:S(2)}) %collective-permute-start.7) | collective-permute-done | bytes 524320 | tf_op jit(solution)/shard_map/ppermute | solution.py:346
  61.7 2.7 %collective-permute-start.12 = (bf16[512,512]{1,0:T(8,128)(2,1)S(1)}, bf16[512,512]{1,0:T(8,128)(2,1)S(1)}, u32[]{:S(2)}, u32[]{:S(2)}) collective-permute-start(bf16[512,512]{1,0:T(8,128)(2,1)S(1)} %collective-permute-done.7.refs_5_), channel_id=1, source_target_pairs={{0,6},{2,0},{4,2},{6,4},{1,7},{3,1},{5,3},{7,5},{8,14},{10,8},{12,... | collective-permute-start | bytes 1572872 | tf_op jit(solution)/shard_map/ppermute | solution.py:350
  64.4 1.4 collective-permute-start.19
  66.8 7.3 %collective-permute-done.10.refs_7_ = bf16[512,512]{1,0:T(8,128)(2,1)S(1)} collective-permute-done((bf16[512,512]{1,0:T(8,128)(2,1)S(1)}, bf16[512,512]{1,0:T(8,128)(2,1)S(1)}, u32[]{:S(2)}, u32[]{:S(2)}) %collective-permute-start.10) | collective-permute-done | bytes 524320 | tf_op jit(solution)/shard_map/ppermute | solution.py:350
  74.2 3.5 %collective-permute-done.11.refs_6_ = bf16[512,512]{1,0:T(8,128)(2,1)S(1)} collective-permute-done((bf16[512,512]{1,0:T(8,128)(2,1)S(1)}, bf16[512,512]{1,0:T(8,128)(2,1)S(1)}, u32[]{:S(2)}, u32[]{:S(2)}) %collective-permute-start.11) | collective-permute-done | bytes 524320 | tf_op jit(solution)/shard_map/ppermute | solution.py:347
  77.6 2.7 %collective-permute-start.15 = (bf16[512,512]{1,0:T(8,128)(2,1)S(1)}, bf16[512,512]{1,0:T(8,128)(2,1)S(1)}, u32[]{:S(2)}, u32[]{:S(2)}) collective-permute-start(bf16[512,512]{1,0:T(8,128)(2,1)S(1)} %collective-permute-done.11.refs_6_), channel_id=1, source_target_pairs={{0,6},{2,0},{4,2},{6,4},{1,7},{3,1},{5,3},{7,5},{8,14},{10,8},{12,... | collective-permute-start | bytes 1572872 | tf_op jit(solution)/shard_map/ppermute | solution.py:354
  80.3 6.0 %collective-permute-done.19.refs_17_ = bf16[512,1024]{1,0:T(8,128)(2,1)S(1)} collective-permute-done((bf16[512,1024]{1,0:T(8,128)(2,1)S(1)}, bf16[512,1024]{1,0:T(8,128)(2,1)S(1)}, u32[]{:S(2)}, u32[]{:S(2)}) %collective-permute-start.19) | collective-permute-done | bytes 1048608 | tf_op jit(solution)/shard_map/ppermute | solution.py:352
  86.3 2.6 %collective-permute-start.20 = (bf16[256,1024]{1,0:T(8,128)(2,1)S(1)}, bf16[256,1024]{1,0:T(8,128)(2,1)S(1)}, u32[]{:S(2)}, u32[]{:S(2)}) collective-permute-start(bf16[256,1024]{1,0:T(8,128)(2,1)S(1)} %slice.24), channel_id=1, source_target_pairs={{0,16},{16,32},{32,48},{48,0},{1,17},{17,33},{33,49},{49,1},{2,18}... | collective-permute-start | bytes 1572872 | tf_op jit(solution)/shard_map/ppermute | solution.py:360
  89.2 2.7 %collective-permute-start.16 = (bf16[512,512]{1,0:T(8,128)(2,1)S(1)}, bf16[512,512]{1,0:T(8,128)(2,1)S(1)}, u32[]{:S(2)}, u32[]{:S(2)}) collective-permute-start(bf16[512,512]{1,0:T(8,128)(2,1)S(1)} %collective-permute-done.15.refs_10_), channel_id=1, source_target_pairs={{0,6},{2,0},{4,2},{6,4},{1,7},{3,1},{5,3},{7,5},{8,14},{10,8},{12,... | collective-permute-start | bytes 1572872 | tf_op jit(solution)/shard_map/ppermute | solution.py:358
  91.9 10.0 %early_product.1 = (f32[1024,512]{1,0:T(8,128)S(1)}, f32[1024,512]{1,0:T(8,128)S(1)}, bf16[1024,512]{1,0:T(8,128)(2,1)S(1)}, bf16[512,1024]{1,0:T(8,128)(2,1)S(1)}) custom-call(bf16[1024,512]{1,0:T(8,128)(2,1)S(1)} %copy-done.2, bf16[1024,512]{1,0:T(8,128)(2,1)S(1)} %collective-permute-done.2.refs_1_, bf16[1024,512]{1,0:T(8,128)(2,1)S(1)} %collective-permute-done.3.refs_2_, ...), custom_call_target="tpu_custom_call" | custom-call | flops 7516192768 | bytes 20971520 | tf_op jit(solution)/shard_map/early_product/pallas_call | solution.py:145
  101.9 3.6 %late_product.1 = (f32[1024,512]{1,0:T(8,128)S(1)}, f32[1024,512]{1,0:T(8,128)S(1)}) custom-call(s32[5]{0:T(128)S(1)} %copy-done.4, bf16[512,512]{1,0:T(8,128)(2,1)S(1)} %collective-permute-done.14.x_top, bf16[512,512]{1,0:T(8,128)(2,1)S(1)} %collective-permute-done.16.x_bottom, bf16[256,1024]{1,0:T(8,128)(2,1)S(1)} %collective-permute-done.20.y_top, ...), custom_call_target="tpu_custom_call" | custom-call | flops 2147483648 | bytes 12582912 | tf_op jit(solution)/shard_map/late_product/pallas_call | solution.py:201
  105.6 4.8 %collective-permute-start.23 = (f32[1024,512]{1,0:T(8,128)S(1)}, f32[1024,512]{1,0:T(8,128)S(1)}, u32[]{:S(2)}, u32[]{:S(2)}) collective-permute-start(f32[1024,512]{1,0:T(8,128)S(1)} %get-tuple-element.48), channel_id=1, source_target_pairs={{0,1},{1,0},{2,3},{3,2},{4,5},{5,4},{6,7},{7,6},{8,9},{9,8},{10,11... | collective-permute-start | bytes 6291464 | tf_op jit(solution)/shard_map/ppermute | solution.py:366
  110.4 3.8 %collective-permute-done.23.peer_ref = f32[1024,512]{1,0:T(8,128)S(1)} collective-permute-done((f32[1024,512]{1,0:T(8,128)S(1)}, f32[1024,512]{1,0:T(8,128)S(1)}, u32[]{:S(2)}, u32[]{:S(2)}) %collective-permute-start.23) | collective-permute-done | bytes 2097184 | tf_op jit(solution)/shard_map/ppermute | solution.py:366
  114.2 3.8 %finish_payload.1 = (bf16[1024,512]{1,0:T(8,128)(2,1)}, bf16[256,128,128]{2,1,0:T(8,128)(2,1)S(1)}) custom-call(s32[5]{0:T(128)S(1)} %copy-done.4, s32[4,8]{1,0:T(4,128)S(1)} %bitcast.22, s32[256]{0:T(256)S(1)} %get-tuple-element.53.index_ref, bf16[1024,512]{1,0:T(8,128)(2,1)S(1)} %copy-done.2, f32[1024,512]{1,0:T(8,128)S(1)} %get-tuple-element.47.own_ref, ...), custom_call_target="tpu_custom_call" | custom-call | flops 2097152 | bytes 15728640 | tf_op jit(solution)/shard_map/finish_payload/pallas_call | solution.py:254
  118.0 109.6 %all_to_all.18.d_ref = bf16[256,128,128]{2,1,0:T(8,128)(2,1)S(1)} all-to-all(bf16[256,128,128]{2,1,0:T(8,128)(2,1)S(1)} %get-tuple-element.50), channel_id=1, replica_groups=mesh['yl'=2,'x'=4,'yh'=2,'z'=4,'c'=2] {'yl','x','yh','z','c'}, dimensions={0} | all-to-all | bytes 16777216 | tf_op jit(solution)/shard_map/all_to_all | solution.py:308
  227.6 6.3 %force_sums.1 = f32[256,128]{1,0:T(8,128)S(1)} custom-call(bf16[256,128,128]{2,1,0:T(8,128)(2,1)S(1)} %all_to_all.18.d_ref, bf16[256,128,128]{2,1,0:T(8,128)(2,1)S(1)} %bitcast.18, bf16[256,128,128]{2,1,0:T(8,128)(2,1)S(1)} %bitcast.20, bf16[256,128]{1,0:T(8,128)(2,1)S(1)} %bitcast.21), custom_call_target="tpu_custom_call" | custom-call | flops 25165824 | bytes 25165824 | tf_op jit(solution)/shard_map/force_sums/pallas_call | solution.py:292
  (80 shorter events, 11.3 us)
Async XLA Ops:
  0.6 5.3 %collective-permute-start.1 = (bf16[1024,512]{1,0:T(8,128)(2,1)}, bf16[1024,512]{1,0:T(8,128)(2,1)S(1)}, u32[]{:S(2)}, u32[]{:S(2)}) collective-permute-start(bf16[1024,512]{1,0:T(8,128)(2,1)} %y_ref.1), channel_id=1, source_target_pairs={{0,1},{1,0},{2,3},{3,2},{4,5},{5,4},{6,7},{7,6},{8,9},{9,8},{10,11... | collective-permute-start | bytes 3145736 | tf_op jit(solution)/shard_map/ppermute | solution.py:328
  1.4 4.6 %collective-permute-start = (s32[4,8]{1,0:T(4,128)}, s32[4,8]{1,0:T(4,128)S(1)}, u32[]{:S(2)}, u32[]{:S(2)}) collective-permute-start(s32[4,8]{1,0:T(4,128)} %bitcast.25), channel_id=1, source_target_pairs={{0,1},{1,0},{2,3},{3,2},{4,5},{5,4},{6,7},{7,6},{8,9},{9,8},{10,11... | collective-permute-start | bytes 392 | tf_op jit(solution)/shard_map/ppermute | solution.py:329
  10.4 34.7 %collective-permute-start.2 = (bf16[1024,512]{1,0:T(8,128)(2,1)S(1)}, bf16[1024,512]{1,0:T(8,128)(2,1)S(1)}, u32[]{:S(2)}, u32[]{:S(2)}) collective-permute-start(bf16[1024,512]{1,0:T(8,128)(2,1)S(1)} %copy-done.2), channel_id=1, source_target_pairs={{0,2},{2,4},{4,6},{6,0},{1,3},{3,5},{5,7},{7,1},{8,10},{10,12},{12... | collective-permute-start | bytes 3145736 | tf_op jit(solution)/shard_map/ppermute | solution.py:337
  12.0 33.0 %collective-permute-start.3 = (bf16[1024,512]{1,0:T(8,128)(2,1)S(1)}, bf16[1024,512]{1,0:T(8,128)(2,1)S(1)}, u32[]{:S(2)}, u32[]{:S(2)}) collective-permute-start(bf16[1024,512]{1,0:T(8,128)(2,1)S(1)} %copy-done.2), channel_id=1, source_target_pairs={{0,6},{2,0},{4,2},{6,4},{1,7},{3,1},{5,3},{7,5},{8,14},{10,8},{12,... | collective-permute-start | bytes 3145736 | tf_op jit(solution)/shard_map/ppermute | solution.py:338
  14.2 30.8 %collective-permute-start.4 = (bf16[512,1024]{1,0:T(8,128)(2,1)}, bf16[512,1024]{1,0:T(8,128)(2,1)S(1)}, u32[]{:S(2)}, u32[]{:S(2)}) collective-permute-start(bf16[512,1024]{1,0:T(8,128)(2,1)} %mask_y.1.refs_11_), channel_id=1, source_target_pairs={{0,16},{16,32},{32,48},{48,0},{1,17},{17,33},{33,49},{49,1},{2,18}... | collective-permute-start | bytes 3145736 | tf_op jit(solution)/shard_map/ppermute | solution.py:333
  14.4 30.6 %collective-permute-start.5 = (bf16[512,1024]{1,0:T(8,128)(2,1)}, bf16[512,1024]{1,0:T(8,128)(2,1)S(1)}, u32[]{:S(2)}, u32[]{:S(2)}) collective-permute-start(bf16[512,1024]{1,0:T(8,128)(2,1)} %mask_y.1.refs_11_), channel_id=1, source_target_pairs={{0,48},{16,0},{32,16},{48,32},{1,49},{17,1},{33,17},{49,33},{2,50}... | collective-permute-start | bytes 3145736 | tf_op jit(solution)/shard_map/ppermute | solution.py:334
  15.7 29.4 %collective-permute-start.6 = (bf16[512,1024]{1,0:T(8,128)(2,1)}, bf16[512,1024]{1,0:T(8,128)(2,1)S(1)}, u32[]{:S(2)}, u32[]{:S(2)}) collective-permute-start(bf16[512,1024]{1,0:T(8,128)(2,1)} %mask_y.1.refs_11_), channel_id=1, source_target_pairs={{0,64},{64,0},{1,65},{65,1},{2,66},{66,2},{3,67},{67,3},{4,68},{68... | collective-permute-start | bytes 3145736 | tf_op jit(solution)/shard_map/ppermute | solution.py:335
  45.1 14.1 %collective-permute-start.8 = (bf16[512,512]{1,0:T(8,128)(2,1)S(1)}, bf16[512,512]{1,0:T(8,128)(2,1)S(1)}, u32[]{:S(2)}, u32[]{:S(2)}) collective-permute-start(bf16[512,512]{1,0:T(8,128)(2,1)S(1)} %slice.18), channel_id=1, source_target_pairs={{0,2},{2,4},{4,6},{6,0},{1,3},{3,5},{5,7},{7,1},{8,10},{10,12},{12... | collective-permute-start | bytes 1572872 | tf_op jit(solution)/shard_map/ppermute | solution.py:344
  45.8 13.4 %collective-permute-start.9 = (bf16[512,512]{1,0:T(8,128)(2,1)S(1)}, bf16[512,512]{1,0:T(8,128)(2,1)S(1)}, u32[]{:S(2)}, u32[]{:S(2)}) collective-permute-start(bf16[512,512]{1,0:T(8,128)(2,1)S(1)} %slice.19), channel_id=1, source_target_pairs={{0,6},{2,0},{4,2},{6,4},{1,7},{3,1},{5,3},{7,5},{8,14},{10,8},{12,... | collective-permute-start | bytes 1572872 | tf_op jit(solution)/shard_map/ppermute | solution.py:344
  48.0 13.7 %collective-permute-start.7 = (bf16[512,512]{1,0:T(8,128)(2,1)S(1)}, bf16[512,512]{1,0:T(8,128)(2,1)S(1)}, u32[]{:S(2)}, u32[]{:S(2)}) collective-permute-start(bf16[512,512]{1,0:T(8,128)(2,1)S(1)} %copy-done.9), channel_id=1, source_target_pairs={{0,8},{8,0},{1,9},{9,1},{2,10},{10,2},{3,11},{11,3},{4,12},{12,4},... | collective-permute-start | bytes 1572872 | tf_op jit(solution)/shard_map/ppermute | solution.py:346
  49.0 15.4 %collective-permute-start.17 = (bf16[256,1024]{1,0:T(8,128)(2,1)S(1)}, bf16[256,1024]{1,0:T(8,128)(2,1)S(1)}, u32[]{:S(2)}, u32[]{:S(2)}) collective-permute-start(bf16[256,1024]{1,0:T(8,128)(2,1)S(1)} %slice.20), channel_id=1, source_target_pairs={{0,16},{16,32},{32,48},{48,0},{1,17},{17,33},{33,49},{49,1},{2,18}... | collective-permute-start | bytes 1572872 | tf_op jit(solution)/shard_map/ppermute | solution.py:345
  50.1 14.2 %collective-permute-start.18 = (bf16[256,1024]{1,0:T(8,128)(2,1)S(1)}, bf16[256,1024]{1,0:T(8,128)(2,1)S(1)}, u32[]{:S(2)}, u32[]{:S(2)}) collective-permute-start(bf16[256,1024]{1,0:T(8,128)(2,1)S(1)} %slice.21), channel_id=1, source_target_pairs={{0,48},{16,0},{32,16},{48,32},{1,49},{17,1},{33,17},{49,33},{2,50}... | collective-permute-start | bytes 1572872 | tf_op jit(solution)/shard_map/ppermute | solution.py:345
  61.7 12.5 %collective-permute-start.10 = (bf16[512,512]{1,0:T(8,128)(2,1)S(1)}, bf16[512,512]{1,0:T(8,128)(2,1)S(1)}, u32[]{:S(2)}, u32[]{:S(2)}) collective-permute-start(bf16[512,512]{1,0:T(8,128)(2,1)S(1)} %collective-permute-done.7.refs_5_), channel_id=1, source_target_pairs={{0,2},{2,4},{4,6},{6,0},{1,3},{3,5},{5,7},{7,1},{8,10},{10,12},{12... | collective-permute-start | bytes 1572872 | tf_op jit(solution)/shard_map/ppermute | solution.py:350
  61.7 12.5 %collective-permute-start.12 = (bf16[512,512]{1,0:T(8,128)(2,1)S(1)}, bf16[512,512]{1,0:T(8,128)(2,1)S(1)}, u32[]{:S(2)}, u32[]{:S(2)}) collective-permute-start(bf16[512,512]{1,0:T(8,128)(2,1)S(1)} %collective-permute-done.7.refs_5_), channel_id=1, source_target_pairs={{0,6},{2,0},{4,2},{6,4},{1,7},{3,1},{5,3},{7,5},{8,14},{10,8},{12,... | collective-permute-start | bytes 1572872 | tf_op jit(solution)/shard_map/ppermute | solution.py:350
  64.4 21.9 %collective-permute-start.19 = (bf16[512,1024]{1,0:T(8,128)(2,1)S(1)}, bf16[512,1024]{1,0:T(8,128)(2,1)S(1)}, u32[]{:S(2)}, u32[]{:S(2)}) collective-permute-start(bf16[512,1024]{1,0:T(8,128)(2,1)S(1)} %collective-permute-done.6.refs_16_), channel_id=1, source_target_pairs={{0,16},{16,32},{32,48},{48,0},{1,17},{17,33},{33,49},{49,1},{2,18}... | collective-permute-start | bytes 3145736 | tf_op jit(solution)/shard_map/ppermute | solution.py:352
  65.7 11.9 %collective-permute-start.11 = (bf16[512,512]{1,0:T(8,128)(2,1)S(1)}, bf16[512,512]{1,0:T(8,128)(2,1)S(1)}, u32[]{:S(2)}, u32[]{:S(2)}) collective-permute-start(bf16[512,512]{1,0:T(8,128)(2,1)S(1)} %copy-done.8), channel_id=1, source_target_pairs={{0,8},{8,0},{1,9},{9,1},{2,10},{10,2},{3,11},{11,3},{4,12},{12,4},... | collective-permute-start | bytes 1572872 | tf_op jit(solution)/shard_map/ppermute | solution.py:347
  66.4 22.6 %collective-permute-start.21 = (bf16[512,1024]{1,0:T(8,128)(2,1)S(1)}, bf16[512,1024]{1,0:T(8,128)(2,1)S(1)}, u32[]{:S(2)}, u32[]{:S(2)}) collective-permute-start(bf16[512,1024]{1,0:T(8,128)(2,1)S(1)} %collective-permute-done.6.refs_16_), channel_id=1, source_target_pairs={{0,48},{16,0},{32,16},{48,32},{1,49},{17,1},{33,17},{49,33},{2,50}... | collective-permute-start | bytes 3145736 | tf_op jit(solution)/shard_map/ppermute | solution.py:352
  77.6 11.5 %collective-permute-start.13 = (bf16[512,512]{1,0:T(8,128)(2,1)S(1)}, bf16[512,512]{1,0:T(8,128)(2,1)S(1)}, u32[]{:S(2)}, u32[]{:S(2)}) collective-permute-start(bf16[512,512]{1,0:T(8,128)(2,1)S(1)} %collective-permute-done.11.refs_6_), channel_id=1, source_target_pairs={{0,2},{2,4},{4,6},{6,0},{1,3},{3,5},{5,7},{7,1},{8,10},{10,12},{12... | collective-permute-start | bytes 1572872 | tf_op jit(solution)/shard_map/ppermute | solution.py:354
  77.6 11.5 %collective-permute-start.15 = (bf16[512,512]{1,0:T(8,128)(2,1)S(1)}, bf16[512,512]{1,0:T(8,128)(2,1)S(1)}, u32[]{:S(2)}, u32[]{:S(2)}) collective-permute-start(bf16[512,512]{1,0:T(8,128)(2,1)S(1)} %collective-permute-done.11.refs_6_), channel_id=1, source_target_pairs={{0,6},{2,0},{4,2},{6,4},{1,7},{3,1},{5,3},{7,5},{8,14},{10,8},{12,... | collective-permute-start | bytes 1572872 | tf_op jit(solution)/shard_map/ppermute | solution.py:354
  86.3 15.5 %collective-permute-start.20 = (bf16[256,1024]{1,0:T(8,128)(2,1)S(1)}, bf16[256,1024]{1,0:T(8,128)(2,1)S(1)}, u32[]{:S(2)}, u32[]{:S(2)}) collective-permute-start(bf16[256,1024]{1,0:T(8,128)(2,1)S(1)} %slice.24), channel_id=1, source_target_pairs={{0,16},{16,32},{32,48},{48,0},{1,17},{17,33},{33,49},{49,1},{2,18}... | collective-permute-start | bytes 1572872 | tf_op jit(solution)/shard_map/ppermute | solution.py:360
  89.0 12.9 %collective-permute-start.22 = (bf16[256,1024]{1,0:T(8,128)(2,1)S(1)}, bf16[256,1024]{1,0:T(8,128)(2,1)S(1)}, u32[]{:S(2)}, u32[]{:S(2)}) collective-permute-start(bf16[256,1024]{1,0:T(8,128)(2,1)S(1)} %slice.25), channel_id=1, source_target_pairs={{0,48},{16,0},{32,16},{48,32},{1,49},{17,1},{33,17},{49,33},{2,50}... | collective-permute-start | bytes 1572872 | tf_op jit(solution)/shard_map/ppermute | solution.py:360
  89.1 12.8 %collective-permute-start.14 = (bf16[512,512]{1,0:T(8,128)(2,1)S(1)}, bf16[512,512]{1,0:T(8,128)(2,1)S(1)}, u32[]{:S(2)}, u32[]{:S(2)}) collective-permute-start(bf16[512,512]{1,0:T(8,128)(2,1)S(1)} %collective-permute-done.10.refs_7_), channel_id=1, source_target_pairs={{0,2},{2,4},{4,6},{6,0},{1,3},{3,5},{5,7},{7,1},{8,10},{10,12},{12... | collective-permute-start | bytes 1572872 | tf_op jit(solution)/shard_map/ppermute | solution.py:357
  89.2 12.7 %collective-permute-start.16 = (bf16[512,512]{1,0:T(8,128)(2,1)S(1)}, bf16[512,512]{1,0:T(8,128)(2,1)S(1)}, u32[]{:S(2)}, u32[]{:S(2)}) collective-permute-start(bf16[512,512]{1,0:T(8,128)(2,1)S(1)} %collective-permute-done.15.refs_10_), channel_id=1, source_target_pairs={{0,6},{2,0},{4,2},{6,4},{1,7},{3,1},{5,3},{7,5},{8,14},{10,8},{12,... | collective-permute-start | bytes 1572872 | tf_op jit(solution)/shard_map/ppermute | solution.py:358
  105.6 8.6 %collective-permute-start.23 = (f32[1024,512]{1,0:T(8,128)S(1)}, f32[1024,512]{1,0:T(8,128)S(1)}, u32[]{:S(2)}, u32[]{:S(2)}) collective-permute-start(f32[1024,512]{1,0:T(8,128)S(1)} %get-tuple-element.48), channel_id=1, source_target_pairs={{0,1},{1,0},{2,3},{3,2},{4,5},{5,4},{6,7},{7,6},{8,9},{9,8},{10,11... | collective-permute-start | bytes 6291464 | tf_op jit(solution)/shard_map/ppermute | solution.py:366
  (16 other events, 678.3 us)

commit v4 on v3

--- a/solution.py
+++ b/solution.py
@@ -10,7 +10,8 @@
 CAP = 2
 RB = 8
 BLOCKS = RB * QB
-SEND = 32
+SEND = 16
+TAIL = 8
 ROWS = RB * BS
 COLS = QB * BS
 RING = 4
@@ -24,26 +25,32 @@
     return (pattern_ref[j, i] > 0).astype(jnp.float32).astype(jnp.bfloat16)
 
 
-def mask_x_kernel(p_ref, x_ref, o_ref, top_ref, bottom_ref):
+def mask_kernel(
+    where_ref, px_ref, py_ref, pz_ref, x_hbm, y_hbm, z_ref, xo_ref, top_ref, bottom_ref, yo_ref, x_ref, y_ref, sem
+):
+    first = where_ref[4] * (RB // 2)
+    own_rows = pl.ds(pl.multiple_of(first * BS, ROWS // 2), ROWS // 2)
+    x_copy = pltpu.make_async_copy(x_hbm, x_ref, sem.at[0])
+    y_copy = pltpu.make_async_copy(y_hbm.at[own_rows], y_ref, sem.at[1])
+    x_copy.start()
+    y_copy.start()
+    x_copy.wait()
     for i in range(RB):
         half_ref, shift = (top_ref, 0) if i < RB // 2 else (bottom_ref, RB // 2)
         for j in range(QB):
             rows, cols = slice(i * BS, (i + 1) * BS), slice(j * BS, (j + 1) * BS)
-            kept = x_ref[rows, cols] * keep_block(p_ref, j, i)
-            o_ref[rows, cols] = kept
+            kept = x_ref[rows, cols] * keep_block(px_ref, j, i)
+            xo_ref[rows, cols] = kept
             half_ref[slice((i - shift) * BS, (i - shift + 1) * BS), cols] = kept
-
-
-def mask_y_kernel(where_ref, p_ref, q_ref, y_ref, z_ref, o_ref):
-    first = where_ref[4] * (RB // 2)
+    y_copy.wait()
     for i in range(RB // 2):
         rows = slice(i * BS, (i + 1) * BS)
-        own_rows = pl.ds(pl.multiple_of((first + i) * BS, BS), BS)
+        peer_rows = pl.ds(pl.multiple_of((first + i) * BS, BS), BS)
         for j in range(QB):
             cols = slice(j * BS, (j + 1) * BS)
             far_cols = slice(COLS + j * BS, COLS + (j + 1) * BS)
-            o_ref[rows, cols] = y_ref[own_rows, cols] * keep_block(p_ref, j, first + i)
-            o_ref[rows, far_cols] = z_ref[own_rows, cols] * keep_block(q_ref, j, first + i)
+            yo_ref[rows, cols] = y_ref[rows, cols] * keep_block(py_ref, j, first + i)
+            yo_ref[rows, far_cols] = z_ref[peer_rows, cols] * keep_block(pz_ref, j, first + i)
 
 
 SMEM = pl.BlockSpec(memory_space=pltpu.SMEM)
@@ -51,30 +58,27 @@
 HBM = pl.BlockSpec(memory_space=pltpu.HBM)
 
 
-def mask_x(x, pattern):
+def masked_tiles(where, pattern_x, pattern_y, pattern_peer, x, y, y_peer):
+    half = jax.ShapeDtypeStruct((ROWS // 2, COLS), jnp.bfloat16)
     return pl.pallas_call(
-        mask_x_kernel,
-        in_specs=[SMEM, VMEM],
-        out_specs=[VMEM] * 3,
+        mask_kernel,
+        in_specs=[SMEM] * 4 + [HBM] * 2 + [VMEM],
+        out_specs=[VMEM] * 4,
         out_shape=[
             jax.ShapeDtypeStruct((ROWS, COLS), jnp.bfloat16),
-            jax.ShapeDtypeStruct((ROWS // 2, COLS), jnp.bfloat16),
-            jax.ShapeDtypeStruct((ROWS // 2, COLS), jnp.bfloat16),
-        ],
-        cost_estimate=pl.CostEstimate(flops=ROWS * COLS, bytes_accessed=6 * ROWS * COLS, transcendentals=0),
-        name="mask_x",
-    )(pattern, x)
-
-
-def mask_y(y, y_peer, pattern, pattern_peer, where):
-    return pl.pallas_call(
-        mask_y_kernel,
-        in_specs=[SMEM] * 3 + [VMEM] * 2,
-        out_specs=VMEM,
-        out_shape=jax.ShapeDtypeStruct((ROWS // 2, 2 * COLS), jnp.bfloat16),
-        cost_estimate=pl.CostEstimate(flops=ROWS * COLS, bytes_accessed=4 * ROWS * COLS, transcendentals=0),
-        name="mask_y",
-    )(where, pattern, pattern_peer, y, y_peer)
+            half,
+            half,
+            jax.ShapeDtypeStruct((ROWS // 2, 2 * COLS), jnp.bfloat16),
+        ],
+        scratch_shapes=[
+            pltpu.VMEM((ROWS, COLS), jnp.bfloat16),
+            pltpu.VMEM((ROWS // 2, COLS), jnp.bfloat16),
+            pltpu.SemaphoreType.DMA((2,)),
+        ],
+        compiler_params=pltpu.CompilerParams(vmem_limit_bytes=12 * 2**20),
+        cost_estimate=pl.CostEstimate(flops=2 * ROWS * COLS, bytes_accessed=12 * ROWS * COLS, transcendentals=0),
+        name="mask_tiles",
+    )(where, pattern_x, pattern_y, pattern_peer, x, y, y_peer)
 
 
 def after(value, *others):
@@ -212,7 +216,7 @@
     )(where, *x_far, *y_far, x_late, y_late, own, far)
 
 
-def finish_kernel(where_ref, pattern_ref, index_ref, xm_ref, own_ref, peer_ref, sign_ref, payload_ref, dens, stage, out_sem):
+def finish_kernel(where_ref, pattern_ref, index_ref, energy_ref, xm_ref, own_ref, peer_ref, sign_ref, payload_ref, dens, stage, out_sem):
     yl, xi, yh, z, core = (where_ref[k] for k in range(5))
     block_row = (yl * 4 + xi) * RB
     block_col = ((yh * 4 + z) * 2 + core) * QB
@@ -235,13 +239,19 @@
     dens[BLOCKS] = jnp.zeros((BS, BS), jnp.bfloat16)
 
     chunks = stage.shape[0] // SEND
-
-    def copy(slot, carry):
-        stage[slot] = dens[index_ref[slot]]
+    line = lax.broadcasted_iota(jnp.int32, (TAIL, BS), 0)
+
+    def copy(owner, carry):
+        energies = jnp.zeros((TAIL, BS), jnp.float32)
+        for k in range(CAP):
+            block = index_ref[owner * CAP + k]
+            stage[owner, k * BS : (k + 1) * BS, :] = dens[block]
+            energies = jnp.where(line == k, energy_ref[block // QB], energies)
+        stage[owner, CAP * BS :, :] = energies.astype(jnp.bfloat16)
         return carry
 
     for chunk in range(chunks):
-        lax.fori_loop(chunk * SEND, (chunk + 1) * SEND, copy, 0, unroll=8)
+        lax.fori_loop(chunk * SEND, (chunk + 1) * SEND, copy, 0, unroll=4)
         part = pl.ds(chunk * SEND, SEND)
         pltpu.make_async_copy(stage.at[part], payload_ref.at[part], out_sem.at[chunk]).start()
     for chunk in range(chunks):
@@ -249,58 +259,61 @@
         pltpu.make_async_copy(stage.at[part], payload_ref.at[part], out_sem.at[chunk]).wait()
 
 
-def finish_and_payload(where, pattern, index, xm, own, peer):
-    slots = index.shape[0]
+def finish_and_payload(where, pattern, index, energy, xm, own, peer):
+    owners = index.shape[0] // CAP
+    packet = (owners, CAP * BS + TAIL, BS)
     return pl.pallas_call(
         finish_kernel,
-        in_specs=[SMEM] * 3 + [VMEM] * 3,
+        in_specs=[SMEM] * 3 + [VMEM] * 4,
         out_specs=[VMEM, HBM],
         out_shape=[
             jax.ShapeDtypeStruct((ROWS, COLS), jnp.bfloat16),
-            jax.ShapeDtypeStruct((slots, BS, BS), jnp.bfloat16),
+            jax.ShapeDtypeStruct(packet, jnp.bfloat16),
         ],
         scratch_shapes=[
             pltpu.VMEM((BLOCKS + 1, BS, BS), jnp.bfloat16),
-            pltpu.VMEM((slots, BS, BS), jnp.bfloat16),
-            pltpu.SemaphoreType.DMA((slots // SEND,)),
-        ],
-        compiler_params=pltpu.CompilerParams(vmem_limit_bytes=24 * 2**20),
+            pltpu.VMEM(packet, jnp.bfloat16),
+            pltpu.SemaphoreType.DMA((owners // SEND,)),
+        ],
+        compiler_params=pltpu.CompilerParams(vmem_limit_bytes=18 * 2**20),
         cost_estimate=pl.CostEstimate(flops=4 * ROWS * COLS, bytes_accessed=15 * 2**20, transcendentals=0),
         name="finish_payload",
-    )(where, pattern, index, xm, own, peer)
-
-
-FCH = 32
-
-
-def force_kernel(d_ref, h_ref, s_ref, e_ref, out_ref):
+    )(where, pattern, index, energy, xm, own, peer)
+
+
+FCH = 16
+
+
+def force_kernel(d_ref, h_ref, s_ref, out_ref):
     same = lax.broadcasted_iota(jnp.int32, (BS, BS), 0) == lax.broadcasted_iota(jnp.int32, (BS, BS), 1)
     ones = jnp.ones((BS, BS), jnp.bfloat16)
-    for k in range(FCH):
-        spread = jnp.where(same, e_ref[k : k + 1, :].astype(jnp.float32), 0.0).astype(jnp.bfloat16)
-        energy = jnp.dot(spread, ones, preferred_element_type=jnp.float32)
-        term = d_ref[k].astype(jnp.float32) * (
-            h_ref[k].astype(jnp.float32) - energy * s_ref[k].astype(jnp.float32)
-        )
-        out_ref[k : k + 1, :] = jnp.sum(term, axis=0, keepdims=True)
-
-
-def force_sums(dens, force_h, force_s, energy):
-    slots = dens.shape[0]
-    block = pl.BlockSpec((FCH, BS, BS), lambda i: (i, 0, 0))
-    line = pl.BlockSpec((FCH, BS), lambda i: (i, 0))
+    for source in range(FCH):
+        energies = d_ref[source, CAP * BS :, :].astype(jnp.float32)
+        for k in range(CAP):
+            slot = source * CAP + k
+            spread = jnp.where(same, energies[k : k + 1, :], 0.0).astype(jnp.bfloat16)
+            energy = jnp.dot(spread, ones, preferred_element_type=jnp.float32)
+            term = d_ref[source, k * BS : (k + 1) * BS, :].astype(jnp.float32) * (
+                h_ref[slot].astype(jnp.float32) - energy * s_ref[slot].astype(jnp.float32)
+            )
+            out_ref[slot : slot + 1, :] = jnp.sum(term, axis=0, keepdims=True)
+
+
+def force_sums(packets, force_h, force_s):
+    slots = force_h.shape[0]
+    block = pl.BlockSpec((FCH * CAP, BS, BS), lambda i: (i, 0, 0))
     partial = pl.pallas_call(
         force_kernel,
-        grid=(slots // FCH,),
-        in_specs=[block, block, block, line],
-        out_specs=line,
+        grid=(slots // (FCH * CAP),),
+        in_specs=[pl.BlockSpec((FCH, CAP * BS + TAIL, BS), lambda i: (i, 0, 0)), block, block],
+        out_specs=pl.BlockSpec((FCH * CAP, BS), lambda i: (i, 0)),
         out_shape=jax.ShapeDtypeStruct((slots, BS), jnp.float32),
-        compiler_params=pltpu.CompilerParams(vmem_limit_bytes=24 * 2**20),
+        compiler_params=pltpu.CompilerParams(vmem_limit_bytes=12 * 2**20),
         cost_estimate=pl.CostEstimate(
             flops=6 * slots * BS * BS, bytes_accessed=6 * slots * BS * BS, transcendentals=0
         ),
         name="force_sums",
-    )(dens, force_h, force_s, energy)
+    )(packets, force_h, force_s)
     return jnp.sum(partial, axis=1)
 
 
@@ -318,33 +331,26 @@
     slot = dest * CAP + rank
     named = slot[None, :] == jnp.arange(slots, dtype=jnp.int32)[:, None]
     index = jnp.sum(jnp.where(named, wanted[None, :] - BLOCKS, 0), axis=1) + BLOCKS
-    pick_row = (index[:, None] // QB == jnp.arange(RB, dtype=jnp.int32)[None, :]).astype(jnp.bfloat16)
-    send_energy = jnp.dot(
-        pick_row, orbital_energy.reshape(RB, BS), preferred_element_type=jnp.float32
-    ).astype(jnp.bfloat16)
+    energy = jnp.pad(orbital_energy.astype(jnp.float32).reshape(RB, 1, BS), ((0, 1), (0, 0), (0, 0)))
 
     where = jnp.stack([lax.axis_index(axis) for axis in AXES]).astype(jnp.int32)
     half, quarter = ROWS // 2, ROWS // 4
     y_peer = lax.ppermute(y, "c", SWAP)
     pattern_peer = lax.ppermute(pattern_y.T, "c", SWAP)
-    xm, xm_top, xm_bottom = mask_x(x, pattern_x.T)
-    ym = mask_y(y, y_peer, pattern_y.T, pattern_peer, where)
-
+    xm, xm_top, xm_bottom, ym = masked_tiles(
+        where, pattern_x.T, pattern_y.T, pattern_peer, x, y, y_peer
+    )
+
+    xb_top = lax.ppermute(xm_top, "yh", SWAP)
+    xa_below = lax.ppermute(xm, "z", UP)
+    xa_above = lax.ppermute(xm, "z", DOWN)
     ya_below = lax.ppermute(ym, "x", UP)
     ya_above = lax.ppermute(ym, "x", DOWN)
-    yb = lax.ppermute(ym, "yl", SWAP)
-    xm_z = after(xm, ym)
-    xa_below = lax.ppermute(xm_z, "z", UP)
-    xa_above = lax.ppermute(xm_z, "z", DOWN)
-    energy = exchange(after(send_energy, xm, ym))
-
-    xa_below, xa_above, ya_below, ya_above, yb, energy = lax.optimization_barrier(
-        (xa_below, xa_above, ya_below, ya_above, yb, energy)
-    )
+    yb = lax.ppermute(after(ym, xb_top), "yl", SWAP)
+    xb_bottom = lax.ppermute(after(xm_bottom, yb), "yh", SWAP)
+
     xa_far = [lax.ppermute(xa_below[:half], "z", UP), lax.ppermute(xa_above[half:], "z", DOWN)]
     ya_far = [lax.ppermute(ya_below[:quarter], "x", UP), lax.ppermute(ya_above[quarter:], "x", DOWN)]
-    xb_top = lax.ppermute(after(xm_top, yb), "yh", SWAP)
-    xb_bottom = lax.ppermute(after(xm_bottom, xb_top), "yh", SWAP)
 
     xb_top_z = after(xb_top, *xa_far)
     xbt_below, xbt_above = lax.ppermute(xb_top_z, "z", UP), lax.ppermute(xb_top_z, "z", DOWN)
@@ -364,9 +370,9 @@
     own, far, x_late, y_late = early_product(x_parts, y_parts, where)
     own, far = late_product(where, xb_far, yb_far, x_late, y_late, own, far)
     peer = lax.ppermute(far, "c", SWAP)
-    sign_next, payload = finish_and_payload(where, pattern_product.T, index, xm, own, peer)
+    sign_next, payload = finish_and_payload(where, pattern_product.T, index, energy, xm, own, peer)
     received = exchange(payload)
-    return sign_next, force_sums(received, force_h, force_s, energy)
+    return sign_next, force_sums(received, force_h, force_s)
 
 
 def solution(mesh):

time: 236 us -> 230 us (0.975)
  blocking collectives: 137 us -> 114 us
  waiting for transfers between devices: 31.7 us -> 50.4 us
  Pallas kernels: 29.4 us -> 26.1 us
    all_to_all x2 -> x1, blocking collectives: 137 us -> 114 us  [exchange(): lax.all_to_all(payload, AXES, split_axis=0, concat_axis=0, tiled=True)]
    ppermute x5, waiting for transfers between devices: 5.96 us -> 19.9 us  [the longest x1 9.94 us: shards(): xb_top = lax.ppermute(xm_top, 'yh', SWAP)]
    ppermute x1, waiting for transfers between devices: 0.01 us -> 8.69 us  [shards(): lax.ppermute(xb_bottom_z, 'z', UP)]
    ppermute x1, waiting for transfers between devices: 5.99 us -> 1.01 us  [shards(): lax.ppermute(yb_x, 'x', UP)]
    ppermute x5, starting transfers between devices: 6.72 us -> 11 us  [the longest x1 2.91 us: shards(): xb_top = lax.ppermute(xm_top, 'yh', SWAP)]
    pallas_call x4 -> x3, Pallas kernels: 15.8 us -> 12.5 us  [the longest x1 6.01 us: force_sums(): pl.pallas_call(force_kernel, grid=(slots // (FCH * CAP),), in_specs=[pl.B...]
  transfers between devices with their start and end apart: 24 -> 24, of which waited for: 6 -> 10; matrix products, arithmetic and copies ran while one was open for 1% -> 0% of each run, Pallas kernels for 5% -> 4%
where the time goes in v4:
time: 230 us
  blocking collectives  114 us (50%)
  waiting for transfers between devices  50.4 us (22%)
  starting transfers between devices  33.2 us (14%)
  Pallas kernels  26.1 us (11%)
  local copies, waits for them, and re-layouts  4.16 us (2%)
    all_to_all x1, blocking collectives, exchange(): lax.all_to_all(payload, AXES, split_axis=0, concat_axis=0, tiled=True)  114 us
    pallas_call x1, Pallas kernels, early_product(): pl.pallas_call(early_kernel, in_specs=[HBM] * (len(X_PIECES) + len(Y_PIEC...  10.1 us
    ppermute x1, waiting for transfers between devices, shards(): xb_top = lax.ppermute(xm_top, 'yh', SWAP)  9.94 us
    ppermute x1, waiting for transfers between devices, shards(): lax.ppermute(xa_below[:half], 'z', UP)  8.69 us
    ppermute x1, waiting for transfers between devices, shards(): lax.ppermute(xb_bottom_z, 'z', UP)  8.69 us
    ppermute x1, waiting for transfers between devices, shards(): xa_below = lax.ppermute(xm, 'z', UP)  7.53 us
    pallas_call x1, Pallas kernels, force_sums(): pl.pallas_call(force_kernel, grid=(slots // (FCH * CAP),), in_specs=[pl.B...  6.01 us
    ppermute x1, waiting for transfers between devices, shards(): lax.ppermute(xb_top_z, 'z', UP)  5.77 us
  transfers between devices with their start and end apart: 24, of which 10 were waited for; matrix products, arithmetic and copies ran while one was open for 0% of the time, Pallas kernels for 4%

profile of v4, /device:TPU:7, one launch (start us, length us, event | category | flops | bytes accessed | tf_op | source)
XLA Modules:
  0.0 229.8 jit_solution(6336394125516965904)
XLA Ops:
  1.6 2.3 %collective-permute-done.pz_ref = s32[4,8]{1,0:T(4,128)S(1)} collective-permute-done((s32[4,8]{1,0:T(4,128)}, s32[4,8]{1,0:T(4,128)S(1)}, u32[]{:S(2)}, u32[]{:S(2)}) %collective-permute-start) | collective-permute-done | bytes 160 | tf_op jit(solution)/shard_map/ppermute | solution.py:339
  9.1 1.7 collective-permute-start.3
  10.8 2.2 collective-permute-start.5
  13.0 2.9 %collective-permute-start.2 = (bf16[512,512]{1,0:T(8,128)(2,1)S(1)}, bf16[512,512]{1,0:T(8,128)(2,1)S(1)}, u32[]{:S(2)}, u32[]{:S(2)}) collective-permute-start(bf16[512,512]{1,0:T(8,128)(2,1)S(1)} %get-tuple-element.21), channel_id=1, source_target_pairs={{0,8},{8,0},{1,9},{9,1},{2,10},{10,2},{3,11},{11,3},{4,12},{12,4},... | collective-permute-start | bytes 1572872 | tf_op jit(solution)/shard_map/ppermute | solution.py:344
  17.4 9.9 %collective-permute-done.2.refs_5_ = bf16[512,512]{1,0:T(8,128)(2,1)S(1)} collective-permute-done((bf16[512,512]{1,0:T(8,128)(2,1)S(1)}, bf16[512,512]{1,0:T(8,128)(2,1)S(1)}, u32[]{:S(2)}, u32[]{:S(2)}) %collective-permute-start.2) | collective-permute-done | bytes 524320 | tf_op jit(solution)/shard_map/ppermute | solution.py:344
  28.6 7.5 %collective-permute-done.3.refs_1_ = bf16[1024,512]{1,0:T(8,128)(2,1)S(1)} collective-permute-done((bf16[1024,512]{1,0:T(8,128)(2,1)S(1)}, bf16[1024,512]{1,0:T(8,128)(2,1)S(1)}, u32[]{:S(2)}, u32[]{:S(2)}) %collective-permute-start.3) | collective-permute-done | bytes 1048608 | tf_op jit(solution)/shard_map/ppermute | solution.py:345
  36.3 2.7 %collective-permute-start.6 = (bf16[512,512]{1,0:T(8,128)(2,1)S(1)}, bf16[512,512]{1,0:T(8,128)(2,1)S(1)}, u32[]{:S(2)}, u32[]{:S(2)}) collective-permute-start(bf16[512,512]{1,0:T(8,128)(2,1)S(1)} %slice.25), channel_id=1, source_target_pairs={{0,6},{2,0},{4,2},{6,4},{1,7},{3,1},{5,3},{7,5},{8,14},{10,8},{12,... | collective-permute-start | bytes 1572872 | tf_op jit(solution)/shard_map/ppermute | solution.py:352
  39.7 1.5 collective-permute-start.16
  41.3 8.7 %collective-permute-done.4.refs_3_ = bf16[512,512]{1,0:T(8,128)(2,1)S(1)} collective-permute-done((bf16[512,512]{1,0:T(8,128)(2,1)S(1)}, bf16[512,512]{1,0:T(8,128)(2,1)S(1)}, u32[]{:S(2)}, u32[]{:S(2)}) %collective-permute-start.4) | collective-permute-done | bytes 524320 | tf_op jit(solution)/shard_map/ppermute | solution.py:352
  50.0 2.7 %collective-permute-start.10 = (bf16[512,512]{1,0:T(8,128)(2,1)S(1)}, bf16[512,512]{1,0:T(8,128)(2,1)S(1)}, u32[]{:S(2)}, u32[]{:S(2)}) collective-permute-start(bf16[512,512]{1,0:T(8,128)(2,1)S(1)} %collective-permute-done.2.refs_5_), channel_id=1, source_target_pairs={{0,6},{2,0},{4,2},{6,4},{1,7},{3,1},{5,3},{7,5},{8,14},{10,8},{12,... | collective-permute-start | bytes 1572872 | tf_op jit(solution)/shard_map/ppermute | solution.py:356
  52.7 2.9 %collective-permute-start.9 = (bf16[512,512]{1,0:T(8,128)(2,1)S(1)}, bf16[512,512]{1,0:T(8,128)(2,1)S(1)}, u32[]{:S(2)}, u32[]{:S(2)}) collective-permute-start(bf16[512,512]{1,0:T(8,128)(2,1)S(1)} %get-tuple-element.26), channel_id=1, source_target_pairs={{0,8},{8,0},{1,9},{9,1},{2,10},{10,2},{3,11},{11,3},{4,12},{12,4},... | collective-permute-start | bytes 1572872 | tf_op jit(solution)/shard_map/ppermute | solution.py:350
  57.1 5.8 %collective-permute-done.7.refs_7_ = bf16[512,512]{1,0:T(8,128)(2,1)S(1)} collective-permute-done((bf16[512,512]{1,0:T(8,128)(2,1)S(1)}, bf16[512,512]{1,0:T(8,128)(2,1)S(1)}, u32[]{:S(2)}, u32[]{:S(2)}) %collective-permute-start.7) | collective-permute-done | bytes 524320 | tf_op jit(solution)/shard_map/ppermute | solution.py:356
  62.9 2.4 %collective-permute-done.9.refs_6_ = bf16[512,512]{1,0:T(8,128)(2,1)S(1)} collective-permute-done((bf16[512,512]{1,0:T(8,128)(2,1)S(1)}, bf16[512,512]{1,0:T(8,128)(2,1)S(1)}, u32[]{:S(2)}, u32[]{:S(2)}) %collective-permute-start.9) | collective-permute-done | bytes 524320 | tf_op jit(solution)/shard_map/ppermute | solution.py:350
  65.3 2.7 %collective-permute-start.13 = (bf16[512,512]{1,0:T(8,128)(2,1)S(1)}, bf16[512,512]{1,0:T(8,128)(2,1)S(1)}, u32[]{:S(2)}, u32[]{:S(2)}) collective-permute-start(bf16[512,512]{1,0:T(8,128)(2,1)S(1)} %collective-permute-done.9.refs_6_), channel_id=1, source_target_pairs={{0,6},{2,0},{4,2},{6,4},{1,7},{3,1},{5,3},{7,5},{8,14},{10,8},{12,... | collective-permute-start | bytes 1572872 | tf_op jit(solution)/shard_map/ppermute | solution.py:360
  68.0 8.7 %collective-permute-done.11.refs_8_ = bf16[512,512]{1,0:T(8,128)(2,1)S(1)} collective-permute-done((bf16[512,512]{1,0:T(8,128)(2,1)S(1)}, bf16[512,512]{1,0:T(8,128)(2,1)S(1)}, u32[]{:S(2)}, u32[]{:S(2)}) %collective-permute-start.11) | collective-permute-done | bytes 524320 | tf_op jit(solution)/shard_map/ppermute | solution.py:360
  77.7 1.5 collective-permute-start.20
  79.4 1.7 collective-permute-start.14
  81.0 10.1 %early_product.1 = (f32[1024,512]{1,0:T(8,128)S(1)}, f32[1024,512]{1,0:T(8,128)S(1)}, bf16[1024,512]{1,0:T(8,128)(2,1)S(1)}, bf16[512,1024]{1,0:T(8,128)(2,1)S(1)}) custom-call(bf16[1024,512]{1,0:T(8,128)(2,1)S(1)} %get-tuple-element.20.refs_0_.xm_ref, bf16[1024,512]{1,0:T(8,128)(2,1)S(1)} %collective-permute-done.3.refs_1_, ...), custom_call_target="tpu_custom_call" | custom-call | flops 7516192768 | bytes 20971520 | tf_op jit(solution)/shard_map/early_product/pallas_call | solution.py:149
  91.2 3.6 %late_product.1 = (f32[1024,512]{1,0:T(8,128)S(1)}, f32[1024,512]{1,0:T(8,128)S(1)}) custom-call(s32[5]{0:T(128)S(1)} %stack.23.where_ref.refs_19_, bf16[512,512]{1,0:T(8,128)(2,1)S(1)} %collective-permute-done.12.x_top, bf16[512,512]{1,0:T(8,128)(2,1)S(1)} %collective-permute-done.14.x_bottom, bf16[256,1024]{1,0:T(8,128)(2,1)S(1)} %collective-permute-done.20.y_top, ...), custom_call_target="tpu_custom_call" | custom-call | flops 2147483648 | bytes 12582912 | tf_op jit(solution)/shard_map/late_product/pallas_call | solution.py:205
  94.8 5.4 %collective-permute-start.23 = (f32[1024,512]{1,0:T(8,128)S(1)}, f32[1024,512]{1,0:T(8,128)S(1)}, u32[]{:S(2)}, u32[]{:S(2)}) collective-permute-start(f32[1024,512]{1,0:T(8,128)S(1)} %get-tuple-element.35), channel_id=1, source_target_pairs={{0,1},{1,0},{2,3},{3,2},{4,5},{5,4},{6,7},{7,6},{8,9},{9,8},{10,11... | collective-permute-start | bytes 6291464 | tf_op jit(solution)/shard_map/ppermute | solution.py:372
  100.6 3.4 %collective-permute-done.23.peer_ref = f32[1024,512]{1,0:T(8,128)S(1)} collective-permute-done((f32[1024,512]{1,0:T(8,128)S(1)}, f32[1024,512]{1,0:T(8,128)S(1)}, u32[]{:S(2)}, u32[]{:S(2)}) %collective-permute-start.23) | collective-permute-done | bytes 2097184 | tf_op jit(solution)/shard_map/ppermute | solution.py:372
  104.0 5.1 %finish_payload.1 = (bf16[1024,512]{1,0:T(8,128)(2,1)}, bf16[128,264,128]{2,1,0:T(8,128)(2,1)S(1)}) custom-call(s32[5]{0:T(128)S(1)} %stack.23.where_ref.refs_19_, s32[4,8]{1,0:T(4,128)S(1)} %bitcast.17, s32[256]{0:T(256)S(1)} %broadcast_add_fusion.index_ref, f32[9,1,128]{2,1,0:T(1,128)S(1)} %pad_convert_fusion.energy_ref, ...), custom_call_target="tpu_custom_call" | custom-call | flops 2097152 | bytes 15728640 | tf_op jit(solution)/shard_map/finish_payload/pallas_call | solution.py:265
  109.1 114.0 %all_to_all.5.d_ref = bf16[128,264,128]{2,1,0:T(8,128)(2,1)S(1)} all-to-all(bf16[128,264,128]{2,1,0:T(8,128)(2,1)S(1)} %get-tuple-element.37), channel_id=1, replica_groups=mesh['yl'=2,'x'=4,'yh'=2,'z'=4,'c'=2] {'yl','x','yh','z','c'}, dimensions={0} | all-to-all | bytes 17301504 | tf_op jit(solution)/shard_map/all_to_all | solution.py:321
  223.1 6.0 %force_sums.1 = f32[256,128]{1,0:T(8,128)S(1)} custom-call(bf16[128,264,128]{2,1,0:T(8,128)(2,1)S(1)} %all_to_all.5.d_ref, bf16[256,128,128]{2,1,0:T(8,128)(2,1)S(1)} %bitcast.14, bf16[256,128,128]{2,1,0:T(8,128)(2,1)S(1)} %bitcast.16), custom_call_target="tpu_custom_call" | custom-call | flops 25165824 | bytes 25165824 | tf_op jit(solution)/shard_map/force_sums/pallas_call | solution.py:305
  (71 shorter events, 13.6 us)
Async XLA Ops:
  0.6 3.3 %collective-permute-start.1 = (bf16[1024,512]{1,0:T(8,128)(2,1)}, bf16[1024,512]{1,0:T(8,128)(2,1)S(1)}, u32[]{:S(2)}, u32[]{:S(2)}) collective-permute-start(bf16[1024,512]{1,0:T(8,128)(2,1)} %y_hbm.1), channel_id=1, source_target_pairs={{0,1},{1,0},{2,3},{3,2},{4,5},{5,4},{6,7},{7,6},{8,9},{9,8},{10,11... | collective-permute-start | bytes 3145736 | tf_op jit(solution)/shard_map/ppermute | solution.py:338
  1.4 2.5 %collective-permute-start = (s32[4,8]{1,0:T(4,128)}, s32[4,8]{1,0:T(4,128)S(1)}, u32[]{:S(2)}, u32[]{:S(2)}) collective-permute-start(s32[4,8]{1,0:T(4,128)} %bitcast.19), channel_id=1, source_target_pairs={{0,1},{1,0},{2,3},{3,2},{4,5},{5,4},{6,7},{7,6},{8,9},{9,8},{10,11... | collective-permute-start | bytes 392 | tf_op jit(solution)/shard_map/ppermute | solution.py:339
  9.1 27.1 %collective-permute-start.3 = (bf16[1024,512]{1,0:T(8,128)(2,1)S(1)}, bf16[1024,512]{1,0:T(8,128)(2,1)S(1)}, u32[]{:S(2)}, u32[]{:S(2)}) collective-permute-start(bf16[1024,512]{1,0:T(8,128)(2,1)S(1)} %get-tuple-element.20.refs_0_.xm_ref), channel_id=1, source_target_pairs={{0,2},{2,4},{4,6},{6,0},{1,3},{3,5},{5,7},{7,1},{8,10},{10,12},{12... | collective-permute-start | bytes 3145736 | tf_op jit(solution)/shard_map/ppermute | solution.py:345
  10.8 25.5 %collective-permute-start.5 = (bf16[1024,512]{1,0:T(8,128)(2,1)S(1)}, bf16[1024,512]{1,0:T(8,128)(2,1)S(1)}, u32[]{:S(2)}, u32[]{:S(2)}) collective-permute-start(bf16[1024,512]{1,0:T(8,128)(2,1)S(1)} %get-tuple-element.20.refs_0_.xm_ref), channel_id=1, source_target_pairs={{0,6},{2,0},{4,2},{6,4},{1,7},{3,1},{5,3},{7,5},{8,14},{10,8},{12,... | collective-permute-start | bytes 3145736 | tf_op jit(solution)/shard_map/ppermute | solution.py:346
  13.0 14.3 %collective-permute-start.2 = (bf16[512,512]{1,0:T(8,128)(2,1)S(1)}, bf16[512,512]{1,0:T(8,128)(2,1)S(1)}, u32[]{:S(2)}, u32[]{:S(2)}) collective-permute-start(bf16[512,512]{1,0:T(8,128)(2,1)S(1)} %get-tuple-element.21), channel_id=1, source_target_pairs={{0,8},{8,0},{1,9},{9,1},{2,10},{10,2},{3,11},{11,3},{4,12},{12,4},... | collective-permute-start | bytes 1572872 | tf_op jit(solution)/shard_map/ppermute | solution.py:344
  15.9 23.7 %collective-permute-start.15 = (bf16[512,1024]{1,0:T(8,128)(2,1)S(1)}, bf16[512,1024]{1,0:T(8,128)(2,1)S(1)}, u32[]{:S(2)}, u32[]{:S(2)}) collective-permute-start(bf16[512,1024]{1,0:T(8,128)(2,1)S(1)} %get-tuple-element.25.refs_11_), channel_id=1, source_target_pairs={{0,16},{16,32},{32,48},{48,0},{1,17},{17,33},{33,49},{49,1},{2,18}... | collective-permute-start | bytes 3145736 | tf_op jit(solution)/shard_map/ppermute | solution.py:347
  16.1 25.1 %collective-permute-start.17 = (bf16[512,1024]{1,0:T(8,128)(2,1)S(1)}, bf16[512,1024]{1,0:T(8,128)(2,1)S(1)}, u32[]{:S(2)}, u32[]{:S(2)}) collective-permute-start(bf16[512,1024]{1,0:T(8,128)(2,1)S(1)} %get-tuple-element.25.refs_11_), channel_id=1, source_target_pairs={{0,48},{16,0},{32,16},{48,32},{1,49},{17,1},{33,17},{49,33},{2,50}... | collective-permute-start | bytes 3145736 | tf_op jit(solution)/shard_map/ppermute | solution.py:348
  27.3 25.4 %collective-permute-start.8 = (bf16[512,1024]{1,0:T(8,128)(2,1)S(1)}, bf16[512,1024]{1,0:T(8,128)(2,1)S(1)}, u32[]{:S(2)}, u32[]{:S(2)}) collective-permute-start(bf16[512,1024]{1,0:T(8,128)(2,1)S(1)} %get-tuple-element.25.refs_11_), channel_id=1, source_target_pairs={{0,64},{64,0},{1,65},{65,1},{2,66},{66,2},{3,67},{67,3},{4,68},{68... | collective-permute-start | bytes 3145736 | tf_op jit(solution)/shard_map/ppermute | solution.py:349
  36.2 13.8 %collective-permute-start.4 = (bf16[512,512]{1,0:T(8,128)(2,1)S(1)}, bf16[512,512]{1,0:T(8,128)(2,1)S(1)}, u32[]{:S(2)}, u32[]{:S(2)}) collective-permute-start(bf16[512,512]{1,0:T(8,128)(2,1)S(1)} %slice.24), channel_id=1, source_target_pairs={{0,2},{2,4},{4,6},{6,0},{1,3},{3,5},{5,7},{7,1},{8,10},{10,12},{12... | collective-permute-start | bytes 1572872 | tf_op jit(solution)/shard_map/ppermute | solution.py:352
  36.3 13.7 %collective-permute-start.6 = (bf16[512,512]{1,0:T(8,128)(2,1)S(1)}, bf16[512,512]{1,0:T(8,128)(2,1)S(1)}, u32[]{:S(2)}, u32[]{:S(2)}) collective-permute-start(bf16[512,512]{1,0:T(8,128)(2,1)S(1)} %slice.25), channel_id=1, source_target_pairs={{0,6},{2,0},{4,2},{6,4},{1,7},{3,1},{5,3},{7,5},{8,14},{10,8},{12,... | collective-permute-start | bytes 1572872 | tf_op jit(solution)/shard_map/ppermute | solution.py:352
  39.7 15.9 %collective-permute-start.16 = (bf16[256,1024]{1,0:T(8,128)(2,1)S(1)}, bf16[256,1024]{1,0:T(8,128)(2,1)S(1)}, u32[]{:S(2)}, u32[]{:S(2)}) collective-permute-start(bf16[256,1024]{1,0:T(8,128)(2,1)S(1)} %slice.26), channel_id=1, source_target_pairs={{0,16},{16,32},{32,48},{48,0},{1,17},{17,33},{33,49},{49,1},{2,18}... | collective-permute-start | bytes 1572872 | tf_op jit(solution)/shard_map/ppermute | solution.py:353
  41.2 14.4 %collective-permute-start.18 = (bf16[256,1024]{1,0:T(8,128)(2,1)S(1)}, bf16[256,1024]{1,0:T(8,128)(2,1)S(1)}, u32[]{:S(2)}, u32[]{:S(2)}) collective-permute-start(bf16[256,1024]{1,0:T(8,128)(2,1)S(1)} %slice.27), channel_id=1, source_target_pairs={{0,48},{16,0},{32,16},{48,32},{1,49},{17,1},{33,17},{49,33},{2,50}... | collective-permute-start | bytes 1572872 | tf_op jit(solution)/shard_map/ppermute | solution.py:353
  50.0 12.8 %collective-permute-start.7 = (bf16[512,512]{1,0:T(8,128)(2,1)S(1)}, bf16[512,512]{1,0:T(8,128)(2,1)S(1)}, u32[]{:S(2)}, u32[]{:S(2)}) collective-permute-start(bf16[512,512]{1,0:T(8,128)(2,1)S(1)} %collective-permute-done.2.refs_5_), channel_id=1, source_target_pairs={{0,2},{2,4},{4,6},{6,0},{1,3},{3,5},{5,7},{7,1},{8,10},{10,12},{12... | collective-permute-start | bytes 1572872 | tf_op jit(solution)/shard_map/ppermute | solution.py:356
  50.0 12.8 %collective-permute-start.10 = (bf16[512,512]{1,0:T(8,128)(2,1)S(1)}, bf16[512,512]{1,0:T(8,128)(2,1)S(1)}, u32[]{:S(2)}, u32[]{:S(2)}) collective-permute-start(bf16[512,512]{1,0:T(8,128)(2,1)S(1)} %collective-permute-done.2.refs_5_), channel_id=1, source_target_pairs={{0,6},{2,0},{4,2},{6,4},{1,7},{3,1},{5,3},{7,5},{8,14},{10,8},{12,... | collective-permute-start | bytes 1572872 | tf_op jit(solution)/shard_map/ppermute | solution.py:356
  52.7 12.6 %collective-permute-start.9 = (bf16[512,512]{1,0:T(8,128)(2,1)S(1)}, bf16[512,512]{1,0:T(8,128)(2,1)S(1)}, u32[]{:S(2)}, u32[]{:S(2)}) collective-permute-start(bf16[512,512]{1,0:T(8,128)(2,1)S(1)} %get-tuple-element.26), channel_id=1, source_target_pairs={{0,8},{8,0},{1,9},{9,1},{2,10},{10,2},{3,11},{11,3},{4,12},{12,4},... | collective-permute-start | bytes 1572872 | tf_op jit(solution)/shard_map/ppermute | solution.py:350
  55.6 22.0 %collective-permute-start.19 = (bf16[512,1024]{1,0:T(8,128)(2,1)S(1)}, bf16[512,1024]{1,0:T(8,128)(2,1)S(1)}, u32[]{:S(2)}, u32[]{:S(2)}) collective-permute-start(bf16[512,1024]{1,0:T(8,128)(2,1)S(1)} %collective-permute-done.8.refs_16_), channel_id=1, source_target_pairs={{0,16},{16,32},{32,48},{48,0},{1,17},{17,33},{33,49},{49,1},{2,18}... | collective-permute-start | bytes 3145736 | tf_op jit(solution)/shard_map/ppermute | solution.py:358
  55.8 23.4 %collective-permute-start.21 = (bf16[512,1024]{1,0:T(8,128)(2,1)S(1)}, bf16[512,1024]{1,0:T(8,128)(2,1)S(1)}, u32[]{:S(2)}, u32[]{:S(2)}) collective-permute-start(bf16[512,1024]{1,0:T(8,128)(2,1)S(1)} %collective-permute-done.8.refs_16_), channel_id=1, source_target_pairs={{0,48},{16,0},{32,16},{48,32},{1,49},{17,1},{33,17},{49,33},{2,50}... | collective-permute-start | bytes 3145736 | tf_op jit(solution)/shard_map/ppermute | solution.py:358
  65.3 11.4 %collective-permute-start.11 = (bf16[512,512]{1,0:T(8,128)(2,1)S(1)}, bf16[512,512]{1,0:T(8,128)(2,1)S(1)}, u32[]{:S(2)}, u32[]{:S(2)}) collective-permute-start(bf16[512,512]{1,0:T(8,128)(2,1)S(1)} %collective-permute-done.9.refs_6_), channel_id=1, source_target_pairs={{0,2},{2,4},{4,6},{6,0},{1,3},{3,5},{5,7},{7,1},{8,10},{10,12},{12... | collective-permute-start | bytes 1572872 | tf_op jit(solution)/shard_map/ppermute | solution.py:360
  65.3 14.1 %collective-permute-start.13 = (bf16[512,512]{1,0:T(8,128)(2,1)S(1)}, bf16[512,512]{1,0:T(8,128)(2,1)S(1)}, u32[]{:S(2)}, u32[]{:S(2)}) collective-permute-start(bf16[512,512]{1,0:T(8,128)(2,1)S(1)} %collective-permute-done.9.refs_6_), channel_id=1, source_target_pairs={{0,6},{2,0},{4,2},{6,4},{1,7},{3,1},{5,3},{7,5},{8,14},{10,8},{12,... | collective-permute-start | bytes 1572872 | tf_op jit(solution)/shard_map/ppermute | solution.py:360
  76.7 14.4 %collective-permute-start.12 = (bf16[512,512]{1,0:T(8,128)(2,1)S(1)}, bf16[512,512]{1,0:T(8,128)(2,1)S(1)}, u32[]{:S(2)}, u32[]{:S(2)}) collective-permute-start(bf16[512,512]{1,0:T(8,128)(2,1)S(1)} %collective-permute-done.7.refs_7_), channel_id=1, source_target_pairs={{0,2},{2,4},{4,6},{6,0},{1,3},{3,5},{5,7},{7,1},{8,10},{10,12},{12... | collective-permute-start | bytes 1572872 | tf_op jit(solution)/shard_map/ppermute | solution.py:363
  77.7 13.4 %collective-permute-start.20 = (bf16[256,1024]{1,0:T(8,128)(2,1)S(1)}, bf16[256,1024]{1,0:T(8,128)(2,1)S(1)}, u32[]{:S(2)}, u32[]{:S(2)}) collective-permute-start(bf16[256,1024]{1,0:T(8,128)(2,1)S(1)} %slice.28), channel_id=1, source_target_pairs={{0,16},{16,32},{32,48},{48,0},{1,17},{17,33},{33,49},{49,1},{2,18}... | collective-permute-start | bytes 1572872 | tf_op jit(solution)/shard_map/ppermute | solution.py:366
  79.2 11.9 %collective-permute-start.22 = (bf16[256,1024]{1,0:T(8,128)(2,1)S(1)}, bf16[256,1024]{1,0:T(8,128)(2,1)S(1)}, u32[]{:S(2)}, u32[]{:S(2)}) collective-permute-start(bf16[256,1024]{1,0:T(8,128)(2,1)S(1)} %slice.29), channel_id=1, source_target_pairs={{0,48},{16,0},{32,16},{48,32},{1,49},{17,1},{33,17},{49,33},{2,50}... | collective-permute-start | bytes 1572872 | tf_op jit(solution)/shard_map/ppermute | solution.py:366
  79.4 11.8 %collective-permute-start.14 = (bf16[512,512]{1,0:T(8,128)(2,1)S(1)}, bf16[512,512]{1,0:T(8,128)(2,1)S(1)}, u32[]{:S(2)}, u32[]{:S(2)}) collective-permute-start(bf16[512,512]{1,0:T(8,128)(2,1)S(1)} %collective-permute-done.13.refs_10_), channel_id=1, source_target_pairs={{0,6},{2,0},{4,2},{6,4},{1,7},{3,1},{5,3},{7,5},{8,14},{10,8},{12,... | collective-permute-start | bytes 1572872 | tf_op jit(solution)/shard_map/ppermute | solution.py:364
  94.8 9.2 %collective-permute-start.23 = (f32[1024,512]{1,0:T(8,128)S(1)}, f32[1024,512]{1,0:T(8,128)S(1)}, u32[]{:S(2)}, u32[]{:S(2)}) collective-permute-start(f32[1024,512]{1,0:T(8,128)S(1)} %get-tuple-element.35), channel_id=1, source_target_pairs={{0,1},{1,0},{2,3},{3,2},{4,5},{5,4},{6,7},{7,6},{8,9},{9,8},{10,11... | collective-permute-start | bytes 6291464 | tf_op jit(solution)/shard_map/ppermute | solution.py:372
  (12 other events, 523.1 us)

commit v5 on v4

--- a/solution.py
+++ b/solution.py
@@ -10,7 +10,6 @@
 CAP = 2
 RB = 8
 BLOCKS = RB * QB
-SEND = 16
 TAIL = 8
 ROWS = RB * BS
 COLS = QB * BS
@@ -25,32 +24,23 @@
     return (pattern_ref[j, i] > 0).astype(jnp.float32).astype(jnp.bfloat16)
 
 
-def mask_kernel(
-    where_ref, px_ref, py_ref, pz_ref, x_hbm, y_hbm, z_ref, xo_ref, top_ref, bottom_ref, yo_ref, x_ref, y_ref, sem
-):
-    first = where_ref[4] * (RB // 2)
-    own_rows = pl.ds(pl.multiple_of(first * BS, ROWS // 2), ROWS // 2)
-    x_copy = pltpu.make_async_copy(x_hbm, x_ref, sem.at[0])
-    y_copy = pltpu.make_async_copy(y_hbm.at[own_rows], y_ref, sem.at[1])
-    x_copy.start()
-    y_copy.start()
-    x_copy.wait()
+def mask_x_kernel(p_ref, x_ref, o_ref):
     for i in range(RB):
-        half_ref, shift = (top_ref, 0) if i < RB // 2 else (bottom_ref, RB // 2)
         for j in range(QB):
             rows, cols = slice(i * BS, (i + 1) * BS), slice(j * BS, (j + 1) * BS)
-            kept = x_ref[rows, cols] * keep_block(px_ref, j, i)
-            xo_ref[rows, cols] = kept
-            half_ref[slice((i - shift) * BS, (i - shift + 1) * BS), cols] = kept
-    y_copy.wait()
+            o_ref[rows, cols] = x_ref[rows, cols] * keep_block(p_ref, j, i)
+
+
+def mask_y_kernel(where_ref, p_ref, q_ref, y_ref, z_ref, o_ref):
+    first = where_ref[4] * (RB // 2)
     for i in range(RB // 2):
         rows = slice(i * BS, (i + 1) * BS)
-        peer_rows = pl.ds(pl.multiple_of((first + i) * BS, BS), BS)
+        own_rows = pl.ds(pl.multiple_of((first + i) * BS, BS), BS)
         for j in range(QB):
             cols = slice(j * BS, (j + 1) * BS)
             far_cols = slice(COLS + j * BS, COLS + (j + 1) * BS)
-            yo_ref[rows, cols] = y_ref[rows, cols] * keep_block(py_ref, j, first + i)
-            yo_ref[rows, far_cols] = z_ref[peer_rows, cols] * keep_block(pz_ref, j, first + i)
+            o_ref[rows, cols] = y_ref[own_rows, cols] * keep_block(p_ref, j, first + i)
+            o_ref[rows, far_cols] = z_ref[own_rows, cols] * keep_block(q_ref, j, first + i)
 
 
 SMEM = pl.BlockSpec(memory_space=pltpu.SMEM)
@@ -58,27 +48,28 @@
 HBM = pl.BlockSpec(memory_space=pltpu.HBM)
 
 
-def masked_tiles(where, pattern_x, pattern_y, pattern_peer, x, y, y_peer):
-    half = jax.ShapeDtypeStruct((ROWS // 2, COLS), jnp.bfloat16)
-    return pl.pallas_call(
-        mask_kernel,
-        in_specs=[SMEM] * 4 + [HBM] * 2 + [VMEM],
-        out_specs=[VMEM] * 4,
-        out_shape=[
-            jax.ShapeDtypeStruct((ROWS, COLS), jnp.bfloat16),
-            half,
-            half,
-            jax.ShapeDtypeStruct((ROWS // 2, 2 * COLS), jnp.bfloat16),
-        ],
-        scratch_shapes=[
-            pltpu.VMEM((ROWS, COLS), jnp.bfloat16),
-            pltpu.VMEM((ROWS // 2, COLS), jnp.bfloat16),
-            pltpu.SemaphoreType.DMA((2,)),
-        ],
-        compiler_params=pltpu.CompilerParams(vmem_limit_bytes=12 * 2**20),
-        cost_estimate=pl.CostEstimate(flops=2 * ROWS * COLS, bytes_accessed=12 * ROWS * COLS, transcendentals=0),
-        name="mask_tiles",
-    )(where, pattern_x, pattern_y, pattern_peer, x, y, y_peer)
+def mask_x(pattern, x):
+    return pl.pallas_call(
+        mask_x_kernel,
+        in_specs=[SMEM, VMEM],
+        out_specs=VMEM,
+        out_shape=jax.ShapeDtypeStruct((ROWS, COLS), jnp.bfloat16),
+        compiler_params=pltpu.CompilerParams(vmem_limit_bytes=8 * 2**20),
+        cost_estimate=pl.CostEstimate(flops=ROWS * COLS, bytes_accessed=4 * ROWS * COLS, transcendentals=0),
+        name="mask_x",
+    )(pattern, x)
+
+
+def mask_y(where, pattern, pattern_peer, y, y_peer):
+    return pl.pallas_call(
+        mask_y_kernel,
+        in_specs=[SMEM] * 3 + [VMEM] * 2,
+        out_specs=VMEM,
+        out_shape=jax.ShapeDtypeStruct((ROWS // 2, 2 * COLS), jnp.bfloat16),
+        compiler_params=pltpu.CompilerParams(vmem_limit_bytes=8 * 2**20),
+        cost_estimate=pl.CostEstimate(flops=ROWS * COLS, bytes_accessed=6 * ROWS * COLS, transcendentals=0),
+        name="mask_y",
+    )(where, pattern, pattern_peer, y, y_peer)
 
 
 def after(value, *others):
@@ -216,7 +207,7 @@
     )(where, *x_far, *y_far, x_late, y_late, own, far)
 
 
-def finish_kernel(where_ref, pattern_ref, index_ref, energy_ref, xm_ref, own_ref, peer_ref, sign_ref, payload_ref, dens, stage, out_sem):
+def finish_kernel(where_ref, pattern_ref, index_ref, energy_ref, xm_ref, own_ref, peer_ref, sign_ref, payload_ref, dens):
     yl, xi, yh, z, core = (where_ref[k] for k in range(5))
     block_row = (yl * 4 + xi) * RB
     block_col = ((yh * 4 + z) * 2 + core) * QB
@@ -238,25 +229,18 @@
     lax.fori_loop(0, RB, finish, 0)
     dens[BLOCKS] = jnp.zeros((BS, BS), jnp.bfloat16)
 
-    chunks = stage.shape[0] // SEND
     line = lax.broadcasted_iota(jnp.int32, (TAIL, BS), 0)
 
     def copy(owner, carry):
         energies = jnp.zeros((TAIL, BS), jnp.float32)
         for k in range(CAP):
             block = index_ref[owner * CAP + k]
-            stage[owner, k * BS : (k + 1) * BS, :] = dens[block]
+            payload_ref[owner, k * BS : (k + 1) * BS, :] = dens[block]
             energies = jnp.where(line == k, energy_ref[block // QB], energies)
-        stage[owner, CAP * BS :, :] = energies.astype(jnp.bfloat16)
+        payload_ref[owner, CAP * BS :, :] = energies.astype(jnp.bfloat16)
         return carry
 
-    for chunk in range(chunks):
-        lax.fori_loop(chunk * SEND, (chunk + 1) * SEND, copy, 0, unroll=4)
-        part = pl.ds(chunk * SEND, SEND)
-        pltpu.make_async_copy(stage.at[part], payload_ref.at[part], out_sem.at[chunk]).start()
-    for chunk in range(chunks):
-        part = pl.ds(chunk * SEND, SEND)
-        pltpu.make_async_copy(stage.at[part], payload_ref.at[part], out_sem.at[chunk]).wait()
+    lax.fori_loop(0, payload_ref.shape[0], copy, 0, unroll=4)
 
 
 def finish_and_payload(where, pattern, index, energy, xm, own, peer):
@@ -265,15 +249,13 @@
     return pl.pallas_call(
         finish_kernel,
         in_specs=[SMEM] * 3 + [VMEM] * 4,
-        out_specs=[VMEM, HBM],
+        out_specs=[VMEM, VMEM],
         out_shape=[
             jax.ShapeDtypeStruct((ROWS, COLS), jnp.bfloat16),
             jax.ShapeDtypeStruct(packet, jnp.bfloat16),
         ],
         scratch_shapes=[
             pltpu.VMEM((BLOCKS + 1, BS, BS), jnp.bfloat16),
-            pltpu.VMEM(packet, jnp.bfloat16),
-            pltpu.SemaphoreType.DMA((owners // SEND,)),
         ],
         compiler_params=pltpu.CompilerParams(vmem_limit_bytes=18 * 2**20),
         cost_estimate=pl.CostEstimate(flops=4 * ROWS * COLS, bytes_accessed=15 * 2**20, transcendentals=0),
@@ -337,17 +319,16 @@
     half, quarter = ROWS // 2, ROWS // 4
     y_peer = lax.ppermute(y, "c", SWAP)
     pattern_peer = lax.ppermute(pattern_y.T, "c", SWAP)
-    xm, xm_top, xm_bottom, ym = masked_tiles(
-        where, pattern_x.T, pattern_y.T, pattern_peer, x, y, y_peer
-    )
-
-    xb_top = lax.ppermute(xm_top, "yh", SWAP)
+    xm = mask_x(pattern_x.T, x)
+    ym = mask_y(where, pattern_y.T, pattern_peer, y, y_peer)
+
+    xb_top = lax.ppermute(xm[:half], "yh", SWAP)
     xa_below = lax.ppermute(xm, "z", UP)
     xa_above = lax.ppermute(xm, "z", DOWN)
     ya_below = lax.ppermute(ym, "x", UP)
     ya_above = lax.ppermute(ym, "x", DOWN)
     yb = lax.ppermute(after(ym, xb_top), "yl", SWAP)
-    xb_bottom = lax.ppermute(after(xm_bottom, yb), "yh", SWAP)
+    xb_bottom = lax.ppermute(after(xm[half:], yb), "yh", SWAP)
 
     xa_far = [lax.ppermute(xa_below[:half], "z", UP), lax.ppermute(xa_above[half:], "z", DOWN)]
     ya_far = [lax.ppermute(ya_below[:quarter], "x", UP), lax.ppermute(ya_above[quarter:], "x", DOWN)]

time: 230 us -> 227 us (0.987)
  waiting for transfers between devices: 50.4 us -> 45.1 us
    ppermute x1, waiting for transfers between devices: 2.32 us -> 0.01 us  [shards(): pattern_peer = lax.ppermute(pattern_y.T, 'c', SWAP)]
  transfers between devices with their start and end apart: 24 -> 24, of which waited for: 10 -> 9; matrix products, arithmetic and copies ran while one was open for 0% -> 2% of each run, Pallas kernels for 4% -> 5%
where the time goes in v5:
time: 227 us
  blocking collectives  114 us (50%)
  waiting for transfers between devices  45.1 us (20%)
  starting transfers between devices  35 us (15%)
  Pallas kernels  25.2 us (11%)
  local copies, waits for them, and re-layouts  5.37 us (2%)
    all_to_all x1, blocking collectives, exchange(): lax.all_to_all(payload, AXES, split_axis=0, concat_axis=0, tiled=True)  114 us
    pallas_call x1, Pallas kernels, early_product(): pl.pallas_call(early_kernel, in_specs=[HBM] * (len(X_PIECES) + len(Y_PIEC...  9.89 us
    ppermute x1, waiting for transfers between devices, shards(): xb_top = lax.ppermute(xm[:half], 'yh', SWAP)  9.66 us
    ppermute x1, waiting for transfers between devices, shards(): lax.ppermute(xb_bottom_z, 'z', UP)  8.98 us
    ppermute x1, waiting for transfers between devices, shards(): lax.ppermute(xa_below[:half], 'z', UP)  7.54 us
    ppermute x1, waiting for transfers between devices, shards(): lax.ppermute(xb_top_z, 'z', UP)  6.27 us
    pallas_call x1, Pallas kernels, force_sums(): pl.pallas_call(force_kernel, grid=(slots // (FCH * CAP),), in_specs=[pl.B...  6.02 us
    ppermute x1, waiting for transfers between devices, shards(): xa_below = lax.ppermute(xm, 'z', UP)  5.79 us
  transfers between devices with their start and end apart: 24, of which 9 were waited for; matrix products, arithmetic and copies ran while one was open for 2% of the time, Pallas kernels for 5%

profile of v5, /device:TPU:7, one launch (start us, length us, event | category | flops | bytes accessed | tf_op | source)
XLA Modules:
  0.0 226.6 jit_solution(16439340387198388734)
XLA Ops:
  4.1 1.7 collective-permute-start.1
  5.8 2.2 collective-permute-start.3
  9.3 2.9 %collective-permute-start = (bf16[512,512]{1,0:T(8,128)(2,1)}, bf16[512,512]{1,0:T(8,128)(2,1)}, u32[]{:S(2)}, u32[]{:S(2)}) collective-permute-start(bf16[512,512]{1,0:T(8,128)(2,1)} %get-tuple-element.31), channel_id=1, source_target_pairs={{0,8},{8,0},{1,9},{9,1},{2,10},{10,2},{3,11},{11,3},{4,12},{12,4},... | collective-permute-start | bytes 1572872 | tf_op jit(solution)/shard_map/ppermute | solution.py:325
  14.8 9.7 %collective-permute-done.refs_5_ = bf16[512,512]{1,0:T(8,128)(2,1)} collective-permute-done((bf16[512,512]{1,0:T(8,128)(2,1)}, bf16[512,512]{1,0:T(8,128)(2,1)}, u32[]{:S(2)}, u32[]{:S(2)}) %collective-permute-start) | collective-permute-done | bytes 524320 | tf_op jit(solution)/shard_map/ppermute | solution.py:325
  24.5 1.3 collective-permute-start.8
  25.8 5.8 %collective-permute-done.1.refs_1_ = bf16[1024,512]{1,0:T(8,128)(2,1)} collective-permute-done((bf16[1024,512]{1,0:T(8,128)(2,1)S(1)}, bf16[1024,512]{1,0:T(8,128)(2,1)}, u32[]{:S(2)}, u32[]{:S(2)}) %collective-permute-start.1) | collective-permute-done | bytes 1048608 | tf_op jit(solution)/shard_map/ppermute | solution.py:326
  33.8 2.7 %collective-permute-start.4 = (bf16[512,512]{1,0:T(8,128)(2,1)S(1)}, bf16[512,512]{1,0:T(8,128)(2,1)S(1)}, u32[]{:S(2)}, u32[]{:S(2)}) collective-permute-start(bf16[512,512]{1,0:T(8,128)(2,1)S(1)} %slice.34), channel_id=1, source_target_pairs={{0,6},{2,0},{4,2},{6,4},{1,7},{3,1},{5,3},{7,5},{8,14},{10,8},{12,... | collective-permute-start | bytes 1572872 | tf_op jit(solution)/shard_map/ppermute | solution.py:333
  37.6 1.5 collective-permute-start.16
  39.3 7.5 %collective-permute-done.2.refs_3_ = bf16[512,512]{1,0:T(8,128)(2,1)S(1)} collective-permute-done((bf16[512,512]{1,0:T(8,128)(2,1)S(1)}, bf16[512,512]{1,0:T(8,128)(2,1)S(1)}, u32[]{:S(2)}, u32[]{:S(2)}) %collective-permute-start.2) | collective-permute-done | bytes 524320 | tf_op jit(solution)/shard_map/ppermute | solution.py:333
  47.0 3.3 %collective-permute-start.10 = (bf16[512,512]{1,0:T(8,128)(2,1)}, bf16[512,512]{1,0:T(8,128)(2,1)S(1)}, u32[]{:S(2)}, u32[]{:S(2)}) collective-permute-start(bf16[512,512]{1,0:T(8,128)(2,1)} %collective-permute-done.refs_5_), channel_id=1, source_target_pairs={{0,6},{2,0},{4,2},{6,4},{1,7},{3,1},{5,3},{7,5},{8,14},{10,8},{12,... | collective-permute-start | bytes 1572872 | tf_op jit(solution)/shard_map/ppermute | solution.py:337
  50.3 2.9 %collective-permute-start.9 = (bf16[512,512]{1,0:T(8,128)(2,1)S(1)}, bf16[512,512]{1,0:T(8,128)(2,1)S(1)}, u32[]{:S(2)}, u32[]{:S(2)}) collective-permute-start(bf16[512,512]{1,0:T(8,128)(2,1)S(1)} %copy-done.5), channel_id=1, source_target_pairs={{0,8},{8,0},{1,9},{9,1},{2,10},{10,2},{3,11},{11,3},{4,12},{12,4},... | collective-permute-start | bytes 1572872 | tf_op jit(solution)/shard_map/ppermute | solution.py:331
  54.7 6.3 %collective-permute-done.5.refs_7_ = bf16[512,512]{1,0:T(8,128)(2,1)S(1)} collective-permute-done((bf16[512,512]{1,0:T(8,128)(2,1)}, bf16[512,512]{1,0:T(8,128)(2,1)S(1)}, u32[]{:S(2)}, u32[]{:S(2)}) %collective-permute-start.5) | collective-permute-done | bytes 524320 | tf_op jit(solution)/shard_map/ppermute | solution.py:337
  61.0 2.2 collective-permute-done.9.refs_6_
  63.2 2.7 %collective-permute-start.13 = (bf16[512,512]{1,0:T(8,128)(2,1)S(1)}, bf16[512,512]{1,0:T(8,128)(2,1)S(1)}, u32[]{:S(2)}, u32[]{:S(2)}) collective-permute-start(bf16[512,512]{1,0:T(8,128)(2,1)S(1)} %collective-permute-done.9.refs_6_), channel_id=1, source_target_pairs={{0,6},{2,0},{4,2},{6,4},{1,7},{3,1},{5,3},{7,5},{8,14},{10,8},{12,... | collective-permute-start | bytes 1572872 | tf_op jit(solution)/shard_map/ppermute | solution.py:341
  65.9 9.0 %collective-permute-done.11.refs_8_ = bf16[512,512]{1,0:T(8,128)(2,1)S(1)} collective-permute-done((bf16[512,512]{1,0:T(8,128)(2,1)S(1)}, bf16[512,512]{1,0:T(8,128)(2,1)S(1)}, u32[]{:S(2)}, u32[]{:S(2)}) %collective-permute-start.11) | collective-permute-done | bytes 524320 | tf_op jit(solution)/shard_map/ppermute | solution.py:341
  74.9 2.7 %collective-permute-start.14 = (bf16[512,512]{1,0:T(8,128)(2,1)S(1)}, bf16[512,512]{1,0:T(8,128)(2,1)S(1)}, u32[]{:S(2)}, u32[]{:S(2)}) collective-permute-start(bf16[512,512]{1,0:T(8,128)(2,1)S(1)} %collective-permute-done.13.refs_10_), channel_id=1, source_target_pairs={{0,6},{2,0},{4,2},{6,4},{1,7},{3,1},{5,3},{7,5},{8,14},{10,8},{12,... | collective-permute-start | bytes 1572872 | tf_op jit(solution)/shard_map/ppermute | solution.py:345
  77.9 1.3 collective-permute-start.22
  79.2 9.9 %early_product.1 = (f32[1024,512]{1,0:T(8,128)S(1)}, f32[1024,512]{1,0:T(8,128)S(1)}, bf16[1024,512]{1,0:T(8,128)(2,1)S(1)}, bf16[512,1024]{1,0:T(8,128)(2,1)S(1)}) custom-call(bf16[1024,512]{1,0:T(8,128)(2,1)S(1)} %mask_x.1.refs_0_.xm_ref, bf16[1024,512]{1,0:T(8,128)(2,1)} %collective-permute-done.1.refs_1_, ...), custom_call_target="tpu_custom_call" | custom-call | flops 7516192768 | bytes 20971520 | tf_op jit(solution)/shard_map/early_product/pallas_call | solution.py:140
  89.2 3.6 %late_product.1 = (f32[1024,512]{1,0:T(8,128)S(1)}, f32[1024,512]{1,0:T(8,128)S(1)}) custom-call(s32[5]{0:T(128)S(1)} %stack.23.where_ref.refs_19_, bf16[512,512]{1,0:T(8,128)(2,1)S(1)} %collective-permute-done.12.x_top, bf16[512,512]{1,0:T(8,128)(2,1)S(1)} %collective-permute-done.14.x_bottom, bf16[256,1024]{1,0:T(8,128)(2,1)S(1)} %collective-permute-done.20.y_top, ...), custom_call_target="tpu_custom_call" | custom-call | flops 2147483648 | bytes 12582912 | tf_op jit(solution)/shard_map/late_product/pallas_call | solution.py:196
  92.8 5.1 %collective-permute-start.23 = (f32[1024,512]{1,0:T(8,128)S(1)}, f32[1024,512]{1,0:T(8,128)S(1)}, u32[]{:S(2)}, u32[]{:S(2)}) collective-permute-start(f32[1024,512]{1,0:T(8,128)S(1)} %get-tuple-element.27), channel_id=1, source_target_pairs={{0,1},{1,0},{2,3},{3,2},{4,5},{5,4},{6,7},{7,6},{8,9},{9,8},{10,11... | collective-permute-start | bytes 6291464 | tf_op jit(solution)/shard_map/ppermute | solution.py:353
  98.3 3.4 %collective-permute-done.23.peer_ref = f32[1024,512]{1,0:T(8,128)S(1)} collective-permute-done((f32[1024,512]{1,0:T(8,128)S(1)}, f32[1024,512]{1,0:T(8,128)S(1)}, u32[]{:S(2)}, u32[]{:S(2)}) %collective-permute-start.23) | collective-permute-done | bytes 2097184 | tf_op jit(solution)/shard_map/ppermute | solution.py:353
  101.7 4.0 %finish_payload.1 = (bf16[1024,512]{1,0:T(8,128)(2,1)}, bf16[128,264,128]{2,1,0:T(8,128)(2,1)S(1)}) custom-call(s32[5]{0:T(128)S(1)} %stack.23.where_ref.refs_19_, s32[4,8]{1,0:T(4,128)S(1)} %bitcast.17, s32[256]{0:T(256)S(1)} %broadcast_add_fusion.index_ref, f32[9,1,128]{2,1,0:T(1,128)S(1)} %pad_convert_fusion.energy_ref, ...), custom_call_target="tpu_custom_call" | custom-call | flops 2097152 | bytes 15728640 | tf_op jit(solution)/shard_map/finish_payload/pallas_call | solution.py:249
  105.7 114.1 %all_to_all.5.d_ref = bf16[128,264,128]{2,1,0:T(8,128)(2,1)S(1)} all-to-all(bf16[128,264,128]{2,1,0:T(8,128)(2,1)S(1)} %get-tuple-element.29), channel_id=1, replica_groups=mesh['yl'=2,'x'=4,'yh'=2,'z'=4,'c'=2] {'yl','x','yh','z','c'}, dimensions={0} | all-to-all | bytes 17301504 | tf_op jit(solution)/shard_map/all_to_all | solution.py:303
  219.9 6.0 %force_sums.1 = f32[256,128]{1,0:T(8,128)S(1)} custom-call(bf16[128,264,128]{2,1,0:T(8,128)(2,1)S(1)} %all_to_all.5.d_ref, bf16[256,128,128]{2,1,0:T(8,128)(2,1)S(1)} %bitcast.14, bf16[256,128,128]{2,1,0:T(8,128)(2,1)S(1)} %bitcast.16), custom_call_target="tpu_custom_call" | custom-call | flops 25165824 | bytes 25165824 | tf_op jit(solution)/shard_map/force_sums/pallas_call | solution.py:287
  (75 shorter events, 13.8 us)
Async XLA Ops:
  0.6 11.7 %collective-permute-start.7 = (bf16[1024,512]{1,0:T(8,128)(2,1)}, bf16[1024,512]{1,0:T(8,128)(2,1)S(1)}, u32[]{:S(2)}, u32[]{:S(2)}) collective-permute-start(bf16[1024,512]{1,0:T(8,128)(2,1)} %y_ref.1), channel_id=1, source_target_pairs={{0,1},{1,0},{2,3},{3,2},{4,5},{5,4},{6,7},{7,6},{8,9},{9,8},{10,11... | collective-permute-start | bytes 3145736 | tf_op jit(solution)/shard_map/ppermute | solution.py:320
  4.1 27.5 %collective-permute-start.1 = (bf16[1024,512]{1,0:T(8,128)(2,1)S(1)}, bf16[1024,512]{1,0:T(8,128)(2,1)}, u32[]{:S(2)}, u32[]{:S(2)}) collective-permute-start(bf16[1024,512]{1,0:T(8,128)(2,1)S(1)} %mask_x.1.refs_0_.xm_ref), channel_id=1, source_target_pairs={{0,2},{2,4},{4,6},{6,0},{1,3},{3,5},{5,7},{7,1},{8,10},{10,12},{12... | collective-permute-start | bytes 3145736 | tf_op jit(solution)/shard_map/ppermute | solution.py:326
  5.8 26.9 %collective-permute-start.3 = (bf16[1024,512]{1,0:T(8,128)(2,1)S(1)}, bf16[1024,512]{1,0:T(8,128)(2,1)}, u32[]{:S(2)}, u32[]{:S(2)}) collective-permute-start(bf16[1024,512]{1,0:T(8,128)(2,1)S(1)} %mask_x.1.refs_0_.xm_ref), channel_id=1, source_target_pairs={{0,6},{2,0},{4,2},{6,4},{1,7},{3,1},{5,3},{7,5},{8,14},{10,8},{12,... | collective-permute-start | bytes 3145736 | tf_op jit(solution)/shard_map/ppermute | solution.py:327
  8.0 4.3 %collective-permute-start.6 = (s32[4,8]{1,0:T(4,128)S(1)}, s32[4,8]{1,0:T(4,128)S(1)}, u32[]{:S(2)}, u32[]{:S(2)}) collective-permute-start(s32[4,8]{1,0:T(4,128)S(1)} %bitcast.19), channel_id=1, source_target_pairs={{0,1},{1,0},{2,3},{3,2},{4,5},{5,4},{6,7},{7,6},{8,9},{9,8},{10,11... | collective-permute-start | bytes 392 | tf_op jit(solution)/shard_map/ppermute | solution.py:321
  9.3 15.1 %collective-permute-start = (bf16[512,512]{1,0:T(8,128)(2,1)}, bf16[512,512]{1,0:T(8,128)(2,1)}, u32[]{:S(2)}, u32[]{:S(2)}) collective-permute-start(bf16[512,512]{1,0:T(8,128)(2,1)} %get-tuple-element.31), channel_id=1, source_target_pairs={{0,8},{8,0},{1,9},{9,1},{2,10},{10,2},{3,11},{11,3},{4,12},{12,4},... | collective-permute-start | bytes 1572872 | tf_op jit(solution)/shard_map/ppermute | solution.py:325
  13.3 24.3 %collective-permute-start.15 = (bf16[512,1024]{1,0:T(8,128)(2,1)S(1)}, bf16[512,1024]{1,0:T(8,128)(2,1)S(1)}, u32[]{:S(2)}, u32[]{:S(2)}) collective-permute-start(bf16[512,1024]{1,0:T(8,128)(2,1)S(1)} %mask_y.1.refs_11_), channel_id=1, source_target_pairs={{0,16},{16,32},{32,48},{48,0},{1,17},{17,33},{33,49},{49,1},{2,18}... | collective-permute-start | bytes 3145736 | tf_op jit(solution)/shard_map/ppermute | solution.py:328
  13.5 25.6 %collective-permute-start.17 = (bf16[512,1024]{1,0:T(8,128)(2,1)S(1)}, bf16[512,1024]{1,0:T(8,128)(2,1)S(1)}, u32[]{:S(2)}, u32[]{:S(2)}) collective-permute-start(bf16[512,1024]{1,0:T(8,128)(2,1)S(1)} %mask_y.1.refs_11_), channel_id=1, source_target_pairs={{0,48},{16,0},{32,16},{48,32},{1,49},{17,1},{33,17},{49,33},{2,50}... | collective-permute-start | bytes 3145736 | tf_op jit(solution)/shard_map/ppermute | solution.py:329
  24.5 25.9 %collective-permute-start.8 = (bf16[512,1024]{1,0:T(8,128)(2,1)S(1)}, bf16[512,1024]{1,0:T(8,128)(2,1)S(1)}, u32[]{:S(2)}, u32[]{:S(2)}) collective-permute-start(bf16[512,1024]{1,0:T(8,128)(2,1)S(1)} %mask_y.1.refs_11_), channel_id=1, source_target_pairs={{0,64},{64,0},{1,65},{65,1},{2,66},{66,2},{3,67},{67,3},{4,68},{68... | collective-permute-start | bytes 3145736 | tf_op jit(solution)/shard_map/ppermute | solution.py:330
  32.6 14.2 %collective-permute-start.2 = (bf16[512,512]{1,0:T(8,128)(2,1)S(1)}, bf16[512,512]{1,0:T(8,128)(2,1)S(1)}, u32[]{:S(2)}, u32[]{:S(2)}) collective-permute-start(bf16[512,512]{1,0:T(8,128)(2,1)S(1)} %slice.33), channel_id=1, source_target_pairs={{0,2},{2,4},{4,6},{6,0},{1,3},{3,5},{5,7},{7,1},{8,10},{10,12},{12... | collective-permute-start | bytes 1572872 | tf_op jit(solution)/shard_map/ppermute | solution.py:333
  33.8 13.1 %collective-permute-start.4 = (bf16[512,512]{1,0:T(8,128)(2,1)S(1)}, bf16[512,512]{1,0:T(8,128)(2,1)S(1)}, u32[]{:S(2)}, u32[]{:S(2)}) collective-permute-start(bf16[512,512]{1,0:T(8,128)(2,1)S(1)} %slice.34), channel_id=1, source_target_pairs={{0,6},{2,0},{4,2},{6,4},{1,7},{3,1},{5,3},{7,5},{8,14},{10,8},{12,... | collective-permute-start | bytes 1572872 | tf_op jit(solution)/shard_map/ppermute | solution.py:333
  37.6 15.6 %collective-permute-start.16 = (bf16[256,1024]{1,0:T(8,128)(2,1)S(1)}, bf16[256,1024]{1,0:T(8,128)(2,1)S(1)}, u32[]{:S(2)}, u32[]{:S(2)}) collective-permute-start(bf16[256,1024]{1,0:T(8,128)(2,1)S(1)} %slice.36), channel_id=1, source_target_pairs={{0,16},{16,32},{32,48},{48,0},{1,17},{17,33},{33,49},{49,1},{2,18}... | collective-permute-start | bytes 1572872 | tf_op jit(solution)/shard_map/ppermute | solution.py:334
  39.1 14.1 %collective-permute-start.18 = (bf16[256,1024]{1,0:T(8,128)(2,1)S(1)}, bf16[256,1024]{1,0:T(8,128)(2,1)S(1)}, u32[]{:S(2)}, u32[]{:S(2)}) collective-permute-start(bf16[256,1024]{1,0:T(8,128)(2,1)S(1)} %slice.37), channel_id=1, source_target_pairs={{0,48},{16,0},{32,16},{48,32},{1,49},{17,1},{33,17},{49,33},{2,50}... | collective-permute-start | bytes 1572872 | tf_op jit(solution)/shard_map/ppermute | solution.py:334
  46.9 14.1 %collective-permute-start.5 = (bf16[512,512]{1,0:T(8,128)(2,1)}, bf16[512,512]{1,0:T(8,128)(2,1)S(1)}, u32[]{:S(2)}, u32[]{:S(2)}) collective-permute-start(bf16[512,512]{1,0:T(8,128)(2,1)} %collective-permute-done.refs_5_), channel_id=1, source_target_pairs={{0,2},{2,4},{4,6},{6,0},{1,3},{3,5},{5,7},{7,1},{8,10},{10,12},{12... | collective-permute-start | bytes 1572872 | tf_op jit(solution)/shard_map/ppermute | solution.py:337
  47.0 14.0 %collective-permute-start.10 = (bf16[512,512]{1,0:T(8,128)(2,1)}, bf16[512,512]{1,0:T(8,128)(2,1)S(1)}, u32[]{:S(2)}, u32[]{:S(2)}) collective-permute-start(bf16[512,512]{1,0:T(8,128)(2,1)} %collective-permute-done.refs_5_), channel_id=1, source_target_pairs={{0,6},{2,0},{4,2},{6,4},{1,7},{3,1},{5,3},{7,5},{8,14},{10,8},{12,... | collective-permute-start | bytes 1572872 | tf_op jit(solution)/shard_map/ppermute | solution.py:337
  50.3 12.9 %collective-permute-start.9 = (bf16[512,512]{1,0:T(8,128)(2,1)S(1)}, bf16[512,512]{1,0:T(8,128)(2,1)S(1)}, u32[]{:S(2)}, u32[]{:S(2)}) collective-permute-start(bf16[512,512]{1,0:T(8,128)(2,1)S(1)} %copy-done.5), channel_id=1, source_target_pairs={{0,8},{8,0},{1,9},{9,1},{2,10},{10,2},{3,11},{11,3},{4,12},{12,4},... | collective-permute-start | bytes 1572872 | tf_op jit(solution)/shard_map/ppermute | solution.py:331
  53.2 24.3 %collective-permute-start.19 = (bf16[512,1024]{1,0:T(8,128)(2,1)S(1)}, bf16[512,1024]{1,0:T(8,128)(2,1)S(1)}, u32[]{:S(2)}, u32[]{:S(2)}) collective-permute-start(bf16[512,1024]{1,0:T(8,128)(2,1)S(1)} %collective-permute-done.8.refs_16_), channel_id=1, source_target_pairs={{0,16},{16,32},{32,48},{48,0},{1,17},{17,33},{33,49},{49,1},{2,18}... | collective-permute-start | bytes 3145736 | tf_op jit(solution)/shard_map/ppermute | solution.py:339
  53.4 24.4 %collective-permute-start.21 = (bf16[512,1024]{1,0:T(8,128)(2,1)S(1)}, bf16[512,1024]{1,0:T(8,128)(2,1)S(1)}, u32[]{:S(2)}, u32[]{:S(2)}) collective-permute-start(bf16[512,1024]{1,0:T(8,128)(2,1)S(1)} %collective-permute-done.8.refs_16_), channel_id=1, source_target_pairs={{0,48},{16,0},{32,16},{48,32},{1,49},{17,1},{33,17},{49,33},{2,50}... | collective-permute-start | bytes 3145736 | tf_op jit(solution)/shard_map/ppermute | solution.py:339
  63.2 11.7 %collective-permute-start.11 = (bf16[512,512]{1,0:T(8,128)(2,1)S(1)}, bf16[512,512]{1,0:T(8,128)(2,1)S(1)}, u32[]{:S(2)}, u32[]{:S(2)}) collective-permute-start(bf16[512,512]{1,0:T(8,128)(2,1)S(1)} %collective-permute-done.9.refs_6_), channel_id=1, source_target_pairs={{0,2},{2,4},{4,6},{6,0},{1,3},{3,5},{5,7},{7,1},{8,10},{10,12},{12... | collective-permute-start | bytes 1572872 | tf_op jit(solution)/shard_map/ppermute | solution.py:341
  63.2 11.7 %collective-permute-start.13 = (bf16[512,512]{1,0:T(8,128)(2,1)S(1)}, bf16[512,512]{1,0:T(8,128)(2,1)S(1)}, u32[]{:S(2)}, u32[]{:S(2)}) collective-permute-start(bf16[512,512]{1,0:T(8,128)(2,1)S(1)} %collective-permute-done.9.refs_6_), channel_id=1, source_target_pairs={{0,6},{2,0},{4,2},{6,4},{1,7},{3,1},{5,3},{7,5},{8,14},{10,8},{12,... | collective-permute-start | bytes 1572872 | tf_op jit(solution)/shard_map/ppermute | solution.py:341
  74.8 14.3 %collective-permute-start.12 = (bf16[512,512]{1,0:T(8,128)(2,1)S(1)}, bf16[512,512]{1,0:T(8,128)(2,1)S(1)}, u32[]{:S(2)}, u32[]{:S(2)}) collective-permute-start(bf16[512,512]{1,0:T(8,128)(2,1)S(1)} %collective-permute-done.5.refs_7_), channel_id=1, source_target_pairs={{0,2},{2,4},{4,6},{6,0},{1,3},{3,5},{5,7},{7,1},{8,10},{10,12},{12... | collective-permute-start | bytes 1572872 | tf_op jit(solution)/shard_map/ppermute | solution.py:344
  74.9 14.3 %collective-permute-start.14 = (bf16[512,512]{1,0:T(8,128)(2,1)S(1)}, bf16[512,512]{1,0:T(8,128)(2,1)S(1)}, u32[]{:S(2)}, u32[]{:S(2)}) collective-permute-start(bf16[512,512]{1,0:T(8,128)(2,1)S(1)} %collective-permute-done.13.refs_10_), channel_id=1, source_target_pairs={{0,6},{2,0},{4,2},{6,4},{1,7},{3,1},{5,3},{7,5},{8,14},{10,8},{12,... | collective-permute-start | bytes 1572872 | tf_op jit(solution)/shard_map/ppermute | solution.py:345
  77.6 11.6 %collective-permute-start.20 = (bf16[256,1024]{1,0:T(8,128)(2,1)S(1)}, bf16[256,1024]{1,0:T(8,128)(2,1)S(1)}, u32[]{:S(2)}, u32[]{:S(2)}) collective-permute-start(bf16[256,1024]{1,0:T(8,128)(2,1)S(1)} %slice.38), channel_id=1, source_target_pairs={{0,16},{16,32},{32,48},{48,0},{1,17},{17,33},{33,49},{49,1},{2,18}... | collective-permute-start | bytes 1572872 | tf_op jit(solution)/shard_map/ppermute | solution.py:347
  77.9 11.3 %collective-permute-start.22 = (bf16[256,1024]{1,0:T(8,128)(2,1)S(1)}, bf16[256,1024]{1,0:T(8,128)(2,1)S(1)}, u32[]{:S(2)}, u32[]{:S(2)}) collective-permute-start(bf16[256,1024]{1,0:T(8,128)(2,1)S(1)} %slice.39), channel_id=1, source_target_pairs={{0,48},{16,0},{32,16},{48,32},{1,49},{17,1},{33,17},{49,33},{2,50}... | collective-permute-start | bytes 1572872 | tf_op jit(solution)/shard_map/ppermute | solution.py:347
  92.8 8.9 %collective-permute-start.23 = (f32[1024,512]{1,0:T(8,128)S(1)}, f32[1024,512]{1,0:T(8,128)S(1)}, u32[]{:S(2)}, u32[]{:S(2)}) collective-permute-start(f32[1024,512]{1,0:T(8,128)S(1)} %get-tuple-element.27), channel_id=1, source_target_pairs={{0,1},{1,0},{2,3},{3,2},{4,5},{5,4},{6,7},{7,6},{8,9},{9,8},{10,11... | collective-permute-start | bytes 6291464 | tf_op jit(solution)/shard_map/ppermute | solution.py:353
  (13 other events, 568.8 us)

commit v6 on v5

--- a/solution.py
+++ b/solution.py
@@ -161,53 +161,48 @@
     )(*x_parts, *y_parts, where)
 
 
-def late_kernel(where_ref, x_top, x_bottom, y_top, y_bottom, x_late, y_late, own_ref, far_ref, own_out, far_out):
+def late_kernel(where_ref, x_top, x_bottom, y_top, y_bottom, x_late, y_late, sum_ref, out_ref):
     last = y_place(where_ref, EARLY)
     quarter = ROWS // 4
 
     def add(x_far, same_chunk):
         x_last = x_far if same_chunk else x_late
-        for sum_ref, out_ref, cols in (
-            (own_ref, own_out, slice(0, COLS)),
-            (far_ref, far_out, slice(COLS, 2 * COLS)),
-        ):
-            total = sum_ref[...]
-            total += jnp.dot(x_last[:, :quarter], y_top[:, cols], preferred_element_type=jnp.float32)
-            total += jnp.dot(x_last[:, quarter:], y_bottom[:, cols], preferred_element_type=jnp.float32)
-            if not same_chunk:
-                total += jnp.dot(x_far[...], y_late[:, cols], preferred_element_type=jnp.float32)
-            out_ref[...] = total
+        total = sum_ref[...]
+        total += jnp.dot(x_last[:, :quarter], y_top[...], preferred_element_type=jnp.float32)
+        total += jnp.dot(x_last[:, quarter:], y_bottom[...], preferred_element_type=jnp.float32)
+        if not same_chunk:
+            total += jnp.dot(x_far[...], y_late[...], preferred_element_type=jnp.float32)
+        out_ref[...] = total
 
     for upper, x_far in ((True, x_top), (False, x_bottom)):
         for same_chunk in (True, False):
-            here = (pl.program_id(0) < 2) == upper
+            here = (pl.program_id(0) < 1) == upper
             pl.when(here & ((last == EARLY) == same_chunk))(lambda x=x_far, t=same_chunk: add(x, t))
 
 
-def late_product(where, x_far, y_far, x_late, y_late, own, far):
-    quarter = ROWS // 4
-    top = pl.BlockSpec((quarter, COLS), lambda m: (jnp.minimum(m, 1), 0))
-    bottom = pl.BlockSpec((quarter, COLS), lambda m: (jnp.maximum(m - 2, 0), 0))
-    rows = pl.BlockSpec((quarter, COLS), lambda m: (m, 0))
-
-    def whole(height):
-        return pl.BlockSpec((height, 2 * COLS), lambda m: (0, 0))
+def late_product(side, where, x_far, y_far, x_late, y_late, total):
+    half, quarter = ROWS // 2, ROWS // 4
+    rows = pl.BlockSpec((half, COLS), lambda m: (m, 0))
+    whole = pl.BlockSpec((half, COLS), lambda m: (0, 0))
+
+    def columns(height):
+        return pl.BlockSpec((height, COLS), lambda m: (0, side))
 
     return pl.pallas_call(
         late_kernel,
-        grid=(4,),
-        in_specs=[SMEM, top, bottom, whole(quarter), whole(quarter), rows, whole(2 * quarter), rows, rows],
-        out_specs=[rows] * 2,
-        out_shape=[jax.ShapeDtypeStruct((ROWS, COLS), jnp.float32)] * 2,
-        compiler_params=pltpu.CompilerParams(vmem_limit_bytes=24 * 2**20),
+        grid=(2,),
+        in_specs=[SMEM, whole, whole, columns(quarter), columns(quarter), rows, columns(half), rows],
+        out_specs=rows,
+        out_shape=jax.ShapeDtypeStruct((ROWS, COLS), jnp.float32),
+        compiler_params=pltpu.CompilerParams(vmem_limit_bytes=16 * 2**20),
         cost_estimate=pl.CostEstimate(
-            flops=4 * ROWS * COLS * ROWS, bytes_accessed=12 * 2**20, transcendentals=0
+            flops=2 * ROWS * COLS * ROWS, bytes_accessed=8 * 2**20, transcendentals=0
         ),
         name="late_product",
-    )(where, *x_far, *y_far, x_late, y_late, own, far)
-
-
-def finish_kernel(where_ref, pattern_ref, index_ref, energy_ref, xm_ref, own_ref, peer_ref, sign_ref, payload_ref, dens):
+    )(where, *x_far, *y_far, x_late, y_late, total)
+
+
+def finish_kernel(where_ref, pattern_ref, index_ref, energy_ref, xm_ref, own_ref, peer_ref, sign_out, payload_ref, dens, sign_ref, sign_sem):
     yl, xi, yh, z, core = (where_ref[k] for k in range(5))
     block_row = (yl * 4 + xi) * RB
     block_col = ((yh * 4 + z) * 2 + core) * QB
@@ -227,6 +222,8 @@
         return carry
 
     lax.fori_loop(0, RB, finish, 0)
+    sign_copy = pltpu.make_async_copy(sign_ref, sign_out, sign_sem)
+    sign_copy.start()
     dens[BLOCKS] = jnp.zeros((BS, BS), jnp.bfloat16)
 
     line = lax.broadcasted_iota(jnp.int32, (TAIL, BS), 0)
@@ -241,6 +238,7 @@
         return carry
 
     lax.fori_loop(0, payload_ref.shape[0], copy, 0, unroll=4)
+    sign_copy.wait()
 
 
 def finish_and_payload(where, pattern, index, energy, xm, own, peer):
@@ -249,13 +247,15 @@
     return pl.pallas_call(
         finish_kernel,
         in_specs=[SMEM] * 3 + [VMEM] * 4,
-        out_specs=[VMEM, VMEM],
+        out_specs=[HBM, VMEM],
         out_shape=[
             jax.ShapeDtypeStruct((ROWS, COLS), jnp.bfloat16),
             jax.ShapeDtypeStruct(packet, jnp.bfloat16),
         ],
         scratch_shapes=[
             pltpu.VMEM((BLOCKS + 1, BS, BS), jnp.bfloat16),
+            pltpu.VMEM((ROWS, COLS), jnp.bfloat16),
+            pltpu.SemaphoreType.DMA,
         ],
         compiler_params=pltpu.CompilerParams(vmem_limit_bytes=18 * 2**20),
         cost_estimate=pl.CostEstimate(flops=4 * ROWS * COLS, bytes_accessed=15 * 2**20, transcendentals=0),
@@ -266,37 +266,50 @@
 FCH = 16
 
 
-def force_kernel(d_ref, h_ref, s_ref, out_ref):
+def force_kernel(d_ref, h_ref, s_ref, out_ref, part_ref):
     same = lax.broadcasted_iota(jnp.int32, (BS, BS), 0) == lax.broadcasted_iota(jnp.int32, (BS, BS), 1)
     ones = jnp.ones((BS, BS), jnp.bfloat16)
-    for source in range(FCH):
-        energies = d_ref[source, CAP * BS :, :].astype(jnp.float32)
-        for k in range(CAP):
-            slot = source * CAP + k
-            spread = jnp.where(same, energies[k : k + 1, :], 0.0).astype(jnp.bfloat16)
-            energy = jnp.dot(spread, ones, preferred_element_type=jnp.float32)
-            term = d_ref[source, k * BS : (k + 1) * BS, :].astype(jnp.float32) * (
-                h_ref[slot].astype(jnp.float32) - energy * s_ref[slot].astype(jnp.float32)
-            )
-            out_ref[slot : slot + 1, :] = jnp.sum(term, axis=0, keepdims=True)
+
+    def group(i, carry):
+        for j in range(FCH):
+            source = i * FCH + j
+            energies = d_ref[source, CAP * BS :, :].astype(jnp.float32)
+            for k in range(CAP):
+                slot = source * CAP + k
+                spread = jnp.where(same, energies[k : k + 1, :], 0.0).astype(jnp.bfloat16)
+                energy = jnp.dot(spread, ones, preferred_element_type=jnp.float32)
+                term = d_ref[source, k * BS : (k + 1) * BS, :].astype(jnp.float32) * (
+                    h_ref[slot].astype(jnp.float32) - energy * s_ref[slot].astype(jnp.float32)
+                )
+                row = j * CAP + k
+                part_ref[i, row : row + 1, :] = jnp.sum(term, axis=0, keepdims=True)
+        return carry
+
+    lax.fori_loop(0, part_ref.shape[0], group, 0)
+    parts = part_ref[...].reshape(out_ref.shape[0], BS)
+    out_ref[...] = lax.dot_general(
+        jnp.ones((8, BS), jnp.float32),
+        parts,
+        (((1,), (1,)), ((), ())),
+        precision=lax.Precision.HIGHEST,
+        preferred_element_type=jnp.float32,
+    )[0]
 
 
 def force_sums(packets, force_h, force_s):
     slots = force_h.shape[0]
-    block = pl.BlockSpec((FCH * CAP, BS, BS), lambda i: (i, 0, 0))
-    partial = pl.pallas_call(
+    return pl.pallas_call(
         force_kernel,
-        grid=(slots // (FCH * CAP),),
-        in_specs=[pl.BlockSpec((FCH, CAP * BS + TAIL, BS), lambda i: (i, 0, 0)), block, block],
-        out_specs=pl.BlockSpec((FCH * CAP, BS), lambda i: (i, 0)),
-        out_shape=jax.ShapeDtypeStruct((slots, BS), jnp.float32),
+        in_specs=[VMEM] * 3,
+        out_specs=VMEM,
+        out_shape=jax.ShapeDtypeStruct((slots,), jnp.float32),
+        scratch_shapes=[pltpu.VMEM((slots // (FCH * CAP), FCH * CAP, BS), jnp.float32)],
         compiler_params=pltpu.CompilerParams(vmem_limit_bytes=12 * 2**20),
         cost_estimate=pl.CostEstimate(
             flops=6 * slots * BS * BS, bytes_accessed=6 * slots * BS * BS, transcendentals=0
         ),
         name="force_sums",
     )(packets, force_h, force_s)
-    return jnp.sum(partial, axis=1)
 
 
 def exchange(payload):
@@ -349,8 +362,9 @@
     x_parts = [xm, xa_below, xa_above, *xa_far, xb_top, xb_bottom, xbt_below, xbb_below, xbt_above, xbb_above]
     y_parts = [ym, ya_below, ya_above, *ya_far, yb, yb_below, yb_above]
     own, far, x_late, y_late = early_product(x_parts, y_parts, where)
-    own, far = late_product(where, xb_far, yb_far, x_late, y_late, own, far)
+    far = late_product(1, where, xb_far, yb_far, x_late, y_late, far)
     peer = lax.ppermute(far, "c", SWAP)
+    own = late_product(0, where, xb_far, yb_far, x_late, y_late, after(own, far))
     sign_next, payload = finish_and_payload(where, pattern_product.T, index, energy, xm, own, peer)
     received = exchange(payload)
     return sign_next, force_sums(received, force_h, force_s)

time: 227 us -> 224 us (0.987)
    pallas_call x2 -> x3, Pallas kernels: 9.63 us -> 10.9 us  [the longest x1 6.73 us: force_sums(): pl.pallas_call(force_kernel, in_specs=[VMEM] * 3, out_specs=VMEM, out_sha...]
  transfers between devices with their start and end apart: 24 -> 24, of which waited for: 9 -> 9; matrix products, arithmetic and copies ran while one was open for 2% -> 2% of each run, Pallas kernels for 5% -> 6%
where the time goes in v6:
time: 224 us
  blocking collectives  114 us (51%)
  waiting for transfers between devices  42.9 us (19%)
  starting transfers between devices  34.9 us (16%)
  Pallas kernels  25.5 us (11%)
  local copies, waits for them, and re-layouts  5.38 us (2%)
    all_to_all x1, blocking collectives, exchange(): lax.all_to_all(payload, AXES, split_axis=0, concat_axis=0, tiled=True)  114 us
    pallas_call x1, Pallas kernels, early_product(): pl.pallas_call(early_kernel, in_specs=[HBM] * (len(X_PIECES) + len(Y_PIEC...  9.89 us
    ppermute x1, waiting for transfers between devices, shards(): xb_top = lax.ppermute(xm[:half], 'yh', SWAP)  9.66 us
    ppermute x1, waiting for transfers between devices, shards(): lax.ppermute(xb_bottom_z, 'z', UP)  8.98 us
    ppermute x1, waiting for transfers between devices, shards(): lax.ppermute(xa_below[:half], 'z', UP)  7.54 us
    pallas_call x1, Pallas kernels, force_sums(): pl.pallas_call(force_kernel, in_specs=[VMEM] * 3, out_specs=VMEM, out_sha...  6.73 us
    ppermute x1, waiting for transfers between devices, shards(): lax.ppermute(xb_top_z, 'z', UP)  6.27 us
    ppermute x1, waiting for transfers between devices, shards(): xa_below = lax.ppermute(xm, 'z', UP)  5.79 us
  transfers between devices with their start and end apart: 24, of which 9 were waited for; matrix products, arithmetic and copies ran while one was open for 2% of the time, Pallas kernels for 6%

profile of v6, /device:TPU:7, one launch (start us, length us, event | category | flops | bytes accessed | tf_op | source)
XLA Modules:
  0.0 224.1 jit_solution(12336571311505198136)
XLA Ops:
  4.1 1.7 collective-permute-start.1
  5.8 2.2 collective-permute-start.3
  9.3 2.9 %collective-permute-start = (bf16[512,512]{1,0:T(8,128)(2,1)}, bf16[512,512]{1,0:T(8,128)(2,1)}, u32[]{:S(2)}, u32[]{:S(2)}) collective-permute-start(bf16[512,512]{1,0:T(8,128)(2,1)} %get-tuple-element.29), channel_id=1, source_target_pairs={{0,8},{8,0},{1,9},{9,1},{2,10},{10,2},{3,11},{11,3},{4,12},{12,4},... | collective-permute-start | bytes 1572872 | tf_op jit(solution)/shard_map/ppermute | solution.py:338
  14.8 9.7 %collective-permute-done.refs_5_ = bf16[512,512]{1,0:T(8,128)(2,1)} collective-permute-done((bf16[512,512]{1,0:T(8,128)(2,1)}, bf16[512,512]{1,0:T(8,128)(2,1)}, u32[]{:S(2)}, u32[]{:S(2)}) %collective-permute-start) | collective-permute-done | bytes 524320 | tf_op jit(solution)/shard_map/ppermute | solution.py:338
  25.8 5.8 %collective-permute-done.1.refs_1_ = bf16[1024,512]{1,0:T(8,128)(2,1)} collective-permute-done((bf16[1024,512]{1,0:T(8,128)(2,1)S(1)}, bf16[1024,512]{1,0:T(8,128)(2,1)}, u32[]{:S(2)}, u32[]{:S(2)}) %collective-permute-start.1) | collective-permute-done | bytes 1048608 | tf_op jit(solution)/shard_map/ppermute | solution.py:339
  33.8 2.7 %collective-permute-start.4 = (bf16[512,512]{1,0:T(8,128)(2,1)S(1)}, bf16[512,512]{1,0:T(8,128)(2,1)S(1)}, u32[]{:S(2)}, u32[]{:S(2)}) collective-permute-start(bf16[512,512]{1,0:T(8,128)(2,1)S(1)} %slice.34), channel_id=1, source_target_pairs={{0,6},{2,0},{4,2},{6,4},{1,7},{3,1},{5,3},{7,5},{8,14},{10,8},{12,... | collective-permute-start | bytes 1572872 | tf_op jit(solution)/shard_map/ppermute | solution.py:346
  37.6 1.5 collective-permute-start.16
  39.3 7.5 %collective-permute-done.2.refs_3_ = bf16[512,512]{1,0:T(8,128)(2,1)S(1)} collective-permute-done((bf16[512,512]{1,0:T(8,128)(2,1)S(1)}, bf16[512,512]{1,0:T(8,128)(2,1)S(1)}, u32[]{:S(2)}, u32[]{:S(2)}) %collective-permute-start.2) | collective-permute-done | bytes 524320 | tf_op jit(solution)/shard_map/ppermute | solution.py:346
  47.0 3.3 %collective-permute-start.10 = (bf16[512,512]{1,0:T(8,128)(2,1)}, bf16[512,512]{1,0:T(8,128)(2,1)S(1)}, u32[]{:S(2)}, u32[]{:S(2)}) collective-permute-start(bf16[512,512]{1,0:T(8,128)(2,1)} %collective-permute-done.refs_5_), channel_id=1, source_target_pairs={{0,6},{2,0},{4,2},{6,4},{1,7},{3,1},{5,3},{7,5},{8,14},{10,8},{12,... | collective-permute-start | bytes 1572872 | tf_op jit(solution)/shard_map/ppermute | solution.py:350
  50.3 2.9 %collective-permute-start.9 = (bf16[512,512]{1,0:T(8,128)(2,1)S(1)}, bf16[512,512]{1,0:T(8,128)(2,1)S(1)}, u32[]{:S(2)}, u32[]{:S(2)}) collective-permute-start(bf16[512,512]{1,0:T(8,128)(2,1)S(1)} %copy-done.5), channel_id=1, source_target_pairs={{0,8},{8,0},{1,9},{9,1},{2,10},{10,2},{3,11},{11,3},{4,12},{12,4},... | collective-permute-start | bytes 1572872 | tf_op jit(solution)/shard_map/ppermute | solution.py:344
  54.7 6.3 %collective-permute-done.5.refs_7_ = bf16[512,512]{1,0:T(8,128)(2,1)S(1)} collective-permute-done((bf16[512,512]{1,0:T(8,128)(2,1)}, bf16[512,512]{1,0:T(8,128)(2,1)S(1)}, u32[]{:S(2)}, u32[]{:S(2)}) %collective-permute-start.5) | collective-permute-done | bytes 524320 | tf_op jit(solution)/shard_map/ppermute | solution.py:350
  61.0 2.2 collective-permute-done.9.refs_6_
  63.2 2.7 %collective-permute-start.13 = (bf16[512,512]{1,0:T(8,128)(2,1)S(1)}, bf16[512,512]{1,0:T(8,128)(2,1)S(1)}, u32[]{:S(2)}, u32[]{:S(2)}) collective-permute-start(bf16[512,512]{1,0:T(8,128)(2,1)S(1)} %collective-permute-done.9.refs_6_), channel_id=1, source_target_pairs={{0,6},{2,0},{4,2},{6,4},{1,7},{3,1},{5,3},{7,5},{8,14},{10,8},{12,... | collective-permute-start | bytes 1572872 | tf_op jit(solution)/shard_map/ppermute | solution.py:354
  65.9 9.0 %collective-permute-done.11.refs_8_ = bf16[512,512]{1,0:T(8,128)(2,1)S(1)} collective-permute-done((bf16[512,512]{1,0:T(8,128)(2,1)S(1)}, bf16[512,512]{1,0:T(8,128)(2,1)S(1)}, u32[]{:S(2)}, u32[]{:S(2)}) %collective-permute-start.11) | collective-permute-done | bytes 524320 | tf_op jit(solution)/shard_map/ppermute | solution.py:354
  74.9 2.7 %collective-permute-start.14 = (bf16[512,512]{1,0:T(8,128)(2,1)S(1)}, bf16[512,512]{1,0:T(8,128)(2,1)S(1)}, u32[]{:S(2)}, u32[]{:S(2)}) collective-permute-start(bf16[512,512]{1,0:T(8,128)(2,1)S(1)} %collective-permute-done.13.refs_10_), channel_id=1, source_target_pairs={{0,6},{2,0},{4,2},{6,4},{1,7},{3,1},{5,3},{7,5},{8,14},{10,8},{12,... | collective-permute-start | bytes 1572872 | tf_op jit(solution)/shard_map/ppermute | solution.py:358
  77.9 1.3 collective-permute-start.22
  79.2 9.9 %early_product.1 = (f32[1024,512]{1,0:T(8,128)S(1)}, f32[1024,512]{1,0:T(8,128)S(1)}, bf16[1024,512]{1,0:T(8,128)(2,1)S(1)}, bf16[512,1024]{1,0:T(8,128)(2,1)S(1)}) custom-call(bf16[1024,512]{1,0:T(8,128)(2,1)S(1)} %mask_x.1.refs_0_.xm_ref, bf16[1024,512]{1,0:T(8,128)(2,1)} %collective-permute-done.1.refs_1_, ...), custom_call_target="tpu_custom_call" | custom-call | flops 7516192768 | bytes 20971520 | tf_op jit(solution)/shard_map/early_product/pallas_call | solution.py:140
  89.2 2.1 late_product.2
  91.3 5.1 %collective-permute-start.23 = (f32[1024,512]{1,0:T(8,128)S(1)}, f32[1024,512]{1,0:T(8,128)S(1)}, u32[]{:S(2)}, u32[]{:S(2)}) collective-permute-start(f32[1024,512]{1,0:T(8,128)S(1)} %late_product.2), channel_id=1, source_target_pairs={{0,1},{1,0},{2,3},{3,2},{4,5},{5,4},{6,7},{7,6},{8,9},{9,8},{10,11... | collective-permute-start | bytes 6291464 | tf_op jit(solution)/shard_map/ppermute | solution.py:366
  96.8 2.1 late_product.3.own_ref
  98.8 1.3 collective-permute-done.23.peer_ref
  100.2 3.0 %finish_payload.1 = (bf16[1024,512]{1,0:T(8,128)(2,1)}, bf16[128,264,128]{2,1,0:T(8,128)(2,1)S(1)}) custom-call(s32[5]{0:T(128)S(1)} %stack.23.where_ref.refs_19_, s32[4,8]{1,0:T(4,128)S(1)} %bitcast.17, s32[256]{0:T(256)S(1)} %broadcast_add_fusion.index_ref, f32[9,1,128]{2,1,0:T(1,128)S(1)} %pad_convert_fusion.energy_ref, ...), custom_call_target="tpu_custom_call" | custom-call | flops 2097152 | bytes 15728640 | tf_op jit(solution)/shard_map/finish_payload/pallas_call | solution.py:247
  103.2 114.1 %all_to_all.5.d_ref = bf16[128,264,128]{2,1,0:T(8,128)(2,1)S(1)} all-to-all(bf16[128,264,128]{2,1,0:T(8,128)(2,1)S(1)} %get-tuple-element.27), channel_id=1, replica_groups=mesh['yl'=2,'x'=4,'yh'=2,'z'=4,'c'=2] {'yl','x','yh','z','c'}, dimensions={0} | all-to-all | bytes 17301504 | tf_op jit(solution)/shard_map/all_to_all | solution.py:316
  217.4 6.7 %force_sums.1 = f32[256]{0:T(256)} custom-call(bf16[128,264,128]{2,1,0:T(8,128)(2,1)S(1)} %all_to_all.5.d_ref, bf16[256,128,128]{2,1,0:T(8,128)(2,1)S(1)} %bitcast.14, bf16[256,128,128]{2,1,0:T(8,128)(2,1)S(1)} %bitcast.16), custom_call_target="tpu_custom_call" | custom-call | flops 25165824 | bytes 25165824 | tf_op jit(solution)/shard_map/force_sums/pallas_call | solution.py:301
  (75 shorter events, 14.5 us)
Async XLA Ops:
  0.6 11.7 %collective-permute-start.7 = (bf16[1024,512]{1,0:T(8,128)(2,1)}, bf16[1024,512]{1,0:T(8,128)(2,1)S(1)}, u32[]{:S(2)}, u32[]{:S(2)}) collective-permute-start(bf16[1024,512]{1,0:T(8,128)(2,1)} %y_ref.1), channel_id=1, source_target_pairs={{0,1},{1,0},{2,3},{3,2},{4,5},{5,4},{6,7},{7,6},{8,9},{9,8},{10,11... | collective-permute-start | bytes 3145736 | tf_op jit(solution)/shard_map/ppermute | solution.py:333
  4.1 27.5 %collective-permute-start.1 = (bf16[1024,512]{1,0:T(8,128)(2,1)S(1)}, bf16[1024,512]{1,0:T(8,128)(2,1)}, u32[]{:S(2)}, u32[]{:S(2)}) collective-permute-start(bf16[1024,512]{1,0:T(8,128)(2,1)S(1)} %mask_x.1.refs_0_.xm_ref), channel_id=1, source_target_pairs={{0,2},{2,4},{4,6},{6,0},{1,3},{3,5},{5,7},{7,1},{8,10},{10,12},{12... | collective-permute-start | bytes 3145736 | tf_op jit(solution)/shard_map/ppermute | solution.py:339
  5.8 26.9 %collective-permute-start.3 = (bf16[1024,512]{1,0:T(8,128)(2,1)S(1)}, bf16[1024,512]{1,0:T(8,128)(2,1)}, u32[]{:S(2)}, u32[]{:S(2)}) collective-permute-start(bf16[1024,512]{1,0:T(8,128)(2,1)S(1)} %mask_x.1.refs_0_.xm_ref), channel_id=1, source_target_pairs={{0,6},{2,0},{4,2},{6,4},{1,7},{3,1},{5,3},{7,5},{8,14},{10,8},{12,... | collective-permute-start | bytes 3145736 | tf_op jit(solution)/shard_map/ppermute | solution.py:340
  8.0 4.3 %collective-permute-start.6 = (s32[4,8]{1,0:T(4,128)S(1)}, s32[4,8]{1,0:T(4,128)S(1)}, u32[]{:S(2)}, u32[]{:S(2)}) collective-permute-start(s32[4,8]{1,0:T(4,128)S(1)} %bitcast.19), channel_id=1, source_target_pairs={{0,1},{1,0},{2,3},{3,2},{4,5},{5,4},{6,7},{7,6},{8,9},{9,8},{10,11... | collective-permute-start | bytes 392 | tf_op jit(solution)/shard_map/ppermute | solution.py:334
  9.3 15.1 %collective-permute-start = (bf16[512,512]{1,0:T(8,128)(2,1)}, bf16[512,512]{1,0:T(8,128)(2,1)}, u32[]{:S(2)}, u32[]{:S(2)}) collective-permute-start(bf16[512,512]{1,0:T(8,128)(2,1)} %get-tuple-element.29), channel_id=1, source_target_pairs={{0,8},{8,0},{1,9},{9,1},{2,10},{10,2},{3,11},{11,3},{4,12},{12,4},... | collective-permute-start | bytes 1572872 | tf_op jit(solution)/shard_map/ppermute | solution.py:338
  13.3 24.3 %collective-permute-start.15 = (bf16[512,1024]{1,0:T(8,128)(2,1)S(1)}, bf16[512,1024]{1,0:T(8,128)(2,1)S(1)}, u32[]{:S(2)}, u32[]{:S(2)}) collective-permute-start(bf16[512,1024]{1,0:T(8,128)(2,1)S(1)} %mask_y.1.refs_11_), channel_id=1, source_target_pairs={{0,16},{16,32},{32,48},{48,0},{1,17},{17,33},{33,49},{49,1},{2,18}... | collective-permute-start | bytes 3145736 | tf_op jit(solution)/shard_map/ppermute | solution.py:341
  13.5 25.6 %collective-permute-start.17 = (bf16[512,1024]{1,0:T(8,128)(2,1)S(1)}, bf16[512,1024]{1,0:T(8,128)(2,1)S(1)}, u32[]{:S(2)}, u32[]{:S(2)}) collective-permute-start(bf16[512,1024]{1,0:T(8,128)(2,1)S(1)} %mask_y.1.refs_11_), channel_id=1, source_target_pairs={{0,48},{16,0},{32,16},{48,32},{1,49},{17,1},{33,17},{49,33},{2,50}... | collective-permute-start | bytes 3145736 | tf_op jit(solution)/shard_map/ppermute | solution.py:342
  24.5 25.8 %collective-permute-start.8 = (bf16[512,1024]{1,0:T(8,128)(2,1)S(1)}, bf16[512,1024]{1,0:T(8,128)(2,1)S(1)}, u32[]{:S(2)}, u32[]{:S(2)}) collective-permute-start(bf16[512,1024]{1,0:T(8,128)(2,1)S(1)} %mask_y.1.refs_11_), channel_id=1, source_target_pairs={{0,64},{64,0},{1,65},{65,1},{2,66},{66,2},{3,67},{67,3},{4,68},{68... | collective-permute-start | bytes 3145736 | tf_op jit(solution)/shard_map/ppermute | solution.py:343
  32.6 14.2 %collective-permute-start.2 = (bf16[512,512]{1,0:T(8,128)(2,1)S(1)}, bf16[512,512]{1,0:T(8,128)(2,1)S(1)}, u32[]{:S(2)}, u32[]{:S(2)}) collective-permute-start(bf16[512,512]{1,0:T(8,128)(2,1)S(1)} %slice.33), channel_id=1, source_target_pairs={{0,2},{2,4},{4,6},{6,0},{1,3},{3,5},{5,7},{7,1},{8,10},{10,12},{12... | collective-permute-start | bytes 1572872 | tf_op jit(solution)/shard_map/ppermute | solution.py:346
  33.8 13.1 %collective-permute-start.4 = (bf16[512,512]{1,0:T(8,128)(2,1)S(1)}, bf16[512,512]{1,0:T(8,128)(2,1)S(1)}, u32[]{:S(2)}, u32[]{:S(2)}) collective-permute-start(bf16[512,512]{1,0:T(8,128)(2,1)S(1)} %slice.34), channel_id=1, source_target_pairs={{0,6},{2,0},{4,2},{6,4},{1,7},{3,1},{5,3},{7,5},{8,14},{10,8},{12,... | collective-permute-start | bytes 1572872 | tf_op jit(solution)/shard_map/ppermute | solution.py:346
  37.6 15.6 %collective-permute-start.16 = (bf16[256,1024]{1,0:T(8,128)(2,1)S(1)}, bf16[256,1024]{1,0:T(8,128)(2,1)S(1)}, u32[]{:S(2)}, u32[]{:S(2)}) collective-permute-start(bf16[256,1024]{1,0:T(8,128)(2,1)S(1)} %slice.36), channel_id=1, source_target_pairs={{0,16},{16,32},{32,48},{48,0},{1,17},{17,33},{33,49},{49,1},{2,18}... | collective-permute-start | bytes 1572872 | tf_op jit(solution)/shard_map/ppermute | solution.py:347
  39.1 14.1 %collective-permute-start.18 = (bf16[256,1024]{1,0:T(8,128)(2,1)S(1)}, bf16[256,1024]{1,0:T(8,128)(2,1)S(1)}, u32[]{:S(2)}, u32[]{:S(2)}) collective-permute-start(bf16[256,1024]{1,0:T(8,128)(2,1)S(1)} %slice.37), channel_id=1, source_target_pairs={{0,48},{16,0},{32,16},{48,32},{1,49},{17,1},{33,17},{49,33},{2,50}... | collective-permute-start | bytes 1572872 | tf_op jit(solution)/shard_map/ppermute | solution.py:347
  46.9 14.1 %collective-permute-start.5 = (bf16[512,512]{1,0:T(8,128)(2,1)}, bf16[512,512]{1,0:T(8,128)(2,1)S(1)}, u32[]{:S(2)}, u32[]{:S(2)}) collective-permute-start(bf16[512,512]{1,0:T(8,128)(2,1)} %collective-permute-done.refs_5_), channel_id=1, source_target_pairs={{0,2},{2,4},{4,6},{6,0},{1,3},{3,5},{5,7},{7,1},{8,10},{10,12},{12... | collective-permute-start | bytes 1572872 | tf_op jit(solution)/shard_map/ppermute | solution.py:350
  47.0 14.0 %collective-permute-start.10 = (bf16[512,512]{1,0:T(8,128)(2,1)}, bf16[512,512]{1,0:T(8,128)(2,1)S(1)}, u32[]{:S(2)}, u32[]{:S(2)}) collective-permute-start(bf16[512,512]{1,0:T(8,128)(2,1)} %collective-permute-done.refs_5_), channel_id=1, source_target_pairs={{0,6},{2,0},{4,2},{6,4},{1,7},{3,1},{5,3},{7,5},{8,14},{10,8},{12,... | collective-permute-start | bytes 1572872 | tf_op jit(solution)/shard_map/ppermute | solution.py:350
  50.3 12.9 %collective-permute-start.9 = (bf16[512,512]{1,0:T(8,128)(2,1)S(1)}, bf16[512,512]{1,0:T(8,128)(2,1)S(1)}, u32[]{:S(2)}, u32[]{:S(2)}) collective-permute-start(bf16[512,512]{1,0:T(8,128)(2,1)S(1)} %copy-done.5), channel_id=1, source_target_pairs={{0,8},{8,0},{1,9},{9,1},{2,10},{10,2},{3,11},{11,3},{4,12},{12,4},... | collective-permute-start | bytes 1572872 | tf_op jit(solution)/shard_map/ppermute | solution.py:344
  53.2 24.3 %collective-permute-start.19 = (bf16[512,1024]{1,0:T(8,128)(2,1)S(1)}, bf16[512,1024]{1,0:T(8,128)(2,1)S(1)}, u32[]{:S(2)}, u32[]{:S(2)}) collective-permute-start(bf16[512,1024]{1,0:T(8,128)(2,1)S(1)} %collective-permute-done.8.refs_16_), channel_id=1, source_target_pairs={{0,16},{16,32},{32,48},{48,0},{1,17},{17,33},{33,49},{49,1},{2,18}... | collective-permute-start | bytes 3145736 | tf_op jit(solution)/shard_map/ppermute | solution.py:352
  53.4 24.4 %collective-permute-start.21 = (bf16[512,1024]{1,0:T(8,128)(2,1)S(1)}, bf16[512,1024]{1,0:T(8,128)(2,1)S(1)}, u32[]{:S(2)}, u32[]{:S(2)}) collective-permute-start(bf16[512,1024]{1,0:T(8,128)(2,1)S(1)} %collective-permute-done.8.refs_16_), channel_id=1, source_target_pairs={{0,48},{16,0},{32,16},{48,32},{1,49},{17,1},{33,17},{49,33},{2,50}... | collective-permute-start | bytes 3145736 | tf_op jit(solution)/shard_map/ppermute | solution.py:352
  63.2 11.7 %collective-permute-start.11 = (bf16[512,512]{1,0:T(8,128)(2,1)S(1)}, bf16[512,512]{1,0:T(8,128)(2,1)S(1)}, u32[]{:S(2)}, u32[]{:S(2)}) collective-permute-start(bf16[512,512]{1,0:T(8,128)(2,1)S(1)} %collective-permute-done.9.refs_6_), channel_id=1, source_target_pairs={{0,2},{2,4},{4,6},{6,0},{1,3},{3,5},{5,7},{7,1},{8,10},{10,12},{12... | collective-permute-start | bytes 1572872 | tf_op jit(solution)/shard_map/ppermute | solution.py:354
  63.2 11.7 %collective-permute-start.13 = (bf16[512,512]{1,0:T(8,128)(2,1)S(1)}, bf16[512,512]{1,0:T(8,128)(2,1)S(1)}, u32[]{:S(2)}, u32[]{:S(2)}) collective-permute-start(bf16[512,512]{1,0:T(8,128)(2,1)S(1)} %collective-permute-done.9.refs_6_), channel_id=1, source_target_pairs={{0,6},{2,0},{4,2},{6,4},{1,7},{3,1},{5,3},{7,5},{8,14},{10,8},{12,... | collective-permute-start | bytes 1572872 | tf_op jit(solution)/shard_map/ppermute | solution.py:354
  74.8 14.3 %collective-permute-start.12 = (bf16[512,512]{1,0:T(8,128)(2,1)S(1)}, bf16[512,512]{1,0:T(8,128)(2,1)S(1)}, u32[]{:S(2)}, u32[]{:S(2)}) collective-permute-start(bf16[512,512]{1,0:T(8,128)(2,1)S(1)} %collective-permute-done.5.refs_7_), channel_id=1, source_target_pairs={{0,2},{2,4},{4,6},{6,0},{1,3},{3,5},{5,7},{7,1},{8,10},{10,12},{12... | collective-permute-start | bytes 1572872 | tf_op jit(solution)/shard_map/ppermute | solution.py:357
  74.9 14.3 %collective-permute-start.14 = (bf16[512,512]{1,0:T(8,128)(2,1)S(1)}, bf16[512,512]{1,0:T(8,128)(2,1)S(1)}, u32[]{:S(2)}, u32[]{:S(2)}) collective-permute-start(bf16[512,512]{1,0:T(8,128)(2,1)S(1)} %collective-permute-done.13.refs_10_), channel_id=1, source_target_pairs={{0,6},{2,0},{4,2},{6,4},{1,7},{3,1},{5,3},{7,5},{8,14},{10,8},{12,... | collective-permute-start | bytes 1572872 | tf_op jit(solution)/shard_map/ppermute | solution.py:358
  77.6 11.6 %collective-permute-start.20 = (bf16[256,1024]{1,0:T(8,128)(2,1)S(1)}, bf16[256,1024]{1,0:T(8,128)(2,1)S(1)}, u32[]{:S(2)}, u32[]{:S(2)}) collective-permute-start(bf16[256,1024]{1,0:T(8,128)(2,1)S(1)} %slice.38), channel_id=1, source_target_pairs={{0,16},{16,32},{32,48},{48,0},{1,17},{17,33},{33,49},{49,1},{2,18}... | collective-permute-start | bytes 1572872 | tf_op jit(solution)/shard_map/ppermute | solution.py:360
  77.9 11.3 %collective-permute-start.22 = (bf16[256,1024]{1,0:T(8,128)(2,1)S(1)}, bf16[256,1024]{1,0:T(8,128)(2,1)S(1)}, u32[]{:S(2)}, u32[]{:S(2)}) collective-permute-start(bf16[256,1024]{1,0:T(8,128)(2,1)S(1)} %slice.39), channel_id=1, source_target_pairs={{0,48},{16,0},{32,16},{48,32},{1,49},{17,1},{33,17},{49,33},{2,50}... | collective-permute-start | bytes 1572872 | tf_op jit(solution)/shard_map/ppermute | solution.py:360
  91.3 8.9 %collective-permute-start.23 = (f32[1024,512]{1,0:T(8,128)S(1)}, f32[1024,512]{1,0:T(8,128)S(1)}, u32[]{:S(2)}, u32[]{:S(2)}) collective-permute-start(f32[1024,512]{1,0:T(8,128)S(1)} %late_product.2), channel_id=1, source_target_pairs={{0,1},{1,0},{2,3},{3,2},{4,5},{5,4},{6,7},{7,6},{8,9},{9,8},{10,11... | collective-permute-start | bytes 6291464 | tf_op jit(solution)/shard_map/ppermute | solution.py:366
  (13 other events, 544.1 us)

commit v7 on v6

--- a/solution.py
+++ b/solution.py
@@ -268,7 +268,7 @@
 
 def force_kernel(d_ref, h_ref, s_ref, out_ref, part_ref):
     same = lax.broadcasted_iota(jnp.int32, (BS, BS), 0) == lax.broadcasted_iota(jnp.int32, (BS, BS), 1)
-    ones = jnp.ones((BS, BS), jnp.bfloat16)
+    eye = jnp.where(same, 1.0, 0.0).astype(jnp.bfloat16)
 
     def group(i, carry):
         for j in range(FCH):
@@ -276,10 +276,10 @@
             energies = d_ref[source, CAP * BS :, :].astype(jnp.float32)
             for k in range(CAP):
                 slot = source * CAP + k
-                spread = jnp.where(same, energies[k : k + 1, :], 0.0).astype(jnp.bfloat16)
-                energy = jnp.dot(spread, ones, preferred_element_type=jnp.float32)
+                spread = eye * energies[k : k + 1, :].astype(jnp.bfloat16)
+                scaled = jnp.dot(spread, s_ref[slot], preferred_element_type=jnp.float32)
                 term = d_ref[source, k * BS : (k + 1) * BS, :].astype(jnp.float32) * (
-                    h_ref[slot].astype(jnp.float32) - energy * s_ref[slot].astype(jnp.float32)
+                    h_ref[slot].astype(jnp.float32) - scaled
                 )
                 row = j * CAP + k
                 part_ref[i, row : row + 1, :] = jnp.sum(term, axis=0, keepdims=True)
@@ -335,9 +335,10 @@
     xm = mask_x(pattern_x.T, x)
     ym = mask_y(where, pattern_y.T, pattern_peer, y, y_peer)
 
-    xb_top = lax.ppermute(xm[:half], "yh", SWAP)
-    xa_below = lax.ppermute(xm, "z", UP)
-    xa_above = lax.ppermute(xm, "z", DOWN)
+    xm_z = after(xm, ym)
+    xb_top = lax.ppermute(xm_z[:half], "yh", SWAP)
+    xa_below = lax.ppermute(xm_z, "z", UP)
+    xa_above = lax.ppermute(xm_z, "z", DOWN)
     ya_below = lax.ppermute(ym, "x", UP)
     ya_above = lax.ppermute(ym, "x", DOWN)
     yb = lax.ppermute(after(ym, xb_top), "yl", SWAP)

time: 224 us -> 221 us (0.987)
  waiting for transfers between devices: 42.9 us -> 45.7 us
  local copies, waits for them, and re-layouts: 5.38 us -> 2.72 us
  transfers between devices with their start and end apart: 24 -> 24, of which waited for: 9 -> 9; matrix products, arithmetic and copies ran while one was open for 2% -> 0% of each run, Pallas kernels for 6% -> 6%
where the time goes in v7:
time: 221 us
  blocking collectives  114 us (52%)
  waiting for transfers between devices  45.7 us (21%)
  starting transfers between devices  33.3 us (15%)
  Pallas kernels  24.1 us (11%)
  local copies, waits for them, and re-layouts  2.72 us (1%)
    all_to_all x1, blocking collectives, exchange(): lax.all_to_all(payload, AXES, split_axis=0, concat_axis=0, tiled=True)  114 us
    pallas_call x1, Pallas kernels, early_product(): pl.pallas_call(early_kernel, in_specs=[HBM] * (len(X_PIECES) + len(Y_PIEC...  10.1 us
    ppermute x1, waiting for transfers between devices, shards(): xb_top = lax.ppermute(xm_z[:half], 'yh', SWAP)  9.89 us
    ppermute x1, waiting for transfers between devices, shards(): lax.ppermute(xb_bottom_z, 'z', UP)  8.63 us
    ppermute x1, waiting for transfers between devices, shards(): lax.ppermute(xa_below[:half], 'z', UP)  8.48 us
    ppermute x1, waiting for transfers between devices, shards(): xa_below = lax.ppermute(xm_z, 'z', UP)  7.42 us
    ppermute x1, waiting for transfers between devices, shards(): lax.ppermute(xb_top_z, 'z', UP)  5.71 us
    ppermute x1, starting transfers between devices, shards(): peer = lax.ppermute(far, 'c', SWAP)  5.45 us
  transfers between devices with their start and end apart: 24, of which 9 were waited for; matrix products, arithmetic and copies ran while one was open for 0% of the time, Pallas kernels for 6%

profile of v7, /device:TPU:7, one launch (start us, length us, event | category | flops | bytes accessed | tf_op | source)
XLA Modules:
  0.0 221.0 jit_solution(9447409421535056740)
XLA Ops:
  5.6 1.7 collective-permute-start.3
  7.3 2.2 collective-permute-start.5
  9.6 3.0 %collective-permute-start.2 = (bf16[512,512]{1,0:T(8,128)(2,1)S(1)}, bf16[512,512]{1,0:T(8,128)(2,1)S(1)}, u32[]{:S(2)}, u32[]{:S(2)}) collective-permute-start(bf16[512,512]{1,0:T(8,128)(2,1)S(1)} %slice.24), channel_id=1, source_target_pairs={{0,8},{8,0},{1,9},{9,1},{2,10},{10,2},{3,11},{11,3},{4,12},{12,4},... | collective-permute-start | bytes 1572872 | tf_op jit(solution)/shard_map/ppermute | solution.py:339
  14.0 9.9 %collective-permute-done.2.refs_5_ = bf16[512,512]{1,0:T(8,128)(2,1)S(1)} collective-permute-done((bf16[512,512]{1,0:T(8,128)(2,1)S(1)}, bf16[512,512]{1,0:T(8,128)(2,1)S(1)}, u32[]{:S(2)}, u32[]{:S(2)}) %collective-permute-start.2) | collective-permute-done | bytes 524320 | tf_op jit(solution)/shard_map/ppermute | solution.py:339
  25.2 7.4 %collective-permute-done.3.refs_1_ = bf16[1024,512]{1,0:T(8,128)(2,1)S(1)} collective-permute-done((bf16[1024,512]{1,0:T(8,128)(2,1)S(1)}, bf16[1024,512]{1,0:T(8,128)(2,1)S(1)}, u32[]{:S(2)}, u32[]{:S(2)}) %collective-permute-start.3) | collective-permute-done | bytes 1048608 | tf_op jit(solution)/shard_map/ppermute | solution.py:340
  32.8 2.7 %collective-permute-start.6 = (bf16[512,512]{1,0:T(8,128)(2,1)S(1)}, bf16[512,512]{1,0:T(8,128)(2,1)S(1)}, u32[]{:S(2)}, u32[]{:S(2)}) collective-permute-start(bf16[512,512]{1,0:T(8,128)(2,1)S(1)} %slice.33), channel_id=1, source_target_pairs={{0,6},{2,0},{4,2},{6,4},{1,7},{3,1},{5,3},{7,5},{8,14},{10,8},{12,... | collective-permute-start | bytes 1572872 | tf_op jit(solution)/shard_map/ppermute | solution.py:347
  36.3 1.5 collective-permute-start.16
  38.0 8.5 %collective-permute-done.4.refs_3_ = bf16[512,512]{1,0:T(8,128)(2,1)S(1)} collective-permute-done((bf16[512,512]{1,0:T(8,128)(2,1)S(1)}, bf16[512,512]{1,0:T(8,128)(2,1)S(1)}, u32[]{:S(2)}, u32[]{:S(2)}) %collective-permute-start.4) | collective-permute-done | bytes 524320 | tf_op jit(solution)/shard_map/ppermute | solution.py:347
  46.4 2.7 %collective-permute-start.10 = (bf16[512,512]{1,0:T(8,128)(2,1)S(1)}, bf16[512,512]{1,0:T(8,128)(2,1)S(1)}, u32[]{:S(2)}, u32[]{:S(2)}) collective-permute-start(bf16[512,512]{1,0:T(8,128)(2,1)S(1)} %collective-permute-done.2.refs_5_), channel_id=1, source_target_pairs={{0,6},{2,0},{4,2},{6,4},{1,7},{3,1},{5,3},{7,5},{8,14},{10,8},{12,... | collective-permute-start | bytes 1572872 | tf_op jit(solution)/shard_map/ppermute | solution.py:351
  49.1 2.9 %collective-permute-start.9 = (bf16[512,512]{1,0:T(8,128)(2,1)S(1)}, bf16[512,512]{1,0:T(8,128)(2,1)S(1)}, u32[]{:S(2)}, u32[]{:S(2)}) collective-permute-start(bf16[512,512]{1,0:T(8,128)(2,1)S(1)} %slice.34), channel_id=1, source_target_pairs={{0,8},{8,0},{1,9},{9,1},{2,10},{10,2},{3,11},{11,3},{4,12},{12,4},... | collective-permute-start | bytes 1572872 | tf_op jit(solution)/shard_map/ppermute | solution.py:345
  53.5 5.7 %collective-permute-done.7.refs_7_ = bf16[512,512]{1,0:T(8,128)(2,1)S(1)} collective-permute-done((bf16[512,512]{1,0:T(8,128)(2,1)S(1)}, bf16[512,512]{1,0:T(8,128)(2,1)S(1)}, u32[]{:S(2)}, u32[]{:S(2)}) %collective-permute-start.7) | collective-permute-done | bytes 524320 | tf_op jit(solution)/shard_map/ppermute | solution.py:351
  59.2 2.4 %collective-permute-done.9.refs_6_ = bf16[512,512]{1,0:T(8,128)(2,1)S(1)} collective-permute-done((bf16[512,512]{1,0:T(8,128)(2,1)S(1)}, bf16[512,512]{1,0:T(8,128)(2,1)S(1)}, u32[]{:S(2)}, u32[]{:S(2)}) %collective-permute-start.9) | collective-permute-done | bytes 524320 | tf_op jit(solution)/shard_map/ppermute | solution.py:345
  61.6 2.7 %collective-permute-start.13 = (bf16[512,512]{1,0:T(8,128)(2,1)S(1)}, bf16[512,512]{1,0:T(8,128)(2,1)S(1)}, u32[]{:S(2)}, u32[]{:S(2)}) collective-permute-start(bf16[512,512]{1,0:T(8,128)(2,1)S(1)} %collective-permute-done.9.refs_6_), channel_id=1, source_target_pairs={{0,6},{2,0},{4,2},{6,4},{1,7},{3,1},{5,3},{7,5},{8,14},{10,8},{12,... | collective-permute-start | bytes 1572872 | tf_op jit(solution)/shard_map/ppermute | solution.py:355
  64.3 8.6 %collective-permute-done.11.refs_8_ = bf16[512,512]{1,0:T(8,128)(2,1)S(1)} collective-permute-done((bf16[512,512]{1,0:T(8,128)(2,1)S(1)}, bf16[512,512]{1,0:T(8,128)(2,1)S(1)}, u32[]{:S(2)}, u32[]{:S(2)}) %collective-permute-start.11) | collective-permute-done | bytes 524320 | tf_op jit(solution)/shard_map/ppermute | solution.py:355
  74.1 1.5 collective-permute-start.20
  75.7 1.6 collective-permute-start.14
  77.3 10.1 %early_product.1 = (f32[1024,512]{1,0:T(8,128)S(1)}, f32[1024,512]{1,0:T(8,128)S(1)}, bf16[1024,512]{1,0:T(8,128)(2,1)S(1)}, bf16[512,1024]{1,0:T(8,128)(2,1)S(1)}) custom-call(bf16[1024,512]{1,0:T(8,128)(2,1)S(1)} %mask_x.1.refs_0_.xm_ref, bf16[1024,512]{1,0:T(8,128)(2,1)S(1)} %collective-permute-done.3.refs_1_, ...), custom_call_target="tpu_custom_call" | custom-call | flops 7516192768 | bytes 20971520 | tf_op jit(solution)/shard_map/early_product/pallas_call | solution.py:140
  87.5 2.1 late_product.2
  89.6 5.5 %collective-permute-start.23 = (f32[1024,512]{1,0:T(8,128)S(1)}, f32[1024,512]{1,0:T(8,128)S(1)}, u32[]{:S(2)}, u32[]{:S(2)}) collective-permute-start(f32[1024,512]{1,0:T(8,128)S(1)} %late_product.2), channel_id=1, source_target_pairs={{0,1},{1,0},{2,3},{3,2},{4,5},{5,4},{6,7},{7,6},{8,9},{9,8},{10,11... | collective-permute-start | bytes 6291464 | tf_op jit(solution)/shard_map/ppermute | solution.py:367
  95.4 2.1 late_product.3.own_ref
  97.5 1.3 collective-permute-done.23.peer_ref
  98.8 3.0 %finish_payload.1 = (bf16[1024,512]{1,0:T(8,128)(2,1)}, bf16[128,264,128]{2,1,0:T(8,128)(2,1)S(1)}) custom-call(s32[5]{0:T(128)S(1)} %stack.23.where_ref.refs_19_, s32[4,8]{1,0:T(4,128)S(1)} %bitcast.17, s32[256]{0:T(256)S(1)} %broadcast_add_fusion.index_ref, f32[9,1,128]{2,1,0:T(1,128)S(1)} %pad_convert_fusion.energy_ref, ...), custom_call_target="tpu_custom_call" | custom-call | flops 2097152 | bytes 15728640 | tf_op jit(solution)/shard_map/finish_payload/pallas_call | solution.py:247
  101.8 114.0 %all_to_all.5.d_ref = bf16[128,264,128]{2,1,0:T(8,128)(2,1)S(1)} all-to-all(bf16[128,264,128]{2,1,0:T(8,128)(2,1)S(1)} %get-tuple-element.29), channel_id=1, replica_groups=mesh['yl'=2,'x'=4,'yh'=2,'z'=4,'c'=2] {'yl','x','yh','z','c'}, dimensions={0} | all-to-all | bytes 17301504 | tf_op jit(solution)/shard_map/all_to_all | solution.py:316
  215.8 5.2 %force_sums.1 = f32[256]{0:T(256)} custom-call(bf16[128,264,128]{2,1,0:T(8,128)(2,1)S(1)} %all_to_all.5.d_ref, bf16[256,128,128]{2,1,0:T(8,128)(2,1)S(1)} %bitcast.14, bf16[256,128,128]{2,1,0:T(8,128)(2,1)S(1)} %bitcast.16), custom_call_target="tpu_custom_call" | custom-call | flops 25165824 | bytes 25165824 | tf_op jit(solution)/shard_map/force_sums/pallas_call | solution.py:301
  (74 shorter events, 12.0 us)
Async XLA Ops:
  0.6 3.7 %collective-permute-start.1 = (bf16[1024,512]{1,0:T(8,128)(2,1)}, bf16[1024,512]{1,0:T(8,128)(2,1)S(1)}, u32[]{:S(2)}, u32[]{:S(2)}) collective-permute-start(bf16[1024,512]{1,0:T(8,128)(2,1)} %y_ref.1), channel_id=1, source_target_pairs={{0,1},{1,0},{2,3},{3,2},{4,5},{5,4},{6,7},{7,6},{8,9},{9,8},{10,11... | collective-permute-start | bytes 3145736 | tf_op jit(solution)/shard_map/ppermute | solution.py:333
  1.4 2.9 %collective-permute-start = (s32[4,8]{1,0:T(4,128)}, s32[4,8]{1,0:T(4,128)S(1)}, u32[]{:S(2)}, u32[]{:S(2)}) collective-permute-start(s32[4,8]{1,0:T(4,128)} %bitcast.19), channel_id=1, source_target_pairs={{0,1},{1,0},{2,3},{3,2},{4,5},{5,4},{6,7},{7,6},{8,9},{9,8},{10,11... | collective-permute-start | bytes 392 | tf_op jit(solution)/shard_map/ppermute | solution.py:334
  5.6 27.0 %collective-permute-start.3 = (bf16[1024,512]{1,0:T(8,128)(2,1)S(1)}, bf16[1024,512]{1,0:T(8,128)(2,1)S(1)}, u32[]{:S(2)}, u32[]{:S(2)}) collective-permute-start(bf16[1024,512]{1,0:T(8,128)(2,1)S(1)} %mask_x.1.refs_0_.xm_ref), channel_id=1, source_target_pairs={{0,2},{2,4},{4,6},{6,0},{1,3},{3,5},{5,7},{7,1},{8,10},{10,12},{12... | collective-permute-start | bytes 3145736 | tf_op jit(solution)/shard_map/ppermute | solution.py:340
  7.3 25.4 %collective-permute-start.5 = (bf16[1024,512]{1,0:T(8,128)(2,1)S(1)}, bf16[1024,512]{1,0:T(8,128)(2,1)S(1)}, u32[]{:S(2)}, u32[]{:S(2)}) collective-permute-start(bf16[1024,512]{1,0:T(8,128)(2,1)S(1)} %mask_x.1.refs_0_.xm_ref), channel_id=1, source_target_pairs={{0,6},{2,0},{4,2},{6,4},{1,7},{3,1},{5,3},{7,5},{8,14},{10,8},{12,... | collective-permute-start | bytes 3145736 | tf_op jit(solution)/shard_map/ppermute | solution.py:341
  9.6 14.3 %collective-permute-start.2 = (bf16[512,512]{1,0:T(8,128)(2,1)S(1)}, bf16[512,512]{1,0:T(8,128)(2,1)S(1)}, u32[]{:S(2)}, u32[]{:S(2)}) collective-permute-start(bf16[512,512]{1,0:T(8,128)(2,1)S(1)} %slice.24), channel_id=1, source_target_pairs={{0,8},{8,0},{1,9},{9,1},{2,10},{10,2},{3,11},{11,3},{4,12},{12,4},... | collective-permute-start | bytes 1572872 | tf_op jit(solution)/shard_map/ppermute | solution.py:339
  12.6 23.7 %collective-permute-start.15 = (bf16[512,1024]{1,0:T(8,128)(2,1)S(1)}, bf16[512,1024]{1,0:T(8,128)(2,1)S(1)}, u32[]{:S(2)}, u32[]{:S(2)}) collective-permute-start(bf16[512,1024]{1,0:T(8,128)(2,1)S(1)} %mask_y.1.refs_11_), channel_id=1, source_target_pairs={{0,16},{16,32},{32,48},{48,0},{1,17},{17,33},{33,49},{49,1},{2,18}... | collective-permute-start | bytes 3145736 | tf_op jit(solution)/shard_map/ppermute | solution.py:342
  12.8 25.0 %collective-permute-start.17 = (bf16[512,1024]{1,0:T(8,128)(2,1)S(1)}, bf16[512,1024]{1,0:T(8,128)(2,1)S(1)}, u32[]{:S(2)}, u32[]{:S(2)}) collective-permute-start(bf16[512,1024]{1,0:T(8,128)(2,1)S(1)} %mask_y.1.refs_11_), channel_id=1, source_target_pairs={{0,48},{16,0},{32,16},{48,32},{1,49},{17,1},{33,17},{49,33},{2,50}... | collective-permute-start | bytes 3145736 | tf_op jit(solution)/shard_map/ppermute | solution.py:343
  23.9 25.2 %collective-permute-start.8 = (bf16[512,1024]{1,0:T(8,128)(2,1)S(1)}, bf16[512,1024]{1,0:T(8,128)(2,1)S(1)}, u32[]{:S(2)}, u32[]{:S(2)}) collective-permute-start(bf16[512,1024]{1,0:T(8,128)(2,1)S(1)} %mask_y.1.refs_11_), channel_id=1, source_target_pairs={{0,64},{64,0},{1,65},{65,1},{2,66},{66,2},{3,67},{67,3},{4,68},{68... | collective-permute-start | bytes 3145736 | tf_op jit(solution)/shard_map/ppermute | solution.py:344
  32.7 13.8 %collective-permute-start.4 = (bf16[512,512]{1,0:T(8,128)(2,1)S(1)}, bf16[512,512]{1,0:T(8,128)(2,1)S(1)}, u32[]{:S(2)}, u32[]{:S(2)}) collective-permute-start(bf16[512,512]{1,0:T(8,128)(2,1)S(1)} %slice.32), channel_id=1, source_target_pairs={{0,2},{2,4},{4,6},{6,0},{1,3},{3,5},{5,7},{7,1},{8,10},{10,12},{12... | collective-permute-start | bytes 1572872 | tf_op jit(solution)/shard_map/ppermute | solution.py:347
  32.8 13.6 %collective-permute-start.6 = (bf16[512,512]{1,0:T(8,128)(2,1)S(1)}, bf16[512,512]{1,0:T(8,128)(2,1)S(1)}, u32[]{:S(2)}, u32[]{:S(2)}) collective-permute-start(bf16[512,512]{1,0:T(8,128)(2,1)S(1)} %slice.33), channel_id=1, source_target_pairs={{0,6},{2,0},{4,2},{6,4},{1,7},{3,1},{5,3},{7,5},{8,14},{10,8},{12,... | collective-permute-start | bytes 1572872 | tf_op jit(solution)/shard_map/ppermute | solution.py:347
  36.3 15.8 %collective-permute-start.16 = (bf16[256,1024]{1,0:T(8,128)(2,1)S(1)}, bf16[256,1024]{1,0:T(8,128)(2,1)S(1)}, u32[]{:S(2)}, u32[]{:S(2)}) collective-permute-start(bf16[256,1024]{1,0:T(8,128)(2,1)S(1)} %slice.35), channel_id=1, source_target_pairs={{0,16},{16,32},{32,48},{48,0},{1,17},{17,33},{33,49},{49,1},{2,18}... | collective-permute-start | bytes 1572872 | tf_op jit(solution)/shard_map/ppermute | solution.py:348
  37.8 14.2 %collective-permute-start.18 = (bf16[256,1024]{1,0:T(8,128)(2,1)S(1)}, bf16[256,1024]{1,0:T(8,128)(2,1)S(1)}, u32[]{:S(2)}, u32[]{:S(2)}) collective-permute-start(bf16[256,1024]{1,0:T(8,128)(2,1)S(1)} %slice.36), channel_id=1, source_target_pairs={{0,48},{16,0},{32,16},{48,32},{1,49},{17,1},{33,17},{49,33},{2,50}... | collective-permute-start | bytes 1572872 | tf_op jit(solution)/shard_map/ppermute | solution.py:348
  46.4 12.8 %collective-permute-start.7 = (bf16[512,512]{1,0:T(8,128)(2,1)S(1)}, bf16[512,512]{1,0:T(8,128)(2,1)S(1)}, u32[]{:S(2)}, u32[]{:S(2)}) collective-permute-start(bf16[512,512]{1,0:T(8,128)(2,1)S(1)} %collective-permute-done.2.refs_5_), channel_id=1, source_target_pairs={{0,2},{2,4},{4,6},{6,0},{1,3},{3,5},{5,7},{7,1},{8,10},{10,12},{12... | collective-permute-start | bytes 1572872 | tf_op jit(solution)/shard_map/ppermute | solution.py:351
  46.4 12.8 %collective-permute-start.10 = (bf16[512,512]{1,0:T(8,128)(2,1)S(1)}, bf16[512,512]{1,0:T(8,128)(2,1)S(1)}, u32[]{:S(2)}, u32[]{:S(2)}) collective-permute-start(bf16[512,512]{1,0:T(8,128)(2,1)S(1)} %collective-permute-done.2.refs_5_), channel_id=1, source_target_pairs={{0,6},{2,0},{4,2},{6,4},{1,7},{3,1},{5,3},{7,5},{8,14},{10,8},{12,... | collective-permute-start | bytes 1572872 | tf_op jit(solution)/shard_map/ppermute | solution.py:351
  49.1 12.5 %collective-permute-start.9 = (bf16[512,512]{1,0:T(8,128)(2,1)S(1)}, bf16[512,512]{1,0:T(8,128)(2,1)S(1)}, u32[]{:S(2)}, u32[]{:S(2)}) collective-permute-start(bf16[512,512]{1,0:T(8,128)(2,1)S(1)} %slice.34), channel_id=1, source_target_pairs={{0,8},{8,0},{1,9},{9,1},{2,10},{10,2},{3,11},{11,3},{4,12},{12,4},... | collective-permute-start | bytes 1572872 | tf_op jit(solution)/shard_map/ppermute | solution.py:345
  52.0 22.0 %collective-permute-start.19 = (bf16[512,1024]{1,0:T(8,128)(2,1)S(1)}, bf16[512,1024]{1,0:T(8,128)(2,1)S(1)}, u32[]{:S(2)}, u32[]{:S(2)}) collective-permute-start(bf16[512,1024]{1,0:T(8,128)(2,1)S(1)} %collective-permute-done.8.refs_16_), channel_id=1, source_target_pairs={{0,16},{16,32},{32,48},{48,0},{1,17},{17,33},{33,49},{49,1},{2,18}... | collective-permute-start | bytes 3145736 | tf_op jit(solution)/shard_map/ppermute | solution.py:353
  52.2 23.3 %collective-permute-start.21 = (bf16[512,1024]{1,0:T(8,128)(2,1)S(1)}, bf16[512,1024]{1,0:T(8,128)(2,1)S(1)}, u32[]{:S(2)}, u32[]{:S(2)}) collective-permute-start(bf16[512,1024]{1,0:T(8,128)(2,1)S(1)} %collective-permute-done.8.refs_16_), channel_id=1, source_target_pairs={{0,48},{16,0},{32,16},{48,32},{1,49},{17,1},{33,17},{49,33},{2,50}... | collective-permute-start | bytes 3145736 | tf_op jit(solution)/shard_map/ppermute | solution.py:353
  61.6 11.3 %collective-permute-start.11 = (bf16[512,512]{1,0:T(8,128)(2,1)S(1)}, bf16[512,512]{1,0:T(8,128)(2,1)S(1)}, u32[]{:S(2)}, u32[]{:S(2)}) collective-permute-start(bf16[512,512]{1,0:T(8,128)(2,1)S(1)} %collective-permute-done.9.refs_6_), channel_id=1, source_target_pairs={{0,2},{2,4},{4,6},{6,0},{1,3},{3,5},{5,7},{7,1},{8,10},{10,12},{12... | collective-permute-start | bytes 1572872 | tf_op jit(solution)/shard_map/ppermute | solution.py:355
  61.6 14.1 %collective-permute-start.13 = (bf16[512,512]{1,0:T(8,128)(2,1)S(1)}, bf16[512,512]{1,0:T(8,128)(2,1)S(1)}, u32[]{:S(2)}, u32[]{:S(2)}) collective-permute-start(bf16[512,512]{1,0:T(8,128)(2,1)S(1)} %collective-permute-done.9.refs_6_), channel_id=1, source_target_pairs={{0,6},{2,0},{4,2},{6,4},{1,7},{3,1},{5,3},{7,5},{8,14},{10,8},{12,... | collective-permute-start | bytes 1572872 | tf_op jit(solution)/shard_map/ppermute | solution.py:355
  72.9 14.4 %collective-permute-start.12 = (bf16[512,512]{1,0:T(8,128)(2,1)S(1)}, bf16[512,512]{1,0:T(8,128)(2,1)S(1)}, u32[]{:S(2)}, u32[]{:S(2)}) collective-permute-start(bf16[512,512]{1,0:T(8,128)(2,1)S(1)} %collective-permute-done.7.refs_7_), channel_id=1, source_target_pairs={{0,2},{2,4},{4,6},{6,0},{1,3},{3,5},{5,7},{7,1},{8,10},{10,12},{12... | collective-permute-start | bytes 1572872 | tf_op jit(solution)/shard_map/ppermute | solution.py:358
  74.1 13.4 %collective-permute-start.20 = (bf16[256,1024]{1,0:T(8,128)(2,1)S(1)}, bf16[256,1024]{1,0:T(8,128)(2,1)S(1)}, u32[]{:S(2)}, u32[]{:S(2)}) collective-permute-start(bf16[256,1024]{1,0:T(8,128)(2,1)S(1)} %slice.37), channel_id=1, source_target_pairs={{0,16},{16,32},{32,48},{48,0},{1,17},{17,33},{33,49},{49,1},{2,18}... | collective-permute-start | bytes 1572872 | tf_op jit(solution)/shard_map/ppermute | solution.py:361
  75.6 11.8 %collective-permute-start.22 = (bf16[256,1024]{1,0:T(8,128)(2,1)S(1)}, bf16[256,1024]{1,0:T(8,128)(2,1)S(1)}, u32[]{:S(2)}, u32[]{:S(2)}) collective-permute-start(bf16[256,1024]{1,0:T(8,128)(2,1)S(1)} %slice.38), channel_id=1, source_target_pairs={{0,48},{16,0},{32,16},{48,32},{1,49},{17,1},{33,17},{49,33},{2,50}... | collective-permute-start | bytes 1572872 | tf_op jit(solution)/shard_map/ppermute | solution.py:361
  75.7 11.7 %collective-permute-start.14 = (bf16[512,512]{1,0:T(8,128)(2,1)S(1)}, bf16[512,512]{1,0:T(8,128)(2,1)S(1)}, u32[]{:S(2)}, u32[]{:S(2)}) collective-permute-start(bf16[512,512]{1,0:T(8,128)(2,1)S(1)} %collective-permute-done.13.refs_10_), channel_id=1, source_target_pairs={{0,6},{2,0},{4,2},{6,4},{1,7},{3,1},{5,3},{7,5},{8,14},{10,8},{12,... | collective-permute-start | bytes 1572872 | tf_op jit(solution)/shard_map/ppermute | solution.py:359
  89.6 9.2 %collective-permute-start.23 = (f32[1024,512]{1,0:T(8,128)S(1)}, f32[1024,512]{1,0:T(8,128)S(1)}, u32[]{:S(2)}, u32[]{:S(2)}) collective-permute-start(f32[1024,512]{1,0:T(8,128)S(1)} %late_product.2), channel_id=1, source_target_pairs={{0,1},{1,0},{2,3},{3,2},{4,5},{5,4},{6,7},{7,6},{8,9},{9,8},{10,11... | collective-permute-start | bytes 6291464 | tf_op jit(solution)/shard_map/ppermute | solution.py:367
  (12 other events, 498.6 us)

commit v8 on v7

--- a/solution.py
+++ b/solution.py
@@ -11,6 +11,7 @@
 RB = 8
 BLOCKS = RB * QB
 TAIL = 8
+SLOTS = 2 * CAP
 ROWS = RB * BS
 COLS = QB * BS
 RING = 4
@@ -202,7 +203,7 @@
     )(where, *x_far, *y_far, x_late, y_late, total)
 
 
-def finish_kernel(where_ref, pattern_ref, index_ref, energy_ref, xm_ref, own_ref, peer_ref, sign_out, payload_ref, dens, sign_ref, sign_sem):
+def finish_kernel(where_ref, pattern_ref, xm_ref, own_ref, peer_ref, sign_ref, dens_ref):
     yl, xi, yh, z, core = (where_ref[k] for k in range(5))
     block_row = (yl * 4 + xi) * RB
     block_col = ((yh * 4 + z) * 2 + core) * QB
@@ -218,52 +219,67 @@
             xnew = 1.5 * xm_ref[rows, cols].astype(jnp.float32) - kept * product
             sign_ref[rows, cols] = xnew.astype(jnp.bfloat16)
             on_diagonal = jnp.where(block_row + i == block_col + j, 1.0, 0.0)
-            dens[i * QB + j] = (on_diagonal * half_eye - 0.5 * xnew).astype(jnp.bfloat16)
+            dens_ref[i * QB + j] = (on_diagonal * half_eye - 0.5 * xnew).astype(jnp.bfloat16)
         return carry
 
     lax.fori_loop(0, RB, finish, 0)
-    sign_copy = pltpu.make_async_copy(sign_ref, sign_out, sign_sem)
+    dens_ref[BLOCKS] = jnp.zeros((BS, BS), jnp.bfloat16)
+
+
+def finish_tile(where, pattern, xm, own, peer):
+    return pl.pallas_call(
+        finish_kernel,
+        in_specs=[SMEM] * 2 + [VMEM] * 3,
+        out_specs=[VMEM] * 2,
+        out_shape=[
+            jax.ShapeDtypeStruct((ROWS, COLS), jnp.bfloat16),
+            jax.ShapeDtypeStruct((BLOCKS + 1, BS, BS), jnp.bfloat16),
+        ],
+        compiler_params=pltpu.CompilerParams(vmem_limit_bytes=18 * 2**20),
+        cost_estimate=pl.CostEstimate(flops=4 * ROWS * COLS, bytes_accessed=9 * 2**20, transcendentals=0),
+        name="finish_tile",
+    )(where, pattern, xm, own, peer)
+
+
+def pack_kernel(where_ref, own_index, peer_index, energy_ref, own_dens, peer_dens, sign_ref, sign_out, payload_ref, sem):
+    core = where_ref[4]
+    sign_copy = pltpu.make_async_copy(sign_ref, sign_out, sem)
     sign_copy.start()
-    dens[BLOCKS] = jnp.zeros((BS, BS), jnp.bfloat16)
-
     line = lax.broadcasted_iota(jnp.int32, (TAIL, BS), 0)
 
-    def copy(owner, carry):
+    def copy(chip, carry):
         energies = jnp.zeros((TAIL, BS), jnp.float32)
-        for k in range(CAP):
-            block = index_ref[owner * CAP + k]
-            payload_ref[owner, k * BS : (k + 1) * BS, :] = dens[block]
-            energies = jnp.where(line == k, energy_ref[block // QB], energies)
-        payload_ref[owner, CAP * BS :, :] = energies.astype(jnp.bfloat16)
+        for index_ref, dens_ref, source in ((own_index, own_dens, core), (peer_index, peer_dens, 1 - core)):
+            for k in range(CAP):
+                block = index_ref[(chip * 2 + core) * CAP + k]
+                place = source * CAP + k
+                payload_ref[chip, pl.ds(pl.multiple_of(place * BS, BS), BS), :] = dens_ref[block]
+                energies = jnp.where(line == place, energy_ref[block // QB], energies)
+        payload_ref[chip, SLOTS * BS :, :] = energies.astype(jnp.bfloat16)
         return carry
 
-    lax.fori_loop(0, payload_ref.shape[0], copy, 0, unroll=4)
+    lax.fori_loop(0, payload_ref.shape[0], copy, 0, unroll=2)
     sign_copy.wait()
 
 
-def finish_and_payload(where, pattern, index, energy, xm, own, peer):
-    owners = index.shape[0] // CAP
-    packet = (owners, CAP * BS + TAIL, BS)
-    return pl.pallas_call(
-        finish_kernel,
+def pack(where, own_index, peer_index, energy, own_dens, peer_dens, sign):
+    chips = own_index.shape[0] // SLOTS
+    return pl.pallas_call(
+        pack_kernel,
         in_specs=[SMEM] * 3 + [VMEM] * 4,
         out_specs=[HBM, VMEM],
         out_shape=[
             jax.ShapeDtypeStruct((ROWS, COLS), jnp.bfloat16),
-            jax.ShapeDtypeStruct(packet, jnp.bfloat16),
+            jax.ShapeDtypeStruct((chips, SLOTS * BS + TAIL, BS), jnp.bfloat16),
         ],
-        scratch_shapes=[
-            pltpu.VMEM((BLOCKS + 1, BS, BS), jnp.bfloat16),
-            pltpu.VMEM((ROWS, COLS), jnp.bfloat16),
-            pltpu.SemaphoreType.DMA,
-        ],
-        compiler_params=pltpu.CompilerParams(vmem_limit_bytes=18 * 2**20),
-        cost_estimate=pl.CostEstimate(flops=4 * ROWS * COLS, bytes_accessed=15 * 2**20, transcendentals=0),
-        name="finish_payload",
-    )(where, pattern, index, energy, xm, own, peer)
-
-
-FCH = 16
+        scratch_shapes=[pltpu.SemaphoreType.DMA],
+        compiler_params=pltpu.CompilerParams(vmem_limit_bytes=16 * 2**20),
+        cost_estimate=pl.CostEstimate(flops=ROWS * COLS, bytes_accessed=12 * 2**20, transcendentals=0),
+        name="pack_payload",
+    )(where, own_index, peer_index, energy, own_dens, peer_dens, sign)
+
+
+FCH = 8
 
 
 def force_kernel(d_ref, h_ref, s_ref, out_ref, part_ref):
@@ -273,15 +289,15 @@
     def group(i, carry):
         for j in range(FCH):
             source = i * FCH + j
-            energies = d_ref[source, CAP * BS :, :].astype(jnp.float32)
-            for k in range(CAP):
-                slot = source * CAP + k
+            energies = d_ref[source, SLOTS * BS :, :].astype(jnp.float32)
+            for k in range(SLOTS):
+                slot = source * SLOTS + k
                 spread = eye * energies[k : k + 1, :].astype(jnp.bfloat16)
                 scaled = jnp.dot(spread, s_ref[slot], preferred_element_type=jnp.float32)
                 term = d_ref[source, k * BS : (k + 1) * BS, :].astype(jnp.float32) * (
                     h_ref[slot].astype(jnp.float32) - scaled
                 )
-                row = j * CAP + k
+                row = j * SLOTS + k
                 part_ref[i, row : row + 1, :] = jnp.sum(term, axis=0, keepdims=True)
         return carry
 
@@ -303,7 +319,7 @@
         in_specs=[VMEM] * 3,
         out_specs=VMEM,
         out_shape=jax.ShapeDtypeStruct((slots,), jnp.float32),
-        scratch_shapes=[pltpu.VMEM((slots // (FCH * CAP), FCH * CAP, BS), jnp.float32)],
+        scratch_shapes=[pltpu.VMEM((slots // (FCH * SLOTS), FCH * SLOTS, BS), jnp.float32)],
         compiler_params=pltpu.CompilerParams(vmem_limit_bytes=12 * 2**20),
         cost_estimate=pl.CostEstimate(
             flops=6 * slots * BS * BS, bytes_accessed=6 * slots * BS * BS, transcendentals=0
@@ -313,7 +329,7 @@
 
 
 def exchange(payload):
-    return lax.all_to_all(payload, AXES, split_axis=0, concat_axis=0, tiled=True)
+    return lax.all_to_all(payload, AXES[:4], split_axis=0, concat_axis=0, tiled=True)
 
 
 def shards(x, y, pattern_x, pattern_y, pattern_product, orbital_energy, pair_dest, pair_block, force_h, force_s):
@@ -331,6 +347,7 @@
     where = jnp.stack([lax.axis_index(axis) for axis in AXES]).astype(jnp.int32)
     half, quarter = ROWS // 2, ROWS // 4
     y_peer = lax.ppermute(y, "c", SWAP)
+    peer_index = lax.ppermute(index, "c", SWAP)
     pattern_peer = lax.ppermute(pattern_y.T, "c", SWAP)
     xm = mask_x(pattern_x.T, x)
     ym = mask_y(where, pattern_y.T, pattern_peer, y, y_peer)
@@ -362,11 +379,13 @@
 
     x_parts = [xm, xa_below, xa_above, *xa_far, xb_top, xb_bottom, xbt_below, xbb_below, xbt_above, xbb_above]
     y_parts = [ym, ya_below, ya_above, *ya_far, yb, yb_below, yb_above]
-    own, far, x_late, y_late = early_product(x_parts, y_parts, where)
+    own, far, x_late, y_late = early_product(x_parts, y_parts, after(where, peer_index))
     far = late_product(1, where, xb_far, yb_far, x_late, y_late, far)
     peer = lax.ppermute(far, "c", SWAP)
     own = late_product(0, where, xb_far, yb_far, x_late, y_late, after(own, far))
-    sign_next, payload = finish_and_payload(where, pattern_product.T, index, energy, xm, own, peer)
+    sign, dens = finish_tile(where, pattern_product.T, xm, own, peer)
+    peer_dens = lax.ppermute(dens, "c", SWAP)
+    sign_next, payload = pack(where, index, peer_index, energy, dens, peer_dens, sign)
     received = exchange(payload)
     return sign_next, force_sums(received, force_h, force_s)
 

time: 221 us -> 221 us (level)
  the two profiles are of different devices: /device:TPU:7 before, /device:TPU:2 now
where the time goes in v8:
time: 221 us
  blocking collectives  110 us (50%)
  waiting for transfers between devices  47.6 us (22%)
  starting transfers between devices  33.9 us (15%)
  Pallas kernels  24.9 us (11%)
  local copies, waits for them, and re-layouts  2.71 us (1%)
    all_to_all x1, blocking collectives, exchange(): lax.all_to_all(payload, AXES[:4], split_axis=0, concat_axis=0, tiled=True)  110 us
    pallas_call x1, Pallas kernels, early_product(): pl.pallas_call(early_kernel, in_specs=[HBM] * (len(X_PIECES) + len(Y_PIEC...  10.1 us
    ppermute x1, waiting for transfers between devices, shards(): xb_top = lax.ppermute(xm_z[:half], 'yh', SWAP)  9.93 us
    ppermute x1, waiting for transfers between devices, shards(): lax.ppermute(xa_below[:half], 'z', UP)  7.89 us
    ppermute x1, waiting for transfers between devices, shards(): lax.ppermute(xb_bottom_z, 'z', UP)  7.64 us
    ppermute x1, waiting for transfers between devices, shards(): xa_below = lax.ppermute(xm_z, 'z', UP)  6.49 us
    pallas_call x1, Pallas kernels, force_sums(): pl.pallas_call(force_kernel, in_specs=[VMEM] * 3, out_specs=VMEM, out_sha...  5.18 us
    ppermute x1, waiting for transfers between devices, shards(): lax.ppermute(xb_top_z, 'z', UP)  5.05 us
  transfers between devices with their start and end apart: 26, of which 11 were waited for; matrix products, arithmetic and copies ran while one was open for 0% of the time, Pallas kernels for 6%

profile of v8, /device:TPU:2, one launch (start us, length us, event | category | flops | bytes accessed | tf_op | source)
XLA Modules:
  0.0 220.8 jit_solution(4831300687760266192)
XLA Ops:
  5.4 2.0 collective-permute-start.4
  7.3 2.2 collective-permute-start.6
  9.6 3.3 %collective-permute-start.3 = (bf16[512,512]{1,0:T(8,128)(2,1)S(1)}, bf16[512,512]{1,0:T(8,128)(2,1)S(1)}, u32[]{:S(2)}, u32[]{:S(2)}) collective-permute-start(bf16[512,512]{1,0:T(8,128)(2,1)S(1)} %slice.24), channel_id=1, source_target_pairs={{0,8},{8,0},{1,9},{9,1},{2,10},{10,2},{3,11},{11,3},{4,12},{12,4},... | collective-permute-start | bytes 1572872 | tf_op jit(solution)/shard_map/ppermute | solution.py:356
  14.9 9.9 %collective-permute-done.3.refs_5_ = bf16[512,512]{1,0:T(8,128)(2,1)S(1)} collective-permute-done((bf16[512,512]{1,0:T(8,128)(2,1)S(1)}, bf16[512,512]{1,0:T(8,128)(2,1)S(1)}, u32[]{:S(2)}, u32[]{:S(2)}) %collective-permute-start.3) | collective-permute-done | bytes 524320 | tf_op jit(solution)/shard_map/ppermute | solution.py:356
  24.8 1.6 collective-permute-start.9
  26.4 6.5 %collective-permute-done.4.refs_1_ = bf16[1024,512]{1,0:T(8,128)(2,1)S(1)} collective-permute-done((bf16[1024,512]{1,0:T(8,128)(2,1)S(1)}, bf16[1024,512]{1,0:T(8,128)(2,1)S(1)}, u32[]{:S(2)}, u32[]{:S(2)}) %collective-permute-start.4) | collective-permute-done | bytes 1048608 | tf_op jit(solution)/shard_map/ppermute | solution.py:357
  33.1 3.3 %collective-permute-start.7 = (bf16[512,512]{1,0:T(8,128)(2,1)S(1)}, bf16[512,512]{1,0:T(8,128)(2,1)S(1)}, u32[]{:S(2)}, u32[]{:S(2)}) collective-permute-start(bf16[512,512]{1,0:T(8,128)(2,1)S(1)} %slice.33), channel_id=1, source_target_pairs={{0,6},{2,0},{4,2},{6,4},{1,7},{3,1},{5,3},{7,5},{8,14},{10,8},{12,... | collective-permute-start | bytes 1572872 | tf_op jit(solution)/shard_map/ppermute | solution.py:364
  39.7 7.9 %collective-permute-done.5.refs_3_ = bf16[512,512]{1,0:T(8,128)(2,1)S(1)} collective-permute-done((bf16[512,512]{1,0:T(8,128)(2,1)S(1)}, bf16[512,512]{1,0:T(8,128)(2,1)S(1)}, u32[]{:S(2)}, u32[]{:S(2)}) %collective-permute-start.5) | collective-permute-done | bytes 524320 | tf_op jit(solution)/shard_map/ppermute | solution.py:364
  47.6 3.2 %collective-permute-start.11 = (bf16[512,512]{1,0:T(8,128)(2,1)S(1)}, bf16[512,512]{1,0:T(8,128)(2,1)S(1)}, u32[]{:S(2)}, u32[]{:S(2)}) collective-permute-start(bf16[512,512]{1,0:T(8,128)(2,1)S(1)} %collective-permute-done.3.refs_5_), channel_id=1, source_target_pairs={{0,6},{2,0},{4,2},{6,4},{1,7},{3,1},{5,3},{7,5},{8,14},{10,8},{12,... | collective-permute-start | bytes 1572872 | tf_op jit(solution)/shard_map/ppermute | solution.py:368
  50.9 3.2 %collective-permute-start.10 = (bf16[512,512]{1,0:T(8,128)(2,1)S(1)}, bf16[512,512]{1,0:T(8,128)(2,1)S(1)}, u32[]{:S(2)}, u32[]{:S(2)}) collective-permute-start(bf16[512,512]{1,0:T(8,128)(2,1)S(1)} %slice.34), channel_id=1, source_target_pairs={{0,8},{8,0},{1,9},{9,1},{2,10},{10,2},{3,11},{11,3},{4,12},{12,4},... | collective-permute-start | bytes 1572872 | tf_op jit(solution)/shard_map/ppermute | solution.py:362
  56.3 5.0 %collective-permute-done.8.refs_7_ = bf16[512,512]{1,0:T(8,128)(2,1)S(1)} collective-permute-done((bf16[512,512]{1,0:T(8,128)(2,1)S(1)}, bf16[512,512]{1,0:T(8,128)(2,1)S(1)}, u32[]{:S(2)}, u32[]{:S(2)}) %collective-permute-start.8) | collective-permute-done | bytes 524320 | tf_op jit(solution)/shard_map/ppermute | solution.py:368
  61.3 3.0 %collective-permute-done.10.refs_6_ = bf16[512,512]{1,0:T(8,128)(2,1)S(1)} collective-permute-done((bf16[512,512]{1,0:T(8,128)(2,1)S(1)}, bf16[512,512]{1,0:T(8,128)(2,1)S(1)}, u32[]{:S(2)}, u32[]{:S(2)}) %collective-permute-start.10) | collective-permute-done | bytes 524320 | tf_op jit(solution)/shard_map/ppermute | solution.py:362
  64.3 3.2 %collective-permute-start.14 = (bf16[512,512]{1,0:T(8,128)(2,1)S(1)}, bf16[512,512]{1,0:T(8,128)(2,1)S(1)}, u32[]{:S(2)}, u32[]{:S(2)}) collective-permute-start(bf16[512,512]{1,0:T(8,128)(2,1)S(1)} %collective-permute-done.10.refs_6_), channel_id=1, source_target_pairs={{0,6},{2,0},{4,2},{6,4},{1,7},{3,1},{5,3},{7,5},{8,14},{10,8},{12,... | collective-permute-start | bytes 1572872 | tf_op jit(solution)/shard_map/ppermute | solution.py:372
  68.9 7.6 %collective-permute-done.12.refs_8_ = bf16[512,512]{1,0:T(8,128)(2,1)S(1)} collective-permute-done((bf16[512,512]{1,0:T(8,128)(2,1)S(1)}, bf16[512,512]{1,0:T(8,128)(2,1)S(1)}, u32[]{:S(2)}, u32[]{:S(2)}) %collective-permute-start.12) | collective-permute-done | bytes 524320 | tf_op jit(solution)/shard_map/ppermute | solution.py:372
  77.3 1.6 collective-permute-start.21
  79.5 2.5 %collective-permute-start.15 = (bf16[512,512]{1,0:T(8,128)(2,1)S(1)}, bf16[512,512]{1,0:T(8,128)(2,1)S(1)}, u32[]{:S(2)}, u32[]{:S(2)}) collective-permute-start(bf16[512,512]{1,0:T(8,128)(2,1)S(1)} %collective-permute-done.14.refs_10_), channel_id=1, source_target_pairs={{0,6},{2,0},{4,2},{6,4},{1,7},{3,1},{5,3},{7,5},{8,14},{10,8},{12,... | collective-permute-start | bytes 1572872 | tf_op jit(solution)/shard_map/ppermute | solution.py:376
  82.0 10.1 %early_product.1 = (f32[1024,512]{1,0:T(8,128)S(1)}, f32[1024,512]{1,0:T(8,128)S(1)}, bf16[1024,512]{1,0:T(8,128)(2,1)S(1)}, bf16[512,1024]{1,0:T(8,128)(2,1)S(1)}) custom-call(bf16[1024,512]{1,0:T(8,128)(2,1)S(1)} %mask_x.1.refs_0_.xm_ref, bf16[1024,512]{1,0:T(8,128)(2,1)S(1)} %collective-permute-done.4.refs_1_, ...), custom_call_target="tpu_custom_call" | custom-call | flops 7516192768 | bytes 20971520 | tf_op jit(solution)/shard_map/early_product/pallas_call | solution.py:141
  92.1 2.1 late_product.2
  94.3 2.1 late_product.3.own_ref
  96.4 2.0 collective-permute-done.24.peer_ref
  100.1 2.6 %collective-permute-done.25.peer_dens = bf16[33,128,128]{2,1,0:T(8,128)(2,1)S(1)} collective-permute-done((bf16[33,128,128]{2,1,0:T(8,128)(2,1)S(1)}, bf16[33,128,128]{2,1,0:T(8,128)(2,1)S(1)}, u32[]{:S(2)}, u32[]{:S(2)}) %collective-permute-start.25) | collective-permute-done | bytes 1081376 | tf_op jit(solution)/shard_map/ppermute | solution.py:387
  102.6 2.5 %pack_payload.1 = (bf16[1024,512]{1,0:T(8,128)(2,1)}, bf16[64,520,128]{2,1,0:T(8,128)(2,1)S(1)}) custom-call(s32[5]{0:T(128)S(1)} %stack.23.where_ref.refs_19_, s32[256]{0:T(256)S(1)} %broadcast_add_fusion.own_index, s32[256]{0:T(256)S(1)} %collective-permute-done.peer_index, f32[9,1,128]{2,1,0:T(1,128)S(1)} %pad_convert_fusion.energy_ref, ...), custom_call_target="tpu_custom_call" | custom-call | flops 524288 | bytes 12582912 | tf_op jit(solution)/shard_map/pack_payload/pallas_call | solution.py:267
  105.1 110.4 %all_to_all.5.d_ref = bf16[64,520,128]{2,1,0:T(8,128)(2,1)S(1)} all-to-all(bf16[64,520,128]{2,1,0:T(8,128)(2,1)S(1)} %get-tuple-element.35), channel_id=1, replica_groups=mesh['yl'=2,'x'=4,'yh'=2,'z'=4,'c'=2] {'yl','x','yh','z'}, dimensions={0} | all-to-all | bytes 17039360 | tf_op jit(solution)/shard_map/all_to_all | solution.py:332
  215.6 5.2 %force_sums.1 = f32[256]{0:T(256)} custom-call(bf16[64,520,128]{2,1,0:T(8,128)(2,1)S(1)} %all_to_all.5.d_ref, bf16[256,128,128]{2,1,0:T(8,128)(2,1)S(1)} %bitcast.14, bf16[256,128,128]{2,1,0:T(8,128)(2,1)S(1)} %bitcast.16), custom_call_target="tpu_custom_call" | custom-call | flops 25165824 | bytes 25165824 | tf_op jit(solution)/shard_map/force_sums/pallas_call | solution.py:317
  (79 shorter events, 16.9 us)
Async XLA Ops:
  0.6 3.4 %collective-permute-start.2 = (bf16[1024,512]{1,0:T(8,128)(2,1)}, bf16[1024,512]{1,0:T(8,128)(2,1)S(1)}, u32[]{:S(2)}, u32[]{:S(2)}) collective-permute-start(bf16[1024,512]{1,0:T(8,128)(2,1)} %y_ref.1), channel_id=1, source_target_pairs={{0,1},{1,0},{2,3},{3,2},{4,5},{5,4},{6,7},{7,6},{8,9},{9,8},{10,11... | collective-permute-start | bytes 3145736 | tf_op jit(solution)/shard_map/ppermute | solution.py:349
  0.7 3.3 %collective-permute-start.1 = (s32[4,8]{1,0:T(4,128)}, s32[4,8]{1,0:T(4,128)S(1)}, u32[]{:S(2)}, u32[]{:S(2)}) collective-permute-start(s32[4,8]{1,0:T(4,128)} %bitcast.19), channel_id=1, source_target_pairs={{0,1},{1,0},{2,3},{3,2},{4,5},{5,4},{6,7},{7,6},{8,9},{9,8},{10,11... | collective-permute-start | bytes 392 | tf_op jit(solution)/shard_map/ppermute | solution.py:351
  5.4 27.5 %collective-permute-start.4 = (bf16[1024,512]{1,0:T(8,128)(2,1)S(1)}, bf16[1024,512]{1,0:T(8,128)(2,1)S(1)}, u32[]{:S(2)}, u32[]{:S(2)}) collective-permute-start(bf16[1024,512]{1,0:T(8,128)(2,1)S(1)} %mask_x.1.refs_0_.xm_ref), channel_id=1, source_target_pairs={{0,2},{2,4},{4,6},{6,0},{1,3},{3,5},{5,7},{7,1},{8,10},{10,12},{12... | collective-permute-start | bytes 3145736 | tf_op jit(solution)/shard_map/ppermute | solution.py:357
  7.3 25.7 %collective-permute-start.6 = (bf16[1024,512]{1,0:T(8,128)(2,1)S(1)}, bf16[1024,512]{1,0:T(8,128)(2,1)S(1)}, u32[]{:S(2)}, u32[]{:S(2)}) collective-permute-start(bf16[1024,512]{1,0:T(8,128)(2,1)S(1)} %mask_x.1.refs_0_.xm_ref), channel_id=1, source_target_pairs={{0,6},{2,0},{4,2},{6,4},{1,7},{3,1},{5,3},{7,5},{8,14},{10,8},{12,... | collective-permute-start | bytes 3145736 | tf_op jit(solution)/shard_map/ppermute | solution.py:358
  9.6 15.2 %collective-permute-start.3 = (bf16[512,512]{1,0:T(8,128)(2,1)S(1)}, bf16[512,512]{1,0:T(8,128)(2,1)S(1)}, u32[]{:S(2)}, u32[]{:S(2)}) collective-permute-start(bf16[512,512]{1,0:T(8,128)(2,1)S(1)} %slice.24), channel_id=1, source_target_pairs={{0,8},{8,0},{1,9},{9,1},{2,10},{10,2},{3,11},{11,3},{4,12},{12,4},... | collective-permute-start | bytes 1572872 | tf_op jit(solution)/shard_map/ppermute | solution.py:356
  12.9 24.6 %collective-permute-start.16 = (bf16[512,1024]{1,0:T(8,128)(2,1)S(1)}, bf16[512,1024]{1,0:T(8,128)(2,1)S(1)}, u32[]{:S(2)}, u32[]{:S(2)}) collective-permute-start(bf16[512,1024]{1,0:T(8,128)(2,1)S(1)} %mask_y.1.refs_11_), channel_id=1, source_target_pairs={{0,16},{16,32},{32,48},{48,0},{1,17},{17,33},{33,49},{49,1},{2,18}... | collective-permute-start | bytes 3145736 | tf_op jit(solution)/shard_map/ppermute | solution.py:359
  14.3 24.7 %collective-permute-start.18 = (bf16[512,1024]{1,0:T(8,128)(2,1)S(1)}, bf16[512,1024]{1,0:T(8,128)(2,1)S(1)}, u32[]{:S(2)}, u32[]{:S(2)}) collective-permute-start(bf16[512,1024]{1,0:T(8,128)(2,1)S(1)} %mask_y.1.refs_11_), channel_id=1, source_target_pairs={{0,48},{16,0},{32,16},{48,32},{1,49},{17,1},{33,17},{49,33},{2,50}... | collective-permute-start | bytes 3145736 | tf_op jit(solution)/shard_map/ppermute | solution.py:360
  24.8 26.1 %collective-permute-start.9 = (bf16[512,1024]{1,0:T(8,128)(2,1)S(1)}, bf16[512,1024]{1,0:T(8,128)(2,1)S(1)}, u32[]{:S(2)}, u32[]{:S(2)}) collective-permute-start(bf16[512,1024]{1,0:T(8,128)(2,1)S(1)} %mask_y.1.refs_11_), channel_id=1, source_target_pairs={{0,64},{64,0},{1,65},{65,1},{2,66},{66,2},{3,67},{67,3},{4,68},{68... | collective-permute-start | bytes 3145736 | tf_op jit(solution)/shard_map/ppermute | solution.py:361
  32.9 14.7 %collective-permute-start.5 = (bf16[512,512]{1,0:T(8,128)(2,1)S(1)}, bf16[512,512]{1,0:T(8,128)(2,1)S(1)}, u32[]{:S(2)}, u32[]{:S(2)}) collective-permute-start(bf16[512,512]{1,0:T(8,128)(2,1)S(1)} %slice.32), channel_id=1, source_target_pairs={{0,2},{2,4},{4,6},{6,0},{1,3},{3,5},{5,7},{7,1},{8,10},{10,12},{12... | collective-permute-start | bytes 1572872 | tf_op jit(solution)/shard_map/ppermute | solution.py:364
  33.1 14.6 %collective-permute-start.7 = (bf16[512,512]{1,0:T(8,128)(2,1)S(1)}, bf16[512,512]{1,0:T(8,128)(2,1)S(1)}, u32[]{:S(2)}, u32[]{:S(2)}) collective-permute-start(bf16[512,512]{1,0:T(8,128)(2,1)S(1)} %slice.33), channel_id=1, source_target_pairs={{0,6},{2,0},{4,2},{6,4},{1,7},{3,1},{5,3},{7,5},{8,14},{10,8},{12,... | collective-permute-start | bytes 1572872 | tf_op jit(solution)/shard_map/ppermute | solution.py:364
  37.5 16.6 %collective-permute-start.17 = (bf16[256,1024]{1,0:T(8,128)(2,1)S(1)}, bf16[256,1024]{1,0:T(8,128)(2,1)S(1)}, u32[]{:S(2)}, u32[]{:S(2)}) collective-permute-start(bf16[256,1024]{1,0:T(8,128)(2,1)S(1)} %slice.35), channel_id=1, source_target_pairs={{0,16},{16,32},{32,48},{48,0},{1,17},{17,33},{33,49},{49,1},{2,18}... | collective-permute-start | bytes 1572872 | tf_op jit(solution)/shard_map/ppermute | solution.py:365
  39.1 15.0 %collective-permute-start.19 = (bf16[256,1024]{1,0:T(8,128)(2,1)S(1)}, bf16[256,1024]{1,0:T(8,128)(2,1)S(1)}, u32[]{:S(2)}, u32[]{:S(2)}) collective-permute-start(bf16[256,1024]{1,0:T(8,128)(2,1)S(1)} %slice.36), channel_id=1, source_target_pairs={{0,48},{16,0},{32,16},{48,32},{1,49},{17,1},{33,17},{49,33},{2,50}... | collective-permute-start | bytes 1572872 | tf_op jit(solution)/shard_map/ppermute | solution.py:365
  47.6 13.7 %collective-permute-start.8 = (bf16[512,512]{1,0:T(8,128)(2,1)S(1)}, bf16[512,512]{1,0:T(8,128)(2,1)S(1)}, u32[]{:S(2)}, u32[]{:S(2)}) collective-permute-start(bf16[512,512]{1,0:T(8,128)(2,1)S(1)} %collective-permute-done.3.refs_5_), channel_id=1, source_target_pairs={{0,2},{2,4},{4,6},{6,0},{1,3},{3,5},{5,7},{7,1},{8,10},{10,12},{12... | collective-permute-start | bytes 1572872 | tf_op jit(solution)/shard_map/ppermute | solution.py:368
  47.6 13.7 %collective-permute-start.11 = (bf16[512,512]{1,0:T(8,128)(2,1)S(1)}, bf16[512,512]{1,0:T(8,128)(2,1)S(1)}, u32[]{:S(2)}, u32[]{:S(2)}) collective-permute-start(bf16[512,512]{1,0:T(8,128)(2,1)S(1)} %collective-permute-done.3.refs_5_), channel_id=1, source_target_pairs={{0,6},{2,0},{4,2},{6,4},{1,7},{3,1},{5,3},{7,5},{8,14},{10,8},{12,... | collective-permute-start | bytes 1572872 | tf_op jit(solution)/shard_map/ppermute | solution.py:368
  50.9 13.4 %collective-permute-start.10 = (bf16[512,512]{1,0:T(8,128)(2,1)S(1)}, bf16[512,512]{1,0:T(8,128)(2,1)S(1)}, u32[]{:S(2)}, u32[]{:S(2)}) collective-permute-start(bf16[512,512]{1,0:T(8,128)(2,1)S(1)} %slice.34), channel_id=1, source_target_pairs={{0,8},{8,0},{1,9},{9,1},{2,10},{10,2},{3,11},{11,3},{4,12},{12,4},... | collective-permute-start | bytes 1572872 | tf_op jit(solution)/shard_map/ppermute | solution.py:362
  54.1 23.2 %collective-permute-start.20 = (bf16[512,1024]{1,0:T(8,128)(2,1)S(1)}, bf16[512,1024]{1,0:T(8,128)(2,1)S(1)}, u32[]{:S(2)}, u32[]{:S(2)}) collective-permute-start(bf16[512,1024]{1,0:T(8,128)(2,1)S(1)} %collective-permute-done.9.refs_16_), channel_id=1, source_target_pairs={{0,16},{16,32},{32,48},{48,0},{1,17},{17,33},{33,49},{49,1},{2,18}... | collective-permute-start | bytes 3145736 | tf_op jit(solution)/shard_map/ppermute | solution.py:370
  55.6 23.3 %collective-permute-start.22 = (bf16[512,1024]{1,0:T(8,128)(2,1)S(1)}, bf16[512,1024]{1,0:T(8,128)(2,1)S(1)}, u32[]{:S(2)}, u32[]{:S(2)}) collective-permute-start(bf16[512,1024]{1,0:T(8,128)(2,1)S(1)} %collective-permute-done.9.refs_16_), channel_id=1, source_target_pairs={{0,48},{16,0},{32,16},{48,32},{1,49},{17,1},{33,17},{49,33},{2,50}... | collective-permute-start | bytes 3145736 | tf_op jit(solution)/shard_map/ppermute | solution.py:370
  64.3 12.2 %collective-permute-start.12 = (bf16[512,512]{1,0:T(8,128)(2,1)S(1)}, bf16[512,512]{1,0:T(8,128)(2,1)S(1)}, u32[]{:S(2)}, u32[]{:S(2)}) collective-permute-start(bf16[512,512]{1,0:T(8,128)(2,1)S(1)} %collective-permute-done.10.refs_6_), channel_id=1, source_target_pairs={{0,2},{2,4},{4,6},{6,0},{1,3},{3,5},{5,7},{7,1},{8,10},{10,12},{12... | collective-permute-start | bytes 1572872 | tf_op jit(solution)/shard_map/ppermute | solution.py:372
  64.3 15.2 %collective-permute-start.14 = (bf16[512,512]{1,0:T(8,128)(2,1)S(1)}, bf16[512,512]{1,0:T(8,128)(2,1)S(1)}, u32[]{:S(2)}, u32[]{:S(2)}) collective-permute-start(bf16[512,512]{1,0:T(8,128)(2,1)S(1)} %collective-permute-done.10.refs_6_), channel_id=1, source_target_pairs={{0,6},{2,0},{4,2},{6,4},{1,7},{3,1},{5,3},{7,5},{8,14},{10,8},{12,... | collective-permute-start | bytes 1572872 | tf_op jit(solution)/shard_map/ppermute | solution.py:372
  76.5 15.6 %collective-permute-start.13 = (bf16[512,512]{1,0:T(8,128)(2,1)S(1)}, bf16[512,512]{1,0:T(8,128)(2,1)S(1)}, u32[]{:S(2)}, u32[]{:S(2)}) collective-permute-start(bf16[512,512]{1,0:T(8,128)(2,1)S(1)} %collective-permute-done.8.refs_7_), channel_id=1, source_target_pairs={{0,2},{2,4},{4,6},{6,0},{1,3},{3,5},{5,7},{7,1},{8,10},{10,12},{12... | collective-permute-start | bytes 1572872 | tf_op jit(solution)/shard_map/ppermute | solution.py:375
  77.3 14.8 %collective-permute-start.21 = (bf16[256,1024]{1,0:T(8,128)(2,1)S(1)}, bf16[256,1024]{1,0:T(8,128)(2,1)S(1)}, u32[]{:S(2)}, u32[]{:S(2)}) collective-permute-start(bf16[256,1024]{1,0:T(8,128)(2,1)S(1)} %slice.37), channel_id=1, source_target_pairs={{0,16},{16,32},{32,48},{48,0},{1,17},{17,33},{33,49},{49,1},{2,18}... | collective-permute-start | bytes 1572872 | tf_op jit(solution)/shard_map/ppermute | solution.py:378
  78.9 13.2 %collective-permute-start.23 = (bf16[256,1024]{1,0:T(8,128)(2,1)S(1)}, bf16[256,1024]{1,0:T(8,128)(2,1)S(1)}, u32[]{:S(2)}, u32[]{:S(2)}) collective-permute-start(bf16[256,1024]{1,0:T(8,128)(2,1)S(1)} %slice.38), channel_id=1, source_target_pairs={{0,48},{16,0},{32,16},{48,32},{1,49},{17,1},{33,17},{49,33},{2,50}... | collective-permute-start | bytes 1572872 | tf_op jit(solution)/shard_map/ppermute | solution.py:378
  79.5 12.6 %collective-permute-start.15 = (bf16[512,512]{1,0:T(8,128)(2,1)S(1)}, bf16[512,512]{1,0:T(8,128)(2,1)S(1)}, u32[]{:S(2)}, u32[]{:S(2)}) collective-permute-start(bf16[512,512]{1,0:T(8,128)(2,1)S(1)} %collective-permute-done.14.refs_10_), channel_id=1, source_target_pairs={{0,6},{2,0},{4,2},{6,4},{1,7},{3,1},{5,3},{7,5},{8,14},{10,8},{12,... | collective-permute-start | bytes 1572872 | tf_op jit(solution)/shard_map/ppermute | solution.py:376
  94.2 4.2 %collective-permute-start.24 = (f32[1024,512]{1,0:T(8,128)S(1)}, f32[1024,512]{1,0:T(8,128)S(1)}, u32[]{:S(2)}, u32[]{:S(2)}) collective-permute-start(f32[1024,512]{1,0:T(8,128)S(1)} %late_product.2), channel_id=1, source_target_pairs={{0,1},{1,0},{2,3},{3,2},{4,5},{5,4},{6,7},{7,6},{8,9},{9,8},{10,11... | collective-permute-start | bytes 6291464 | tf_op jit(solution)/shard_map/ppermute | solution.py:384
  (14 other events, 525.0 us)

commit v9 on v7

--- a/solution.py
+++ b/solution.py
@@ -94,40 +94,41 @@
     nx, ny = len(X_PIECES), len(Y_PIECES)
     x_in, y_in, where_ref = refs[:nx], refs[nx : nx + ny], refs[nx + ny]
     own_ref, far_ref, x_late, y_late = refs[nx + ny + 1 : nx + ny + 5]
-    x_buf, y_buf, x_sem, y_sem = refs[nx + ny + 5 :]
-
-    for k in range(max(nx, ny)):
-        for pieces, source, buf, sem, half in (
-            (X_PIECES, x_in, x_buf, x_sem, ROWS // 2),
-            (Y_PIECES, y_in, y_buf, y_sem, ROWS // 4),
-        ):
-            if k < len(pieces):
-                position, start, size = pieces[k]
-                target = buf.at[position, pl.ds(start * half, size * half)]
-                pltpu.make_async_copy(source[k], target, sem.at[position]).start()
+    y_buf, y_sem = refs[nx + ny + 5 :]
+    half = ROWS // 2
+
+    for k, (position, start, size) in enumerate(Y_PIECES):
+        target = y_buf.at[position, pl.ds(start * (half // 2), size * (half // 2))]
+        pltpu.make_async_copy(y_in[k], target, y_sem.at[position]).start()
 
     own_ref[...] = jnp.zeros_like(own_ref)
     far_ref[...] = jnp.zeros_like(far_ref)
 
-    def step(position, carry):
-        pltpu.make_async_copy(x_buf.at[position], x_buf.at[position], x_sem.at[position]).wait()
+    def x_halves(position):
+        pieces = [(x_in[k], piece) for k, piece in enumerate(X_PIECES) if piece[0] == position]
+        if len(pieces) == 1:
+            return [pieces[0][0].at[pl.ds(part * half, half)] for part in range(2)]
+        return [ref for ref, _ in pieces]
+
+    for position in range(EARLY):
         y_position = y_place(where_ref, position)
+        halves = x_halves(position)
 
         @pl.when(y_position != EARLY)
         def _():
             pltpu.make_async_copy(y_buf.at[y_position], y_buf.at[y_position], y_sem.at[y_position]).wait()
-            for out_ref, cols in ((own_ref, slice(0, COLS)), (far_ref, slice(COLS, 2 * COLS))):
-                out_ref[...] += jnp.dot(
-                    x_buf[position], y_buf[y_position, :, cols], preferred_element_type=jnp.float32
-                )
+            for part, x_ref in enumerate(halves):
+                rows = slice(part * half, (part + 1) * half)
+                for out_ref, cols in ((own_ref, slice(0, COLS)), (far_ref, slice(COLS, 2 * COLS))):
+                    out_ref[rows, :] += jnp.dot(
+                        x_ref[...], y_buf[y_position, :, cols], preferred_element_type=jnp.float32
+                    )
 
         @pl.when(y_position == EARLY)
         def _():
-            x_late[...] = x_buf[position]
-
-        return carry
-
-    lax.fori_loop(0, EARLY, step, 0)
+            for part, x_ref in enumerate(halves):
+                x_late[slice(part * half, (part + 1) * half), :] = x_ref[...]
+
     last = y_place(where_ref, EARLY)
 
     @pl.when(last != EARLY)
@@ -139,7 +140,7 @@
 def early_product(x_parts, y_parts, where):
     return pl.pallas_call(
         early_kernel,
-        in_specs=[HBM] * (len(X_PIECES) + len(Y_PIECES)) + [SMEM],
+        in_specs=[VMEM] * len(X_PIECES) + [HBM] * len(Y_PIECES) + [SMEM],
         out_specs=[VMEM] * 4,
         out_shape=[
             jax.ShapeDtypeStruct((ROWS, COLS), jnp.float32),
@@ -148,9 +149,7 @@
             jax.ShapeDtypeStruct((ROWS // 2, 2 * COLS), jnp.bfloat16),
         ],
         scratch_shapes=[
-            pltpu.VMEM((EARLY, ROWS, COLS), jnp.bfloat16),
             pltpu.VMEM((EARLY, ROWS // 2, 2 * COLS), jnp.bfloat16),
-            pltpu.SemaphoreType.DMA((EARLY,)),
             pltpu.SemaphoreType.DMA((EARLY,)),
         ],
         compiler_params=pltpu.CompilerParams(vmem_limit_bytes=24 * 2**20),

time: 221 us -> 221 us (level)
  no operation moved by 1% of the time
where the time goes in v9:
time: 221 us
  blocking collectives  114 us (52%)
  waiting for transfers between devices  45.7 us (21%)
  starting transfers between devices  33.3 us (15%)
  Pallas kernels  23.6 us (11%)
  local copies, waits for them, and re-layouts  2.72 us (1%)
    all_to_all x1, blocking collectives, exchange(): lax.all_to_all(payload, AXES, split_axis=0, concat_axis=0, tiled=True)  114 us
    ppermute x1, waiting for transfers between devices, shards(): xb_top = lax.ppermute(xm_z[:half], 'yh', SWAP)  9.89 us
    pallas_call x1, Pallas kernels, early_product(): pl.pallas_call(early_kernel, in_specs=[VMEM] * len(X_PIECES) + [HBM] * le...  9.56 us
    ppermute x1, waiting for transfers between devices, shards(): lax.ppermute(xb_bottom_z, 'z', UP)  8.63 us
    ppermute x1, waiting for transfers between devices, shards(): lax.ppermute(xa_below[:half], 'z', UP)  8.48 us
    ppermute x1, waiting for transfers between devices, shards(): xa_below = lax.ppermute(xm_z, 'z', UP)  7.42 us
    ppermute x1, waiting for transfers between devices, shards(): lax.ppermute(xb_top_z, 'z', UP)  5.71 us
    ppermute x1, starting transfers between devices, shards(): peer = lax.ppermute(far, 'c', SWAP)  5.45 us
  transfers between devices with their start and end apart: 24, of which 9 were waited for; matrix products, arithmetic and copies ran while one was open for 0% of the time, Pallas kernels for 6%

profile of v9, /device:TPU:7, one launch (start us, length us, event | category | flops | bytes accessed | tf_op | source)
XLA Modules:
  0.0 220.8 jit_solution(1487925181329178293)
XLA Ops:
  5.6 1.7 collective-permute-start.3
  7.3 2.2 collective-permute-start.5
  9.6 3.0 %collective-permute-start.2 = (bf16[512,512]{1,0:T(8,128)(2,1)S(1)}, bf16[512,512]{1,0:T(8,128)(2,1)S(1)}, u32[]{:S(2)}, u32[]{:S(2)}) collective-permute-start(bf16[512,512]{1,0:T(8,128)(2,1)S(1)} %slice.24), channel_id=1, source_target_pairs={{0,8},{8,0},{1,9},{9,1},{2,10},{10,2},{3,11},{11,3},{4,12},{12,4},... | collective-permute-start | bytes 1572872 | tf_op jit(solution)/shard_map/ppermute | solution.py:338
  14.0 9.9 %collective-permute-done.2.refs_5_ = bf16[512,512]{1,0:T(8,128)(2,1)S(1)} collective-permute-done((bf16[512,512]{1,0:T(8,128)(2,1)S(1)}, bf16[512,512]{1,0:T(8,128)(2,1)S(1)}, u32[]{:S(2)}, u32[]{:S(2)}) %collective-permute-start.2) | collective-permute-done | bytes 524320 | tf_op jit(solution)/shard_map/ppermute | solution.py:338
  25.2 7.4 %collective-permute-done.3.refs_1_ = bf16[1024,512]{1,0:T(8,128)(2,1)S(1)} collective-permute-done((bf16[1024,512]{1,0:T(8,128)(2,1)S(1)}, bf16[1024,512]{1,0:T(8,128)(2,1)S(1)}, u32[]{:S(2)}, u32[]{:S(2)}) %collective-permute-start.3) | collective-permute-done | bytes 1048608 | tf_op jit(solution)/shard_map/ppermute | solution.py:339
  32.8 2.7 %collective-permute-start.6 = (bf16[512,512]{1,0:T(8,128)(2,1)S(1)}, bf16[512,512]{1,0:T(8,128)(2,1)S(1)}, u32[]{:S(2)}, u32[]{:S(2)}) collective-permute-start(bf16[512,512]{1,0:T(8,128)(2,1)S(1)} %slice.33), channel_id=1, source_target_pairs={{0,6},{2,0},{4,2},{6,4},{1,7},{3,1},{5,3},{7,5},{8,14},{10,8},{12,... | collective-permute-start | bytes 1572872 | tf_op jit(solution)/shard_map/ppermute | solution.py:346
  36.3 1.5 collective-permute-start.16
  38.0 8.5 %collective-permute-done.4.refs_3_ = bf16[512,512]{1,0:T(8,128)(2,1)S(1)} collective-permute-done((bf16[512,512]{1,0:T(8,128)(2,1)S(1)}, bf16[512,512]{1,0:T(8,128)(2,1)S(1)}, u32[]{:S(2)}, u32[]{:S(2)}) %collective-permute-start.4) | collective-permute-done | bytes 524320 | tf_op jit(solution)/shard_map/ppermute | solution.py:346
  46.4 2.7 %collective-permute-start.10 = (bf16[512,512]{1,0:T(8,128)(2,1)S(1)}, bf16[512,512]{1,0:T(8,128)(2,1)S(1)}, u32[]{:S(2)}, u32[]{:S(2)}) collective-permute-start(bf16[512,512]{1,0:T(8,128)(2,1)S(1)} %collective-permute-done.2.refs_5_), channel_id=1, source_target_pairs={{0,6},{2,0},{4,2},{6,4},{1,7},{3,1},{5,3},{7,5},{8,14},{10,8},{12,... | collective-permute-start | bytes 1572872 | tf_op jit(solution)/shard_map/ppermute | solution.py:350
  49.1 2.9 %collective-permute-start.9 = (bf16[512,512]{1,0:T(8,128)(2,1)S(1)}, bf16[512,512]{1,0:T(8,128)(2,1)S(1)}, u32[]{:S(2)}, u32[]{:S(2)}) collective-permute-start(bf16[512,512]{1,0:T(8,128)(2,1)S(1)} %slice.34), channel_id=1, source_target_pairs={{0,8},{8,0},{1,9},{9,1},{2,10},{10,2},{3,11},{11,3},{4,12},{12,4},... | collective-permute-start | bytes 1572872 | tf_op jit(solution)/shard_map/ppermute | solution.py:344
  53.5 5.7 %collective-permute-done.7.refs_7_ = bf16[512,512]{1,0:T(8,128)(2,1)S(1)} collective-permute-done((bf16[512,512]{1,0:T(8,128)(2,1)S(1)}, bf16[512,512]{1,0:T(8,128)(2,1)S(1)}, u32[]{:S(2)}, u32[]{:S(2)}) %collective-permute-start.7) | collective-permute-done | bytes 524320 | tf_op jit(solution)/shard_map/ppermute | solution.py:350
  59.2 2.4 %collective-permute-done.9.refs_6_ = bf16[512,512]{1,0:T(8,128)(2,1)S(1)} collective-permute-done((bf16[512,512]{1,0:T(8,128)(2,1)S(1)}, bf16[512,512]{1,0:T(8,128)(2,1)S(1)}, u32[]{:S(2)}, u32[]{:S(2)}) %collective-permute-start.9) | collective-permute-done | bytes 524320 | tf_op jit(solution)/shard_map/ppermute | solution.py:344
  61.6 2.7 %collective-permute-start.13 = (bf16[512,512]{1,0:T(8,128)(2,1)S(1)}, bf16[512,512]{1,0:T(8,128)(2,1)S(1)}, u32[]{:S(2)}, u32[]{:S(2)}) collective-permute-start(bf16[512,512]{1,0:T(8,128)(2,1)S(1)} %collective-permute-done.9.refs_6_), channel_id=1, source_target_pairs={{0,6},{2,0},{4,2},{6,4},{1,7},{3,1},{5,3},{7,5},{8,14},{10,8},{12,... | collective-permute-start | bytes 1572872 | tf_op jit(solution)/shard_map/ppermute | solution.py:354
  64.3 8.6 %collective-permute-done.11.refs_8_ = bf16[512,512]{1,0:T(8,128)(2,1)S(1)} collective-permute-done((bf16[512,512]{1,0:T(8,128)(2,1)S(1)}, bf16[512,512]{1,0:T(8,128)(2,1)S(1)}, u32[]{:S(2)}, u32[]{:S(2)}) %collective-permute-start.11) | collective-permute-done | bytes 524320 | tf_op jit(solution)/shard_map/ppermute | solution.py:354
  74.1 1.5 collective-permute-start.20
  75.7 1.6 collective-permute-start.14
  77.3 9.6 %early_product.1 = (f32[1024,512]{1,0:T(8,128)S(1)}, f32[1024,512]{1,0:T(8,128)S(1)}, bf16[1024,512]{1,0:T(8,128)(2,1)S(1)}, bf16[512,1024]{1,0:T(8,128)(2,1)S(1)}) custom-call(bf16[1024,512]{1,0:T(8,128)(2,1)S(1)} %mask_x.1.refs_0_.xm_ref, bf16[1024,512]{1,0:T(8,128)(2,1)S(1)} %collective-permute-done.3.refs_1_, ...), custom_call_target="tpu_custom_call" | custom-call | flops 7516192768 | bytes 20971520 | tf_op jit(solution)/shard_map/early_product/pallas_call | solution.py:141
  87.0 2.1 late_product.2
  89.1 5.5 %collective-permute-start.23 = (f32[1024,512]{1,0:T(8,128)S(1)}, f32[1024,512]{1,0:T(8,128)S(1)}, u32[]{:S(2)}, u32[]{:S(2)}) collective-permute-start(f32[1024,512]{1,0:T(8,128)S(1)} %late_product.2), channel_id=1, source_target_pairs={{0,1},{1,0},{2,3},{3,2},{4,5},{5,4},{6,7},{7,6},{8,9},{9,8},{10,11... | collective-permute-start | bytes 6291464 | tf_op jit(solution)/shard_map/ppermute | solution.py:366
  94.9 2.1 late_product.3.own_ref
  97.0 1.3 collective-permute-done.23.peer_ref
  98.3 3.0 %finish_payload.1 = (bf16[1024,512]{1,0:T(8,128)(2,1)}, bf16[128,264,128]{2,1,0:T(8,128)(2,1)S(1)}) custom-call(s32[5]{0:T(128)S(1)} %stack.23.where_ref.refs_19_, s32[4,8]{1,0:T(4,128)S(1)} %bitcast.17, s32[256]{0:T(256)S(1)} %broadcast_add_fusion.index_ref, f32[9,1,128]{2,1,0:T(1,128)S(1)} %pad_convert_fusion.energy_ref, ...), custom_call_target="tpu_custom_call" | custom-call | flops 2097152 | bytes 15728640 | tf_op jit(solution)/shard_map/finish_payload/pallas_call | solution.py:246
  101.3 114.3 %all_to_all.5.d_ref = bf16[128,264,128]{2,1,0:T(8,128)(2,1)S(1)} all-to-all(bf16[128,264,128]{2,1,0:T(8,128)(2,1)S(1)} %get-tuple-element.29), channel_id=1, replica_groups=mesh['yl'=2,'x'=4,'yh'=2,'z'=4,'c'=2] {'yl','x','yh','z','c'}, dimensions={0} | all-to-all | bytes 17301504 | tf_op jit(solution)/shard_map/all_to_all | solution.py:315
  215.6 5.2 %force_sums.1 = f32[256]{0:T(256)} custom-call(bf16[128,264,128]{2,1,0:T(8,128)(2,1)S(1)} %all_to_all.5.d_ref, bf16[256,128,128]{2,1,0:T(8,128)(2,1)S(1)} %bitcast.14, bf16[256,128,128]{2,1,0:T(8,128)(2,1)S(1)} %bitcast.16), custom_call_target="tpu_custom_call" | custom-call | flops 25165824 | bytes 25165824 | tf_op jit(solution)/shard_map/force_sums/pallas_call | solution.py:300
  (74 shorter events, 12.0 us)
Async XLA Ops:
  0.6 3.7 %collective-permute-start.1 = (bf16[1024,512]{1,0:T(8,128)(2,1)}, bf16[1024,512]{1,0:T(8,128)(2,1)S(1)}, u32[]{:S(2)}, u32[]{:S(2)}) collective-permute-start(bf16[1024,512]{1,0:T(8,128)(2,1)} %y_ref.1), channel_id=1, source_target_pairs={{0,1},{1,0},{2,3},{3,2},{4,5},{5,4},{6,7},{7,6},{8,9},{9,8},{10,11... | collective-permute-start | bytes 3145736 | tf_op jit(solution)/shard_map/ppermute | solution.py:332
  1.4 2.9 %collective-permute-start = (s32[4,8]{1,0:T(4,128)}, s32[4,8]{1,0:T(4,128)S(1)}, u32[]{:S(2)}, u32[]{:S(2)}) collective-permute-start(s32[4,8]{1,0:T(4,128)} %bitcast.19), channel_id=1, source_target_pairs={{0,1},{1,0},{2,3},{3,2},{4,5},{5,4},{6,7},{7,6},{8,9},{9,8},{10,11... | collective-permute-start | bytes 392 | tf_op jit(solution)/shard_map/ppermute | solution.py:333
  5.6 27.0 %collective-permute-start.3 = (bf16[1024,512]{1,0:T(8,128)(2,1)S(1)}, bf16[1024,512]{1,0:T(8,128)(2,1)S(1)}, u32[]{:S(2)}, u32[]{:S(2)}) collective-permute-start(bf16[1024,512]{1,0:T(8,128)(2,1)S(1)} %mask_x.1.refs_0_.xm_ref), channel_id=1, source_target_pairs={{0,2},{2,4},{4,6},{6,0},{1,3},{3,5},{5,7},{7,1},{8,10},{10,12},{12... | collective-permute-start | bytes 3145736 | tf_op jit(solution)/shard_map/ppermute | solution.py:339
  7.3 25.4 %collective-permute-start.5 = (bf16[1024,512]{1,0:T(8,128)(2,1)S(1)}, bf16[1024,512]{1,0:T(8,128)(2,1)S(1)}, u32[]{:S(2)}, u32[]{:S(2)}) collective-permute-start(bf16[1024,512]{1,0:T(8,128)(2,1)S(1)} %mask_x.1.refs_0_.xm_ref), channel_id=1, source_target_pairs={{0,6},{2,0},{4,2},{6,4},{1,7},{3,1},{5,3},{7,5},{8,14},{10,8},{12,... | collective-permute-start | bytes 3145736 | tf_op jit(solution)/shard_map/ppermute | solution.py:340
  9.6 14.3 %collective-permute-start.2 = (bf16[512,512]{1,0:T(8,128)(2,1)S(1)}, bf16[512,512]{1,0:T(8,128)(2,1)S(1)}, u32[]{:S(2)}, u32[]{:S(2)}) collective-permute-start(bf16[512,512]{1,0:T(8,128)(2,1)S(1)} %slice.24), channel_id=1, source_target_pairs={{0,8},{8,0},{1,9},{9,1},{2,10},{10,2},{3,11},{11,3},{4,12},{12,4},... | collective-permute-start | bytes 1572872 | tf_op jit(solution)/shard_map/ppermute | solution.py:338
  12.6 23.7 %collective-permute-start.15 = (bf16[512,1024]{1,0:T(8,128)(2,1)S(1)}, bf16[512,1024]{1,0:T(8,128)(2,1)S(1)}, u32[]{:S(2)}, u32[]{:S(2)}) collective-permute-start(bf16[512,1024]{1,0:T(8,128)(2,1)S(1)} %mask_y.1.refs_11_), channel_id=1, source_target_pairs={{0,16},{16,32},{32,48},{48,0},{1,17},{17,33},{33,49},{49,1},{2,18}... | collective-permute-start | bytes 3145736 | tf_op jit(solution)/shard_map/ppermute | solution.py:341
  12.8 25.0 %collective-permute-start.17 = (bf16[512,1024]{1,0:T(8,128)(2,1)S(1)}, bf16[512,1024]{1,0:T(8,128)(2,1)S(1)}, u32[]{:S(2)}, u32[]{:S(2)}) collective-permute-start(bf16[512,1024]{1,0:T(8,128)(2,1)S(1)} %mask_y.1.refs_11_), channel_id=1, source_target_pairs={{0,48},{16,0},{32,16},{48,32},{1,49},{17,1},{33,17},{49,33},{2,50}... | collective-permute-start | bytes 3145736 | tf_op jit(solution)/shard_map/ppermute | solution.py:342
  23.9 25.2 %collective-permute-start.8 = (bf16[512,1024]{1,0:T(8,128)(2,1)S(1)}, bf16[512,1024]{1,0:T(8,128)(2,1)S(1)}, u32[]{:S(2)}, u32[]{:S(2)}) collective-permute-start(bf16[512,1024]{1,0:T(8,128)(2,1)S(1)} %mask_y.1.refs_11_), channel_id=1, source_target_pairs={{0,64},{64,0},{1,65},{65,1},{2,66},{66,2},{3,67},{67,3},{4,68},{68... | collective-permute-start | bytes 3145736 | tf_op jit(solution)/shard_map/ppermute | solution.py:343
  32.7 13.8 %collective-permute-start.4 = (bf16[512,512]{1,0:T(8,128)(2,1)S(1)}, bf16[512,512]{1,0:T(8,128)(2,1)S(1)}, u32[]{:S(2)}, u32[]{:S(2)}) collective-permute-start(bf16[512,512]{1,0:T(8,128)(2,1)S(1)} %slice.32), channel_id=1, source_target_pairs={{0,2},{2,4},{4,6},{6,0},{1,3},{3,5},{5,7},{7,1},{8,10},{10,12},{12... | collective-permute-start | bytes 1572872 | tf_op jit(solution)/shard_map/ppermute | solution.py:346
  32.8 13.6 %collective-permute-start.6 = (bf16[512,512]{1,0:T(8,128)(2,1)S(1)}, bf16[512,512]{1,0:T(8,128)(2,1)S(1)}, u32[]{:S(2)}, u32[]{:S(2)}) collective-permute-start(bf16[512,512]{1,0:T(8,128)(2,1)S(1)} %slice.33), channel_id=1, source_target_pairs={{0,6},{2,0},{4,2},{6,4},{1,7},{3,1},{5,3},{7,5},{8,14},{10,8},{12,... | collective-permute-start | bytes 1572872 | tf_op jit(solution)/shard_map/ppermute | solution.py:346
  36.3 15.8 %collective-permute-start.16 = (bf16[256,1024]{1,0:T(8,128)(2,1)S(1)}, bf16[256,1024]{1,0:T(8,128)(2,1)S(1)}, u32[]{:S(2)}, u32[]{:S(2)}) collective-permute-start(bf16[256,1024]{1,0:T(8,128)(2,1)S(1)} %slice.35), channel_id=1, source_target_pairs={{0,16},{16,32},{32,48},{48,0},{1,17},{17,33},{33,49},{49,1},{2,18}... | collective-permute-start | bytes 1572872 | tf_op jit(solution)/shard_map/ppermute | solution.py:347
  37.8 14.2 %collective-permute-start.18 = (bf16[256,1024]{1,0:T(8,128)(2,1)S(1)}, bf16[256,1024]{1,0:T(8,128)(2,1)S(1)}, u32[]{:S(2)}, u32[]{:S(2)}) collective-permute-start(bf16[256,1024]{1,0:T(8,128)(2,1)S(1)} %slice.36), channel_id=1, source_target_pairs={{0,48},{16,0},{32,16},{48,32},{1,49},{17,1},{33,17},{49,33},{2,50}... | collective-permute-start | bytes 1572872 | tf_op jit(solution)/shard_map/ppermute | solution.py:347
  46.4 12.8 %collective-permute-start.7 = (bf16[512,512]{1,0:T(8,128)(2,1)S(1)}, bf16[512,512]{1,0:T(8,128)(2,1)S(1)}, u32[]{:S(2)}, u32[]{:S(2)}) collective-permute-start(bf16[512,512]{1,0:T(8,128)(2,1)S(1)} %collective-permute-done.2.refs_5_), channel_id=1, source_target_pairs={{0,2},{2,4},{4,6},{6,0},{1,3},{3,5},{5,7},{7,1},{8,10},{10,12},{12... | collective-permute-start | bytes 1572872 | tf_op jit(solution)/shard_map/ppermute | solution.py:350
  46.4 12.8 %collective-permute-start.10 = (bf16[512,512]{1,0:T(8,128)(2,1)S(1)}, bf16[512,512]{1,0:T(8,128)(2,1)S(1)}, u32[]{:S(2)}, u32[]{:S(2)}) collective-permute-start(bf16[512,512]{1,0:T(8,128)(2,1)S(1)} %collective-permute-done.2.refs_5_), channel_id=1, source_target_pairs={{0,6},{2,0},{4,2},{6,4},{1,7},{3,1},{5,3},{7,5},{8,14},{10,8},{12,... | collective-permute-start | bytes 1572872 | tf_op jit(solution)/shard_map/ppermute | solution.py:350
  49.1 12.5 %collective-permute-start.9 = (bf16[512,512]{1,0:T(8,128)(2,1)S(1)}, bf16[512,512]{1,0:T(8,128)(2,1)S(1)}, u32[]{:S(2)}, u32[]{:S(2)}) collective-permute-start(bf16[512,512]{1,0:T(8,128)(2,1)S(1)} %slice.34), channel_id=1, source_target_pairs={{0,8},{8,0},{1,9},{9,1},{2,10},{10,2},{3,11},{11,3},{4,12},{12,4},... | collective-permute-start | bytes 1572872 | tf_op jit(solution)/shard_map/ppermute | solution.py:344
  52.0 22.0 %collective-permute-start.19 = (bf16[512,1024]{1,0:T(8,128)(2,1)S(1)}, bf16[512,1024]{1,0:T(8,128)(2,1)S(1)}, u32[]{:S(2)}, u32[]{:S(2)}) collective-permute-start(bf16[512,1024]{1,0:T(8,128)(2,1)S(1)} %collective-permute-done.8.refs_16_), channel_id=1, source_target_pairs={{0,16},{16,32},{32,48},{48,0},{1,17},{17,33},{33,49},{49,1},{2,18}... | collective-permute-start | bytes 3145736 | tf_op jit(solution)/shard_map/ppermute | solution.py:352
  52.2 23.3 %collective-permute-start.21 = (bf16[512,1024]{1,0:T(8,128)(2,1)S(1)}, bf16[512,1024]{1,0:T(8,128)(2,1)S(1)}, u32[]{:S(2)}, u32[]{:S(2)}) collective-permute-start(bf16[512,1024]{1,0:T(8,128)(2,1)S(1)} %collective-permute-done.8.refs_16_), channel_id=1, source_target_pairs={{0,48},{16,0},{32,16},{48,32},{1,49},{17,1},{33,17},{49,33},{2,50}... | collective-permute-start | bytes 3145736 | tf_op jit(solution)/shard_map/ppermute | solution.py:352
  61.6 11.3 %collective-permute-start.11 = (bf16[512,512]{1,0:T(8,128)(2,1)S(1)}, bf16[512,512]{1,0:T(8,128)(2,1)S(1)}, u32[]{:S(2)}, u32[]{:S(2)}) collective-permute-start(bf16[512,512]{1,0:T(8,128)(2,1)S(1)} %collective-permute-done.9.refs_6_), channel_id=1, source_target_pairs={{0,2},{2,4},{4,6},{6,0},{1,3},{3,5},{5,7},{7,1},{8,10},{10,12},{12... | collective-permute-start | bytes 1572872 | tf_op jit(solution)/shard_map/ppermute | solution.py:354
  61.6 14.1 %collective-permute-start.13 = (bf16[512,512]{1,0:T(8,128)(2,1)S(1)}, bf16[512,512]{1,0:T(8,128)(2,1)S(1)}, u32[]{:S(2)}, u32[]{:S(2)}) collective-permute-start(bf16[512,512]{1,0:T(8,128)(2,1)S(1)} %collective-permute-done.9.refs_6_), channel_id=1, source_target_pairs={{0,6},{2,0},{4,2},{6,4},{1,7},{3,1},{5,3},{7,5},{8,14},{10,8},{12,... | collective-permute-start | bytes 1572872 | tf_op jit(solution)/shard_map/ppermute | solution.py:354
  72.9 13.9 %collective-permute-start.12 = (bf16[512,512]{1,0:T(8,128)(2,1)S(1)}, bf16[512,512]{1,0:T(8,128)(2,1)S(1)}, u32[]{:S(2)}, u32[]{:S(2)}) collective-permute-start(bf16[512,512]{1,0:T(8,128)(2,1)S(1)} %collective-permute-done.7.refs_7_), channel_id=1, source_target_pairs={{0,2},{2,4},{4,6},{6,0},{1,3},{3,5},{5,7},{7,1},{8,10},{10,12},{12... | collective-permute-start | bytes 1572872 | tf_op jit(solution)/shard_map/ppermute | solution.py:357
  74.1 12.9 %collective-permute-start.20 = (bf16[256,1024]{1,0:T(8,128)(2,1)S(1)}, bf16[256,1024]{1,0:T(8,128)(2,1)S(1)}, u32[]{:S(2)}, u32[]{:S(2)}) collective-permute-start(bf16[256,1024]{1,0:T(8,128)(2,1)S(1)} %slice.37), channel_id=1, source_target_pairs={{0,16},{16,32},{32,48},{48,0},{1,17},{17,33},{33,49},{49,1},{2,18}... | collective-permute-start | bytes 1572872 | tf_op jit(solution)/shard_map/ppermute | solution.py:360
  75.6 11.3 %collective-permute-start.22 = (bf16[256,1024]{1,0:T(8,128)(2,1)S(1)}, bf16[256,1024]{1,0:T(8,128)(2,1)S(1)}, u32[]{:S(2)}, u32[]{:S(2)}) collective-permute-start(bf16[256,1024]{1,0:T(8,128)(2,1)S(1)} %slice.38), channel_id=1, source_target_pairs={{0,48},{16,0},{32,16},{48,32},{1,49},{17,1},{33,17},{49,33},{2,50}... | collective-permute-start | bytes 1572872 | tf_op jit(solution)/shard_map/ppermute | solution.py:360
  75.7 11.2 %collective-permute-start.14 = (bf16[512,512]{1,0:T(8,128)(2,1)S(1)}, bf16[512,512]{1,0:T(8,128)(2,1)S(1)}, u32[]{:S(2)}, u32[]{:S(2)}) collective-permute-start(bf16[512,512]{1,0:T(8,128)(2,1)S(1)} %collective-permute-done.13.refs_10_), channel_id=1, source_target_pairs={{0,6},{2,0},{4,2},{6,4},{1,7},{3,1},{5,3},{7,5},{8,14},{10,8},{12,... | collective-permute-start | bytes 1572872 | tf_op jit(solution)/shard_map/ppermute | solution.py:358
  89.1 9.2 %collective-permute-start.23 = (f32[1024,512]{1,0:T(8,128)S(1)}, f32[1024,512]{1,0:T(8,128)S(1)}, u32[]{:S(2)}, u32[]{:S(2)}) collective-permute-start(f32[1024,512]{1,0:T(8,128)S(1)} %late_product.2), channel_id=1, source_target_pairs={{0,1},{1,0},{2,3},{3,2},{4,5},{5,4},{6,7},{7,6},{8,9},{9,8},{10,11... | collective-permute-start | bytes 6291464 | tf_op jit(solution)/shard_map/ppermute | solution.py:366
  (12 other events, 499.8 us)
